TPU v7x, 512 devices: a whole 4x4x16 slice. The times are simulated.
512 devices in a mesh: fsdp: 16 (over z_lo, core), tp: 32 (over x, y, z_hi).
Axes of the slice: x: 4, y: 4, z: 16 (z_hi: 2, z_lo: 8; z = z_hi * 8 + z_lo), core: 2. Of those that a mesh axis runs over, the one named last changes fastest.
Arguments:
- inputs: bfloat16 [128, 16, 8192], P('tp', None, 'fsdp'), may hold values from -6 to 6
- featurizer: bfloat16 [8192, 3, 8192], P('fsdp', None, 'tp'), may hold values from -0.0625 to 0.0625
- short_filter: float32 [3, 3, 8192], P(None, None, 'tp'), may hold values from -3 to 3
- long_filter: float32 [512, 128], P('tp'), may hold values from -1.2 to 1.2
- decay_rate: float32 [512], P('tp'), may hold values from 0.004 to 0.08
- skip_gain: float32 [8192], P('tp'), may hold values from -1 to 1
- output_grad: bfloat16 [128, 16, 8192], P(None, 'fsdp', 'tp'), may hold values from -6 to 6
Outputs:
- hyena_out: bfloat16 [128, 16, 8192], P(None, 'fsdp', 'tp')
- input_grad: bfloat16 [128, 16, 8192], P('tp', None, 'fsdp')
- weight_grad: bfloat16 [8192, 3, 8192], P('fsdp', None, 'tp')
All inputs are finite; a program needn't handle non-finite values.
Results may differ from a plain program's by a relative error of at most 0.028.
Values may be sent and summed in bfloat16 or wider, within the bound.
No kernel may reach another device: no remote copies, remote signals or barrier semaphores. Data moves between devices by JAX's collectives and lax.ppermute only.
A program may use at most 64 MiB of HBM per device.

v0:
```python
import jax
import jax.numpy as jnp
from jax import lax
from jax.sharding import PartitionSpec as P


def from_behind(x, axis, by):
    devices = lax.axis_size(axis)
    pairs = [(i, i + by) for i in range(devices) if 0 <= i + by < devices]
    return lax.ppermute(x, axis, pairs)


def toeplitz_pair(kernel, tokens):
    tap_count = kernel.shape[1]
    positions = jnp.arange(tokens)
    lag_grid = positions[:, None] - positions[None, :]
    near_inside = (lag_grid >= 0) & (lag_grid < tap_count)
    near_taken = jnp.take(kernel, jnp.clip(lag_grid, 0, tap_count - 1), axis=1)
    near_matrix = jnp.where(near_inside[None], near_taken, jnp.zeros_like(near_taken))
    far_grid = lag_grid + tokens
    far_inside = far_grid < tap_count
    far_taken = jnp.take(kernel, jnp.clip(far_grid, 0, tap_count - 1), axis=1)
    far_matrix = jnp.where(far_inside[None], far_taken, jnp.zeros_like(far_taken))
    return (near_matrix, far_matrix)


def add_sources(pieces):
    return tuple((jnp.sum(member, axis=1) for member in pieces))


def shards(inputs, featurizer, short_filter, long_filter, decay_rate, skip_gain, output_grad):
    gathered = lax.all_gather(inputs, "tp", axis=0, tiled=True)
    tokens, blocks, block_rows = gathered.shape
    halo_rows = short_filter.shape[0] - 1
    channels = featurizer.shape[2]
    wide_columns = 3 * channels
    border = jnp.zeros((halo_rows, 1, block_rows), gathered.dtype)
    earlier_rows = jnp.concatenate([border, gathered[tokens - halo_rows :, : blocks - 1]], axis=1)
    extended = jnp.concatenate([earlier_rows, gathered], axis=0)
    flat_ext = extended.reshape((tokens + halo_rows) * blocks, block_rows)
    partials = [
        jnp.dot(flat_ext, featurizer[:, stream, :], preferred_element_type=jnp.float32).reshape(
            tokens + halo_rows, blocks, channels
        )
        for stream in range(3)
    ]
    summed = add_sources(
        (
            lax.all_to_all(
                partials[0].astype(jnp.bfloat16), "fsdp", split_axis=1, concat_axis=1, tiled=True
            ).astype(jnp.float32),
            lax.all_to_all(
                partials[1].astype(jnp.bfloat16), "fsdp", split_axis=1, concat_axis=1, tiled=True
            ).astype(jnp.float32),
            lax.all_to_all(
                partials[2].astype(jnp.bfloat16), "fsdp", split_axis=1, concat_axis=1, tiled=True
            ).astype(jnp.float32),
        )
    )
    features = jnp.stack([member.astype(jnp.bfloat16) for member in summed], axis=1)
    feat_wide = features.astype(jnp.float32)
    filtered = short_filter[0] * feat_wide[halo_rows:]
    for lag_step in range(1, halo_rows + 1):
        filtered = (
            filtered
            + short_filter[lag_step]
            * feat_wide[halo_rows - lag_step : halo_rows - lag_step + tokens]
        )
    queries = filtered[:, 0]
    key_part = filtered[:, 1]
    value_part = filtered[:, 2]
    product = key_part * value_part
    offsets = jnp.arange(long_filter.shape[1]).astype(jnp.float32)
    kernel = long_filter * jnp.exp(-decay_rate[:, None] * offsets[None, :])
    near_matrix, far_matrix = toeplitz_pair(kernel, tokens)
    filter_count = kernel.shape[0]
    group_width = channels // filter_count
    grouped = product.reshape(tokens, filter_count, group_width)
    local_conv = jnp.einsum(
        "nst,tnc->snc", near_matrix, grouped, precision=lax.Precision.HIGHEST
    ).reshape(tokens, channels)
    earlier = from_behind(product.astype(jnp.bfloat16), "fsdp", 1).astype(product.dtype)
    far_conv = jnp.einsum(
        "nst,tnc->snc",
        far_matrix,
        earlier.reshape(tokens, filter_count, group_width),
        precision=lax.Precision.HIGHEST,
    ).reshape(tokens, channels)
    convolved = local_conv + far_conv + skip_gain * product
    hyena_out = (queries * convolved).astype(jnp.bfloat16).reshape(tokens, 1, channels)
    upstream = output_grad.reshape(tokens, channels).astype(jnp.float32)
    query_grad = upstream * convolved
    conv_grad = upstream * queries
    conv_grouped = conv_grad.reshape(tokens, filter_count, group_width)
    local_back = jnp.einsum(
        "nst,snc->tnc", near_matrix, conv_grouped, precision=lax.Precision.HIGHEST
    ).reshape(tokens, channels)
    later_grad = from_behind(conv_grad.astype(jnp.bfloat16), "fsdp", -1).astype(conv_grad.dtype)
    far_back = jnp.einsum(
        "nst,snc->tnc",
        far_matrix,
        later_grad.reshape(tokens, filter_count, group_width),
        precision=lax.Precision.HIGHEST,
    ).reshape(tokens, channels)
    product_grad = local_back + far_back + skip_gain * conv_grad
    filtered_grad = jnp.stack(
        [query_grad, product_grad * value_part, product_grad * key_part], axis=1
    )
    next_head = from_behind(filtered_grad[:halo_rows], "fsdp", -1)
    padded = jnp.concatenate([filtered_grad, next_head], axis=0)
    feature_grad = short_filter[0] * filtered_grad
    for lag_step in range(1, halo_rows + 1):
        feature_grad = feature_grad + short_filter[lag_step] * padded[lag_step : lag_step + tokens]
    grad_own = feature_grad.astype(jnp.bfloat16).reshape(tokens, 1, wide_columns)
    grad_all = lax.all_gather(grad_own, "fsdp", axis=1, tiled=True)
    weight_block = featurizer.reshape(block_rows, wide_columns)
    weight_grad = lax.dot_general(
        gathered, grad_all, (((0, 1), (0, 1)), ((), ())), preferred_element_type=jnp.float32
    )
    weight_grad = weight_grad.astype(jnp.bfloat16).reshape(featurizer.shape)
    own_count = tokens // lax.axis_size("tp")
    flat_piece = grad_all.reshape(own_count * lax.axis_size("tp") * blocks, wide_columns)
    result = lax.dot_general(
        flat_piece, weight_block, (((1,), (1,)), ((), ())), preferred_element_type=jnp.float32
    )
    input_grad = lax.psum_scatter(
        result.reshape(own_count * lax.axis_size("tp"), blocks, block_rows).astype(jnp.bfloat16),
        "tp",
        scatter_dimension=0,
        tiled=True,
    )
    return (hyena_out, input_grad, weight_grad)


def solution(mesh):
    in_specs = (
        P("tp", None, "fsdp"),
        P("fsdp", None, "tp"),
        P(None, None, "tp"),
        P("tp", None),
        P("tp"),
        P("tp"),
        P(None, "fsdp", "tp"),
    )
    out_specs = (P(None, "fsdp", "tp"), P("tp", None, "fsdp"), P("fsdp", None, "tp"))
    return jax.shard_map(shards, mesh=mesh, in_specs=in_specs, out_specs=out_specs, check_vma=False)
```

profile of v0, /device:TPU:4, one launch (start us, length us, event | category | flops | bytes accessed | tf_op | source)
XLA Modules:
  0.0 920.4 jit_solution(7407251781027713006)
XLA Ops:
  7.2 0.7 all-gather.3.cloned.1.call-update
  7.9 139.1 %all-gather.3.cloned.1.call-done = bf16[128,16,512]{2,1,0:T(8,128)(2,1)} async-done(((bf16[4,16,512]{2,1,0:T(8,128)(2,1)}), bf16[128,16,512]{2,1,0:T(8,128)(2,1)}) %all-gather.3.cloned.1.call-update) | async-done | bytes 2097168 | tf_op jit(solution)/shard_map/all_gather | solution.py:32
  147.0 0.8 slice.71
  147.8 2.3 convolution_convert_fusion.3
  150.1 1.4 copy.59
  151.4 3.7 all-to-all-start
  155.2 2.3 convolution_convert_fusion.2
  157.5 1.4 copy.61
  158.9 42.5 %all-to-all-done = bf16[130,16,256]{2,0,1:T(8,128)(2,1)S(1)} async-done(((bf16[130,16,256]{2,0,1:T(8,128)(2,1)}), bf16[130,16,256]{2,0,1:T(8,128)(2,1)S(1)}, u32[]{:S(2)}, u32[]{:S(2)}) %all-to-all-start) | async-done | bytes 1064992 | tf_op jit(solution)/shard_map/all_to_all | solution.py:49
  201.3 11.8 %all-to-all-start.1 = ((bf16[130,16,256]{2,0,1:T(8,128)(2,1)}), bf16[130,16,256]{2,0,1:T(8,128)(2,1)S(1)}, u32[]{:S(2)}, u32[]{:S(2)}) async-start(bf16[130,16,256]{2,0,1:T(8,128)(2,1)} %copy.61), calls=%async_computation.1 | async-start | bytes 2228224 | tf_op jit(solution)/shard_map/all_to_all | solution.py:52
  213.1 2.3 convolution_convert_fusion.1
  215.4 1.4 copy.63
  216.8 42.5 %all-to-all-done.1 = bf16[130,16,256]{2,0,1:T(8,128)(2,1)S(1)} async-done(((bf16[130,16,256]{2,0,1:T(8,128)(2,1)}), bf16[130,16,256]{2,0,1:T(8,128)(2,1)S(1)}, u32[]{:S(2)}, u32[]{:S(2)}) %all-to-all-start.1) | async-done | bytes 1064992 | tf_op jit(solution)/shard_map/all_to_all | solution.py:52
  259.3 11.8 %all-to-all-start.2 = ((bf16[130,16,256]{2,0,1:T(8,128)(2,1)}), bf16[130,16,256]{2,0,1:T(8,128)(2,1)}, u32[]{:S(2)}, u32[]{:S(2)}) async-start(bf16[130,16,256]{2,0,1:T(8,128)(2,1)} %copy.63), calls=%async_computation.2 | async-start | bytes 2228224 | tf_op jit(solution)/shard_map/all_to_all | solution.py:55
  271.3 0.1 copy.66
  271.4 54.8 %gather_fusion = f32[16384,16]{1,0:T(8,128)} fusion(f32[16,128]{0,1:T(8,128)S(1)} %copy.66, s32[16384]{0:T(1024)S(1)} %bitcast_clamp_fusion.1), kind=kCustom, calls=%fused_computation.clone | custom fusion | bytes 2162688 | tf_op jit(solution)/shard_map/jit(_take)/gather | solution.py:18
  326.2 5.2 copy.67
  331.5 54.8 %gather_fusion.1 = f32[16384,16]{1,0:T(8,128)} fusion(f32[16,128]{0,1:T(8,128)S(1)} %copy.66, s32[16384]{0:T(1024)S(1)} %bitcast_clamp_fusion), kind=kCustom, calls=%fused_computation.1.clone | custom fusion | bytes 2162688 | tf_op jit(solution)/shard_map/jit(_take)/gather | solution.py:22
  386.3 5.2 copy.70
  391.7 0.2 reduce_sum.36
  391.8 1.4 reduce_sum.37
  393.3 1.4 reduce_sum.38
  394.7 0.1 fusion.27
  395.0 2.3 collective-permute-start
  397.4 1.7 fusion.7
  399.1 1.0 fusion.6
  400.2 1.4 collective-permute-start.1
  401.6 0.1 copy.68
  401.7 1.0 convolution_add_fusion.1
  402.7 0.1 copy.71
  402.8 1.8 collective-permute-done.1
  404.6 0.1 copy.73
  404.7 0.7 convolution_add_fusion
  405.4 0.1 copy.74
  405.5 0.7 slice_multiply_fusion.5
  406.2 1.4 collective-permute-start.2
  407.7 4.2 collective-permute-done.2
  411.9 0.1 fusion.25
  412.1 0.2 copy.75
  412.2 0.8 copy.76
  413.1 0.2 reduce-scatter.2.cloned.1.call-start
  413.3 0.3 copy.77
  413.6 102.8 %all-gather.5.cloned.1.call-done = bf16[128,16,768]{2,0,1:T(8,128)(2,1)} async-done(((bf16[128,1,768]{2,0,1:T(8,128)(2,1)}), bf16[128,16,768]{2,0,1:T(8,128)(2,1)}) %all-gather.5.cloned.1.call-update) | async-done | bytes 3145744 | tf_op jit(solution)/shard_map/all_gather | solution.py:115
  516.4 3.7 convolution_convert_fusion
  520.1 2.5 copy.79
  522.7 5.3 bitcast_convert_fusion
  528.0 1.2 copy.82
  529.2 384.7 %reduce-scatter.2.cloned.1.call-done = bf16[4,16,512]{2,1,0:T(8,128)(2,1)} async-done(((bf16[128,16,512]{2,1,0:T(8,128)(2,1)}), bf16[4,16,512]{2,1,0:T(8,128)(2,1)}) %reduce-scatter.2.cloned.1.call-update) | async-done | bytes 65552 | tf_op jit(solution)/shard_map/reduce_scatter | solution.py:126
  (39 shorter events, 0.7 us)
Async XLA Ops:
  7.2 139.8 %all-gather.3.cloned.1.call-start = ((), (), s32[]{:S(2)}) async-start(), calls=%async_computation.4 | async-start | bytes 2162688 | tf_op jit(solution)/shard_map/all_gather | solution.py:32
  150.1 5.1 copy-start.1
  151.4 49.9 %all-to-all-start = ((bf16[130,16,256]{2,0,1:T(8,128)(2,1)}), bf16[130,16,256]{2,0,1:T(8,128)(2,1)S(1)}, u32[]{:S(2)}, u32[]{:S(2)}) async-start(bf16[130,16,256]{2,0,1:T(8,128)(2,1)} %copy.59), calls=%async_computation | async-start | bytes 2228224 | tf_op jit(solution)/shard_map/all_to_all | solution.py:49
  201.3 58.0 %all-to-all-start.1 = ((bf16[130,16,256]{2,0,1:T(8,128)(2,1)}), bf16[130,16,256]{2,0,1:T(8,128)(2,1)S(1)}, u32[]{:S(2)}, u32[]{:S(2)}) async-start(bf16[130,16,256]{2,0,1:T(8,128)(2,1)} %copy.61), calls=%async_computation.1 | async-start | bytes 2228224 | tf_op jit(solution)/shard_map/all_to_all | solution.py:52
  215.4 55.7 %copy-start.8 = (f32[16]{0:T(128)S(1)}, f32[16]{0:T(128)}, u32[]{:S(2)}) copy-start(f32[16]{0:T(128)} %param.13) | copy-start | bytes 196
  215.4 55.8 %copy-start.5 = (f32[16,128]{1,0:T(8,128)S(1)}, f32[16,128]{1,0:T(8,128)}, u32[]{:S(2)}) copy-start(f32[16,128]{1,0:T(8,128)} %param.12) | copy-start | bytes 24580
  259.3 11.9 %copy-start = (bf16[130,16,256]{2,0,1:T(8,128)(2,1)}, bf16[130,16,256]{2,0,1:T(8,128)(2,1)S(1)}, u32[]{:S(2)}) copy-start(bf16[130,16,256]{2,0,1:T(8,128)(2,1)S(1)} %all-to-all-done.1) | copy-start | bytes 3194884
  259.3 134.0 %all-to-all-start.2 = ((bf16[130,16,256]{2,0,1:T(8,128)(2,1)}), bf16[130,16,256]{2,0,1:T(8,128)(2,1)}, u32[]{:S(2)}, u32[]{:S(2)}) async-start(bf16[130,16,256]{2,0,1:T(8,128)(2,1)} %copy.63), calls=%async_computation.2 | async-start | bytes 2228224 | tf_op jit(solution)/shard_map/all_to_all | solution.py:55
  271.1 245.4 %all-gather.5.cloned.1.call-start = ((), (), s32[]{:S(2)}) async-start(), calls=%async_computation.5 | async-start | bytes 3342336 | tf_op jit(solution)/shard_map/all_gather | solution.py:115
  386.3 5.3 copy-start.4
  391.8 3.0 copy-start.3
  395.0 6.6 collective-permute-start
  400.2 5.3 copy-start.6
  400.2 4.4 collective-permute-start.1
  406.2 7.1 copy-start.2
  406.2 5.6 collective-permute-start.2
  413.1 500.8 %reduce-scatter.2.cloned.1.call-start = ((), (), s32[]{:S(2)}) async-start(), calls=%async_computation.6 | async-start | bytes 2162688 | tf_op jit(solution)/shard_map/reduce_scatter | solution.py:126
  520.1 2.6 copy-start.7
Sparse Core Ops, SparseCore 0:
  12.3 134.6 all-gather.2
  413.2 103.1 all-gather.4
  522.8 391.0 reduce-scatter.1
where the time goes:
time: 921 us; the launch traced here: 920 us
  waiting for transfers between devices  718 us (78%)
  local copies, waits for them, and re-layouts  131 us (14%)
  starting transfers between devices  32.6 us (4%)
  matrix products  20.3 us (2%)
  between operations  14.1 us (2%)
    reduce_scatter x1, waiting for transfers between devices, shards(): lax.psum_scatter(result.reshape(own_count * lax.axis_size('tp'), blocks,...  385 us
    all_gather x1, waiting for transfers between devices, shards(): gathered = lax.all_gather(inputs, 'tp', axis=0, tiled=True)  139 us
    all_gather x1, waiting for transfers between devices, shards(): grad_all = lax.all_gather(grad_own, 'fsdp', axis=1, tiled=True)  103 us
    gather x2, local copies, waits for them, and re-layouts, toeplitz_pair(): far_taken = jnp.take(kernel, jnp.clip(far_grid, 0, tap_count - 1), axis=1)  60 us
    gather x2, local copies, waits for them, and re-layouts, toeplitz_pair(): near_taken = jnp.take(kernel, jnp.clip(lag_grid, 0, tap_count - 1), axis=1)  60 us
    all_to_all x1, waiting for transfers between devices, shards(): lax.all_to_all(partials[1].astype(jnp.bfloat16), 'fsdp', split_axis=1, co...  42.5 us
    all_to_all x1, waiting for transfers between devices, shards(): lax.all_to_all(partials[0].astype(jnp.bfloat16), 'fsdp', split_axis=1, co...  42.5 us
  transfers between devices with their start and end apart: 9, of which 7 were waited for; matrix products, arithmetic and copies ran while one was open for 15% of the time, Pallas kernels for 0%

commit v1 on v0

v1 whole, which is shorter than its diff:
```python
import functools
import math

import jax
import jax.numpy as jnp
from jax import lax
from jax.experimental import pallas as pl
from jax.experimental.pallas import tpu as pltpu
from jax.sharding import Mesh
from jax.sharding import PartitionSpec as P

F32 = jnp.float32
BF16 = jnp.bfloat16
INTERPRET = False


def call(body, outs, *args, scratch=()):
    whole = pl.BlockSpec(memory_space=pltpu.VMEM)
    many = isinstance(outs, (tuple, list))
    size = sum(math.prod(a.shape) * a.dtype.itemsize for a in args)
    return pl.pallas_call(
        body,
        out_shape=outs,
        in_specs=[whole] * len(args),
        out_specs=[whole] * len(outs) if many else whole,
        scratch_shapes=list(scratch),
        cost_estimate=pl.CostEstimate(flops=10**9, bytes_accessed=size, transcendentals=0),
        interpret=INTERPRET,
    )(*args)


def shape(dims, kind):
    return jax.ShapeDtypeStruct(dims, kind)


def dot(a, b):
    return jnp.dot(a, b, preferred_element_type=F32)


def dot_nt(a, b):
    return lax.dot_general(a, b, (((1,), (1,)), ((), ())), preferred_element_type=F32)


def bit_reversed(count):
    bits = count.bit_length() - 1
    return [int(format(i, f"0{bits}b")[::-1], 2) if bits else 0 for i in range(count)]


def row_order(pieces, members, tokens, inverse):
    rows = pieces * members * tokens
    r = lax.broadcasted_iota(jnp.int32, (rows, rows), 0)
    c = lax.broadcasted_iota(jnp.int32, (rows, rows), 1)
    if inverse:
        r, c = c, r
    member, rest = r // (pieces * tokens), r % (pieces * tokens)
    piece, token = rest // tokens, rest % tokens
    return jnp.where(c == (piece * members + member) * tokens + token, 1.0, 0.0).astype(BF16)


def token_order(half, tokens, count, inverse):
    r = lax.broadcasted_iota(jnp.int32, (count, count), 0)
    c = lax.broadcasted_iota(jnp.int32, (count, count), 1)
    if inverse:
        r, c = c, r
    piece, rest = r // (2 * tokens), r % (2 * tokens)
    side, token = rest // tokens, rest % tokens
    relative = jnp.where(side == half, 0, 1)
    return jnp.where(c == relative * (count // 2) + piece * tokens + token, 1.0, 0.0).astype(BF16)


def toeplitz_body(taps_ref, rev_ref, decay_ref, fwd_ref, bwd_ref):
    filters, taps = taps_ref.shape
    lag = lax.broadcasted_iota(jnp.int32, (1, taps), 1)
    back = jnp.where(lag == 0, 0, taps - lag)
    row = lax.broadcasted_iota(jnp.int32, (taps, taps), 0)
    col = lax.broadcasted_iota(jnp.int32, (taps, taps), 1)
    for n in range(filters):
        rate = -decay_ref[n : n + 1, :]
        plain = taps_ref[n : n + 1, :] * jnp.exp(rate * lag.astype(F32))
        turned = rev_ref[n : n + 1, :] * jnp.exp(rate * back.astype(F32))
        rows = slice(n * taps, (n + 1) * taps)
        for source, ref, near in ((turned, fwd_ref, col <= row), (plain, bwd_ref, col >= row)):
            ring = pltpu.roll(jnp.broadcast_to(source, (taps, taps)), 0, 1, stride=1, stride_axis=0)
            ref[rows, :taps] = jnp.where(near, ring, 0.0).astype(BF16)
            ref[rows, taps:] = jnp.where(near, 0.0, ring).astype(BF16)


def project_body(pieces, members, x_ref, own_ref, peer_ref, out_ref):
    rows, width = x_ref.shape
    half = width // 2
    order = row_order(pieces, members, rows // (pieces * members), False)
    x = dot(order, x_ref[...]).astype(BF16)
    streams, _, channels = own_ref.shape
    for i in range(streams):
        part = dot(x[:, :half], own_ref[i]) + dot(x[:, half:], peer_ref[i])
        out_ref[:, :, i * channels : (i + 1) * channels] = part.astype(BF16).reshape(
            members, rows // members, channels
        )


def back_body(pieces, members, g_ref, own_ref, peer_ref, out_ref, turned_ref):
    rows = g_ref.shape[0] * g_ref.shape[1]
    order = row_order(pieces, members, rows // (pieces * members), True)
    streams, half, channels = own_ref.shape
    g = dot(order, g_ref[...].reshape(rows, streams * channels)).astype(BF16)
    turned_ref[...] = g
    for side, ref in ((0, own_ref), (1, peer_ref)):
        total = dot_nt(g[:, :channels], ref[0])
        for i in range(1, streams):
            total = total + dot_nt(g[:, i * channels : (i + 1) * channels], ref[i])
        out_ref[:, side * half : (side + 1) * half] = total.astype(BF16)


def later(x, border, by):
    row = lax.broadcasted_iota(jnp.int32, x.shape, 0)
    moved = pltpu.roll(x, by, 0)
    for i in range(by):
        moved = jnp.where(row == i, border[8 - by + i : 9 - by + i], moved)
    return moved


def sooner(x, border, by):
    count = x.shape[0]
    row = lax.broadcasted_iota(jnp.int32, x.shape, 0)
    moved = pltpu.roll(x, count - by, 0)
    for i in range(by):
        moved = jnp.where(row == count - by + i, border[i : i + 1], moved)
    return moved


def gate_body(tokens, f0_ref, f1_ref, halo_ref, short_ref, up_ref, half_ref, q_ref, k_ref, v_ref, prod_ref, cg_ref):
    count = f0_ref.shape[0] * 2
    order = token_order(half_ref[0, 0], tokens, count, False)
    features = dot(order, jnp.concatenate([f0_ref[...], f1_ref[...]], axis=0))
    channels = up_ref.shape[1]
    outs = (q_ref, k_ref, v_ref)
    halo = halo_ref[...].astype(F32)
    for i in range(3):
        cols = slice(i * channels, (i + 1) * channels)
        x, border = features[:, cols], halo[:, cols]
        total = short_ref[0, i : i + 1] * x
        for lag in range(1, short_ref.shape[0]):
            total = total + short_ref[lag, i : i + 1] * later(x, border, lag)
        outs[i][...] = total
    prod_ref[...] = (k_ref[...] * v_ref[...]).astype(BF16)
    cg_ref[...] = (up_ref[...].astype(F32) * q_ref[...]).astype(BF16)


def convolve(t_ref, own, far):
    both = jnp.concatenate([own, far], axis=0)
    count, channels = own.shape
    filters = t_ref.shape[0] // count
    group = lax.broadcasted_iota(jnp.int32, (1, channels), 1) // (channels // filters)
    total = jnp.zeros((count, channels), F32)
    for n in range(filters):
        part = dot(t_ref[n * count : (n + 1) * count, :], both)
        total = jnp.where(group == n, part, total)
    return total


def hyena_body(fwd_ref, bwd_ref, prod_ref, prev_ref, cg_ref, next_ref, q_ref, k_ref, v_ref, up_ref, skip_ref, out_ref, fg_ref):
    channels = up_ref.shape[1]
    up, q, k, v, skip = up_ref[...].astype(F32), q_ref[...], k_ref[...], v_ref[...], skip_ref[...]
    convolved = convolve(fwd_ref, prod_ref[...], prev_ref[...]) + skip * (k * v)
    out_ref[...] = (q * convolved).astype(BF16)
    fg_ref[:, :channels] = up * convolved
    back = convolve(bwd_ref, cg_ref[...], next_ref[...]) + skip * (up * q)
    fg_ref[:, channels : 2 * channels] = back * v
    fg_ref[:, 2 * channels :] = back * k


def grad_body(tokens, fg_ref, head_ref, short_ref, half_ref, out0_ref, out1_ref):
    count, wide = fg_ref.shape
    channels = wide // 3
    order = token_order(half_ref[0, 0], tokens, count, True)
    for i in range(3):
        cols = slice(i * channels, (i + 1) * channels)
        x, border = fg_ref[:, cols], head_ref[:, cols]
        total = short_ref[0, i : i + 1] * x
        for lag in range(1, short_ref.shape[0]):
            total = total + short_ref[lag, i : i + 1] * sooner(x, border, lag)
        turned = dot(order, total.astype(BF16)).astype(BF16)
        out0_ref[:, cols] = turned[: count // 2]
        out1_ref[:, cols] = turned[count // 2 :]


def swap(x, axis, by=1):
    return lax.ppermute(x, axis, [(i, i ^ by) for i in range(lax.axis_size(axis))])


def shifted(x, by):
    axis = ("zl", "core")
    count = lax.axis_size("zl") * lax.axis_size("core")
    return lax.ppermute(x, axis, [(i, i + by) for i in range(count) if 0 <= i + by < count])


def line_scatter(x):
    count, by = x.shape[0], 1
    while count > 1:
        half = count // 2
        got = swap(x[half:], "zl", by)
        x = (x[:half].astype(F32) + got.astype(F32)).astype(BF16)
        count, by = half, by * 2
    return x[0]


def line_gather(x):
    x = x[None]
    by = lax.axis_size("zl") // 2
    while by:
        x = jnp.concatenate([x, swap(x, "zl", by)], axis=0)
        by //= 2
    return x


def shards(inputs, featurizer, short_filter, long_filter, decay_rate, skip_gain, output_grad):
    tokens, blocks, rows = inputs.shape
    members = lax.axis_size("zl")
    pieces = lax.axis_size("x") * lax.axis_size("y")
    channels = featurizer.shape[2]
    wide = 3 * channels
    count = output_grad.shape[0]
    zl, core, zh = lax.axis_index("zl"), lax.axis_index("core"), lax.axis_index("zh")
    short_filter = short_filter.astype(F32)

    w_own = featurizer.transpose(1, 0, 2)
    w_peer = swap(w_own, "core")
    rolled = jnp.roll(long_filter[:, ::-1], 1, axis=1)
    matrix = shape((long_filter.shape[0] * count, 2 * count), BF16)
    t_fwd, t_bwd = call(toeplitz_body, (matrix, matrix), long_filter, rolled, decay_rate[:, None])

    order = jnp.array(bit_reversed(members), jnp.int32)
    wanted = (((order ^ zl) * 2)[None, :] + (jnp.arange(2, dtype=jnp.int32) ^ core)[:, None]).reshape(-1)
    pick = (wanted[:, None] == jnp.arange(blocks, dtype=jnp.int32)[None, :]).astype(BF16)
    sorted_in = jnp.einsum("kb,tbd->ktd", pick, inputs, preferred_element_type=F32).astype(BF16)
    mine, other = sorted_in[:members], sorted_in[members:]
    local = jnp.concatenate([mine, swap(other, "core")], axis=2).reshape(members * tokens, 2 * rows)

    def spread(x):
        wider = jnp.broadcast_to(x[None], (pieces, *x.shape))
        return lax.all_to_all(wider, ("x", "y"), 0, 0, tiled=True).reshape(-1, x.shape[1])

    far = swap(local, "zh")
    project = functools.partial(project_body, pieces, members)
    part_shape = shape((members, pieces * tokens, wide), BF16)
    x_near = spread(local)
    f_near = line_scatter(call(project, part_shape, x_near, w_own, w_peer))
    x_far = spread(far)
    f_far = line_scatter(call(project, part_shape, x_far, w_own, w_peer))

    last = jnp.where(zh == 1, f_near[-8:], f_far[-8:])
    halo = shifted(last, 1)
    half = zh.astype(jnp.int32).reshape(1, 1)
    upstream = output_grad.reshape(count, channels)
    plane = shape((count, channels), F32)
    thin = shape((count, channels), BF16)
    q, k, v, prod, cg = call(
        functools.partial(gate_body, tokens), (plane, plane, plane, thin, thin), f_near, f_far, halo, short_filter, upstream, half
    )
    prev, nxt = shifted(prod, 1), shifted(cg, -1)
    hyena, fg = call(
        hyena_body,
        (thin, shape((count, wide), F32)),
        t_fwd, t_bwd, prod, prev, cg, nxt, q, k, v, upstream, skip_gain[None, :],
    )
    head = shifted(fg[:8], -1)
    piece_shape = shape((count // 2, wide), BF16)
    g_near, g_far = call(functools.partial(grad_body, tokens), (piece_shape, piece_shape), fg, head, short_filter, half)
    back = functools.partial(back_body, pieces, members)
    back_shapes = (shape((members * pieces * tokens, 2 * rows), BF16), shape((members * pieces * tokens, wide), BF16))

    def collect(x):
        x = lax.all_to_all(x.reshape(pieces, members * tokens, 2 * rows), ("x", "y"), 0, 0, tiled=True)
        return jnp.sum(x.astype(F32), axis=0)

    d_far, turned_far = call(back, back_shapes, line_gather(g_far), w_own, w_peer)
    sent = swap(collect(d_far).astype(BF16), "zh")
    d_near, turned_near = call(back, back_shapes, line_gather(g_near), w_own, w_peer)
    total = (collect(d_near) + sent.astype(F32)).astype(BF16).reshape(members, tokens, 2 * rows)
    both = jnp.concatenate([total[:, :, :rows], swap(total[:, :, rows:], "core")], axis=0)
    input_grad = jnp.einsum("kb,ktd->tbd", pick, both, preferred_element_type=F32).astype(BF16)

    def outer(x, g):
        return lax.dot_general(x, g, (((0,), (0,)), ((), ())), preferred_element_type=F32)

    w_grad = outer(x_near, turned_near) + outer(x_far, turned_far)
    w_far = swap(w_grad[rows:].astype(BF16), "core")
    weight_grad = (w_grad[:rows] + w_far.astype(F32)).astype(BF16).reshape(featurizer.shape)
    return (hyena.reshape(output_grad.shape), input_grad, weight_grad)


def solution(mesh):
    fsdp, tp = (mesh.shape[name] for name in ("fsdp", "tp"))
    side = math.isqrt(tp // 2)
    fine = Mesh(mesh.devices.reshape(fsdp // 2, 2, side, side, 2), ("zl", "core", "x", "y", "zh"))
    f, t = ("zl", "core"), ("x", "y", "zh")
    in_specs = (P(t, None, f), P(f, None, t), P(None, None, t), P(t, None), P(t), P(t), P(None, f, t))
    out_specs = (P(None, f, t), P(t, None, f), P(f, None, t))
    return jax.shard_map(shards, mesh=fine, in_specs=in_specs, out_specs=out_specs, check_vma=False)
```

time: 921 us -> 265 us (0.29)
  the two profiles are of different devices: /device:TPU:4 before, /device:TPU:1 now
where the time goes in v1:
time: 265 us; the launch traced here: 264 us
  starting transfers between devices  121 us (46%)
  waiting for transfers between devices  85.3 us (32%)
  Pallas kernels  27.6 us (10%)
  local copies, waits for them, and re-layouts  12.9 us (5%)
  other arithmetic  12.7 us (5%)
  matrix products  3.09 us (1%)
    ppermute x18, starting transfers between devices, swap(): lax.ppermute(x, axis, [(i, i ^ by) for i in range(lax.axis_size(axis))])  88.3 us
    ppermute x18, waiting for transfers between devices, swap(): lax.ppermute(x, axis, [(i, i ^ by) for i in range(lax.axis_size(axis))])  73.1 us
    pallas_call x8, Pallas kernels, call(): pl.pallas_call(body, out_shape=outs, in_specs=[whole] * len(args), out_sp...  27.6 us
    all_to_all x2, starting transfers between devices, collect(): lax.all_to_all(x.reshape(pieces, members * tokens, 2 * rows), ('x', 'y'),...  13.2 us
    all_to_all x2, starting transfers between devices, spread(): lax.all_to_all(wider, ('x', 'y'), 0, 0, tiled=True).reshape(-1, x.shape[1])  10.1 us
    ppermute x4, starting transfers between devices, shifted(): lax.ppermute(x, axis, [(i, i + by) for i in range(count) if 0 <= i + by <...  9.4 us
    all_to_all x2, waiting for transfers between devices, spread(): lax.all_to_all(wider, ('x', 'y'), 0, 0, tiled=True).reshape(-1, x.shape[1])  6.8 us
    unnamed x41, local copies, waits for them, and re-layouts  5.55 us
  transfers between devices with their start and end apart: 26, of which 14 were waited for; matrix products, arithmetic and copies ran while one was open for 7% of the time, Pallas kernels for 8%

profile of v1, /device:TPU:1, one launch (start us, length us, event | category | flops | bytes accessed | tf_op | source)
XLA Modules:
  0.0 263.8 jit_solution(8297849608738301979)
XLA Ops:
  1.8 8.7 %collective-permute-start = (bf16[8,4,512]{2,0,1:T(8,128)(2,1)S(1)}, bf16[8,4,512]{2,0,1:T(8,128)(2,1)S(1)}, u32[]{:S(2)}, u32[]{:S(2)}) collective-permute-start(bf16[8,4,512]{2,0,1:T(8,128)(2,1)S(1)} %get-tuple-element.42), channel_id=1, source_target_pairs={{0,32},{32,0},{1,33},{33,1},{2,34},{34,2},{3,35},{35,3},{4,36},{36... | collective-permute-start | bytes 98312 | tf_op jit(solution)/shard_map/ppermute | solution.py:188
  12.6 3.7 %all-to-all-start = ((bf16[16,32,1024]{2,1,0:T(8,128)(2,1)}), bf16[16,32,1024]{2,1,0:T(8,128)(2,1)S(1)}, u32[]{:S(2)}, u32[]{:S(2)}) async-start(bf16[16,32,1024]{2,1,0:T(8,128)(2,1)} %broadcast_in_dim.30), calls=%async_computation | async-start | bytes 2097152 | tf_op jit(solution)/shard_map/all_to_all | solution.py:241
  16.2 13.2 %collective-permute-start.5 = (bf16[32,1024]{1,0:T(8,128)(2,1)S(1)}, bf16[32,1024]{1,0:T(8,128)(2,1)S(1)}, u32[]{:S(2)}, u32[]{:S(2)}) collective-permute-start(bf16[32,1024]{1,0:T(8,128)(2,1)S(1)} %broadcast_in_dim.29), channel_id=1, source_target_pairs={{0,1},{1,0},{2,3},{3,2},{4,5},{5,4},{6,7},{7,6},{8,9},{9,8},{10,11... | collective-permute-start | bytes 196616 | tf_op jit(solution)/shard_map/ppermute | solution.py:188
  29.5 2.8 %collective-permute-start.1 = (bf16[3,512,256]{2,1,0:T(8,128)(2,1)S(1)}, bf16[3,512,256]{2,1,0:T(8,128)(2,1)}, u32[]{:S(2)}, u32[]{:S(2)}) collective-permute-start(bf16[3,512,256]{2,1,0:T(8,128)(2,1)S(1)} %bitcast.53), channel_id=1, source_target_pairs={{0,32},{32,0},{1,33},{33,1},{2,34},{34,2},{3,35},{35,3},{4,36},{36... | collective-permute-start | bytes 2359304 | tf_op jit(solution)/shard_map/ppermute | solution.py:188
  34.0 6.5 %all-to-all-start.1 = ((bf16[16,32,1024]{2,1,0:T(8,128)(2,1)}), bf16[16,32,1024]{2,1,0:T(8,128)(2,1)S(1)}, u32[]{:S(2)}, u32[]{:S(2)}) async-start(bf16[16,32,1024]{2,1,0:T(8,128)(2,1)} %broadcast_in_dim.31), calls=%async_computation.1 | async-start | bytes 2097152 | tf_op jit(solution)/shard_map/all_to_all | solution.py:241
  40.5 4.5 %shard_map.104 = bf16[8,64,768]{2,1,0:T(8,128)(2,1)} custom-call(bf16[512,1024]{1,0:T(8,128)(2,1)} %bitcast.32, bf16[3,512,256]{2,1,0:T(8,128)(2,1)} %bitcast.49, bf16[3,512,256]{2,1,0:T(8,128)(2,1)} %collective-permute-done.1.peer_ref), custom_call_target="tpu_custom_call" | custom-call | flops 1000000000 | bytes 2621440 | tf_op jit(solution)/shard_map/pallas_call | solution.py:21
  46.1 2.6 %collective-permute-start.2 = (bf16[4,64,768]{2,1,0:T(8,128)(2,1)S(1)}, bf16[4,64,768]{2,1,0:T(8,128)(2,1)S(1)}, u32[]{:S(2)}, u32[]{:S(2)}) collective-permute-start(bf16[4,64,768]{2,1,0:T(8,128)(2,1)S(1)} %slice.105), channel_id=1, source_target_pairs={{0,64},{64,0},{128,192},{192,128},{256,320},{320,256},{384,448},{4... | collective-permute-start | bytes 1179656 | tf_op jit(solution)/shard_map/ppermute | solution.py:188
  48.8 6.4 %all-to-all-done.1 = bf16[16,32,1024]{2,1,0:T(8,128)(2,1)S(1)} async-done(((bf16[16,32,1024]{2,1,0:T(8,128)(2,1)}), bf16[16,32,1024]{2,1,0:T(8,128)(2,1)S(1)}, u32[]{:S(2)}, u32[]{:S(2)}) %all-to-all-start.1) | async-done | bytes 1048608 | tf_op jit(solution)/shard_map/all_to_all | solution.py:241
  56.1 4.5 %shard_map.105 = bf16[8,64,768]{2,1,0:T(8,128)(2,1)} custom-call(bf16[512,1024]{1,0:T(8,128)(2,1)} %bitcast.30, bf16[3,512,256]{2,1,0:T(8,128)(2,1)} %bitcast.50, bf16[3,512,256]{2,1,0:T(8,128)(2,1)} %collective-permute-done.1.peer_ref), custom_call_target="tpu_custom_call" | custom-call | flops 1000000000 | bytes 2621440 | tf_op jit(solution)/shard_map/pallas_call | solution.py:21
  61.6 3.2 %collective-permute-start.6 = (bf16[4,64,768]{2,1,0:T(8,128)(2,1)S(1)}, bf16[4,64,768]{2,1,0:T(8,128)(2,1)S(1)}, u32[]{:S(2)}, u32[]{:S(2)}) collective-permute-start(bf16[4,64,768]{2,1,0:T(8,128)(2,1)S(1)} %slice.111), channel_id=1, source_target_pairs={{0,64},{64,0},{128,192},{192,128},{256,320},{320,256},{384,448},{4... | collective-permute-start | bytes 1179656 | tf_op jit(solution)/shard_map/ppermute | solution.py:188
  65.1 2.3 collective-permute-start.3
  67.4 5.3 %collective-permute-done.6 = bf16[4,64,768]{2,1,0:T(8,128)(2,1)S(1)} collective-permute-done((bf16[4,64,768]{2,1,0:T(8,128)(2,1)S(1)}, bf16[4,64,768]{2,1,0:T(8,128)(2,1)S(1)}, u32[]{:S(2)}, u32[]{:S(2)}) %collective-permute-start.6) | collective-permute-done | bytes 393248 | tf_op jit(solution)/shard_map/ppermute | solution.py:188
  73.8 2.0 collective-permute-start.7
  75.9 10.6 %collective-permute-start.4 = (bf16[1,64,768]{2,1,0:T(8,128)(2,1)S(1)}, bf16[1,64,768]{2,1,0:T(8,128)(2,1)S(1)}, u32[]{:S(2)}, u32[]{:S(2)}) collective-permute-start(bf16[1,64,768]{2,1,0:T(8,128)(2,1)S(1)} %slice.109), channel_id=1, source_target_pairs={{0,256},{64,320},{128,384},{192,448},{256,0},{320,64},{384,128},{4... | collective-permute-start | bytes 294920 | tf_op jit(solution)/shard_map/ppermute | solution.py:188
  86.6 12.6 %collective-permute-start.8 = (bf16[1,64,768]{2,1,0:T(8,128)(2,1)S(1)}, bf16[1,64,768]{2,1,0:T(8,128)(2,1)S(1)}, u32[]{:S(2)}, u32[]{:S(2)}) collective-permute-start(bf16[1,64,768]{2,1,0:T(8,128)(2,1)S(1)} %slice.115), channel_id=1, source_target_pairs={{0,256},{64,320},{128,384},{192,448},{256,0},{320,64},{384,128},{4... | collective-permute-start | bytes 294920 | tf_op jit(solution)/shard_map/ppermute | solution.py:188
  99.2 10.4 %collective-permute-done.8 = bf16[1,64,768]{2,1,0:T(8,128)(2,1)S(1)} collective-permute-done((bf16[1,64,768]{2,1,0:T(8,128)(2,1)S(1)}, bf16[1,64,768]{2,1,0:T(8,128)(2,1)S(1)}, u32[]{:S(2)}, u32[]{:S(2)}) %collective-permute-start.8) | collective-permute-done | bytes 98336 | tf_op jit(solution)/shard_map/ppermute | solution.py:188
  109.7 1.9 collective-permute-start.9
  113.6 2.0 shard_map.106
  115.6 3.6 %collective-permute-start.10 = (bf16[128,256]{1,0:T(8,128)(2,1)}, bf16[128,256]{1,0:T(8,128)(2,1)S(1)}, u32[]{:S(2)}, u32[]{:S(2)}) collective-permute-start(bf16[128,256]{1,0:T(8,128)(2,1)} %get-tuple-element.20.prod_ref), channel_id=1, source_target_pairs={{0,32},{32,64},{64,96},{96,128},{128,160},{160,192},{192,224},{224... | collective-permute-start | bytes 196616 | tf_op jit(solution)/shard_map/ppermute | solution.py:194
  119.2 1.9 collective-permute-start.11
  121.2 3.4 %shard_map.103 = (bf16[2048,256]{1,0:T(8,128)(2,1)}, bf16[2048,256]{1,0:T(8,128)(2,1)}) custom-call(f32[16,128]{1,0:T(8,128)} %taps_ref.1, f32[16,128]{1,0:T(8,128)} %pad_maximum_fusion.7.rev_ref, f32[16,1]{1,0:T(8,128)} %copy.14.decay_ref), custom_call_target="tpu_custom_call" | custom-call | flops 1000000000 | bytes 16448 | tf_op jit(solution)/shard_map/pallas_call | solution.py:21
  125.6 3.2 %shard_map.107 = (bf16[128,256]{1,0:T(8,128)(2,1)}, f32[128,768]{1,0:T(8,128)}) custom-call(bf16[2048,256]{1,0:T(8,128)(2,1)} %get-tuple-element.18.fwd_ref, bf16[2048,256]{1,0:T(8,128)(2,1)} %get-tuple-element.19.bwd_ref, bf16[128,256]{1,0:T(8,128)(2,1)} %get-tuple-element.20.prod_ref, bf16[128,256]{1,0:T(8,128)(2,1)} %copy-done.15, ...), custom_call_target="tpu_custom_call" | custom-call | flops 1000000000 | bytes 2819072 | tf_op jit(solution)/shard_map/pallas_call | solution.py:21
  129.6 1.9 collective-permute-start.12
  131.5 3.2 %collective-permute-done.12.head_ref = f32[8,768]{1,0:T(8,128)S(1)} collective-permute-done((f32[8,768]{1,0:T(8,128)S(1)}, f32[8,768]{1,0:T(8,128)S(1)}, u32[]{:S(2)}, u32[]{:S(2)}) %collective-permute-start.12) | collective-permute-done | bytes 24608 | tf_op jit(solution)/shard_map/ppermute | solution.py:194
  135.3 2.0 shard_map.108
  137.3 5.1 %collective-permute-start.16 = (bf16[1,64,768]{2,1,0:T(8,128)(2,1)}, bf16[1,64,768]{2,1,0:T(8,128)(2,1)S(1)}, u32[]{:S(2)}, u32[]{:S(2)}) collective-permute-start(bf16[1,64,768]{2,1,0:T(8,128)(2,1)} %bitcast.41), channel_id=1, source_target_pairs={{0,256},{64,320},{128,384},{192,448},{256,0},{320,64},{384,128},{4... | collective-permute-start | bytes 294920 | tf_op jit(solution)/shard_map/ppermute | solution.py:188
  142.4 11.0 %collective-permute-done.16 = bf16[1,64,768]{2,1,0:T(8,128)(2,1)S(1)} collective-permute-done((bf16[1,64,768]{2,1,0:T(8,128)(2,1)}, bf16[1,64,768]{2,1,0:T(8,128)(2,1)S(1)}, u32[]{:S(2)}, u32[]{:S(2)}) %collective-permute-start.16) | collective-permute-done | bytes 98336 | tf_op jit(solution)/shard_map/ppermute | solution.py:188
  154.3 1.9 collective-permute-start.17
  156.3 8.7 %collective-permute-done.17 = bf16[2,64,768]{2,1,0:T(8,128)(2,1)S(1)} collective-permute-done((bf16[2,64,768]{2,1,0:T(8,128)(2,1)S(1)}, bf16[2,64,768]{2,1,0:T(8,128)(2,1)S(1)}, u32[]{:S(2)}, u32[]{:S(2)}) %collective-permute-start.17) | collective-permute-done | bytes 196640 | tf_op jit(solution)/shard_map/ppermute | solution.py:188
  165.9 1.9 collective-permute-start.18
  167.9 3.1 %collective-permute-start.13 = (bf16[1,64,768]{2,1,0:T(8,128)(2,1)}, bf16[1,64,768]{2,1,0:T(8,128)(2,1)S(1)}, u32[]{:S(2)}, u32[]{:S(2)}) collective-permute-start(bf16[1,64,768]{2,1,0:T(8,128)(2,1)} %bitcast.37), channel_id=1, source_target_pairs={{0,256},{64,320},{128,384},{192,448},{256,0},{320,64},{384,128},{4... | collective-permute-start | bytes 294920 | tf_op jit(solution)/shard_map/ppermute | solution.py:188
  171.0 8.3 %collective-permute-done.18 = bf16[4,64,768]{2,1,0:T(8,128)(2,1)S(1)} collective-permute-done((bf16[4,64,768]{2,1,0:T(8,128)(2,1)S(1)}, bf16[4,64,768]{2,1,0:T(8,128)(2,1)S(1)}, u32[]{:S(2)}, u32[]{:S(2)}) %collective-permute-start.18) | collective-permute-done | bytes 393248 | tf_op jit(solution)/shard_map/ppermute | solution.py:188
  179.3 1.9 pad_maximum_fusion.1.g_ref
  181.2 4.0 %shard_map.110 = (bf16[512,1024]{1,0:T(8,128)(2,1)}, bf16[512,768]{1,0:T(8,128)(2,1)}) custom-call(bf16[8,64,768]{2,1,0:T(8,128)(2,1)} %pad_maximum_fusion.1.g_ref, bf16[3,512,256]{2,1,0:T(8,128)(2,1)} %bitcast.51, bf16[3,512,256]{2,1,0:T(8,128)(2,1)} %collective-permute-done.1.peer_ref), custom_call_target="tpu_custom_call" | custom-call | flops 1000000000 | bytes 2359296 | tf_op jit(solution)/shard_map/pallas_call | solution.py:21
  185.2 6.5 %all-to-all-start.3 = ((bf16[16,32,1024]{2,1,0:T(8,128)(2,1)}), bf16[16,32,1024]{2,1,0:T(8,128)(2,1)S(1)}, u32[]{:S(2)}, u32[]{:S(2)}) async-start(bf16[16,32,1024]{2,1,0:T(8,128)(2,1)} %bitcast.35), calls=%async_computation.3 | async-start | bytes 2097152 | tf_op jit(solution)/shard_map/all_to_all | solution.py:273
  191.7 5.1 %collective-permute-start.14 = (bf16[2,64,768]{2,1,0:T(8,128)(2,1)S(1)}, bf16[2,64,768]{2,1,0:T(8,128)(2,1)S(1)}, u32[]{:S(2)}, u32[]{:S(2)}) collective-permute-start(bf16[2,64,768]{2,1,0:T(8,128)(2,1)S(1)} %pad_maximum_fusion.4), channel_id=1, source_target_pairs={{0,128},{64,192},{128,0},{192,64},{256,384},{320,448},{384,256},{4... | collective-permute-start | bytes 589832 | tf_op jit(solution)/shard_map/ppermute | solution.py:188
  196.9 9.6 %collective-permute-done.14 = bf16[2,64,768]{2,1,0:T(8,128)(2,1)S(1)} collective-permute-done((bf16[2,64,768]{2,1,0:T(8,128)(2,1)S(1)}, bf16[2,64,768]{2,1,0:T(8,128)(2,1)S(1)}, u32[]{:S(2)}, u32[]{:S(2)}) %collective-permute-start.14) | collective-permute-done | bytes 196640 | tf_op jit(solution)/shard_map/ppermute | solution.py:188
  206.5 1.9 collective-permute-start.15
  208.4 10.1 %collective-permute-done.15 = bf16[4,64,768]{2,1,0:T(8,128)(2,1)S(1)} collective-permute-done((bf16[4,64,768]{2,1,0:T(8,128)(2,1)S(1)}, bf16[4,64,768]{2,1,0:T(8,128)(2,1)S(1)}, u32[]{:S(2)}, u32[]{:S(2)}) %collective-permute-start.15) | collective-permute-done | bytes 393248 | tf_op jit(solution)/shard_map/ppermute | solution.py:188
  219.5 4.1 %shard_map.109 = (bf16[512,1024]{1,0:T(8,128)(2,1)}, bf16[512,768]{1,0:T(8,128)(2,1)}) custom-call(bf16[8,64,768]{2,1,0:T(8,128)(2,1)} %pad_maximum_fusion.g_ref, bf16[3,512,256]{2,1,0:T(8,128)(2,1)} %bitcast.52, bf16[3,512,256]{2,1,0:T(8,128)(2,1)} %collective-permute-done.1.peer_ref), custom_call_target="tpu_custom_call" | custom-call | flops 1000000000 | bytes 2359296 | tf_op jit(solution)/shard_map/pallas_call | solution.py:21
  223.6 6.7 %all-to-all-start.2 = ((bf16[16,32,1024]{2,1,0:T(8,128)(2,1)}), bf16[16,32,1024]{2,1,0:T(8,128)(2,1)}, u32[]{:S(2)}, u32[]{:S(2)}) async-start(bf16[16,32,1024]{2,1,0:T(8,128)(2,1)} %bitcast.36), calls=%async_computation.2 | async-start | bytes 2097152 | tf_op jit(solution)/shard_map/all_to_all | solution.py:273
  233.9 3.5 %collective-permute-start.21 = (bf16[512,768]{0,1:T(8,128)(2,1)}, bf16[512,768]{0,1:T(8,128)(2,1)}, u32[]{:S(2)}, u32[]{:S(2)}) collective-permute-start(bf16[512,768]{0,1:T(8,128)(2,1)} %slice.136), channel_id=1, source_target_pairs={{0,32},{32,0},{1,33},{33,1},{2,34},{34,2},{3,35},{35,3},{4,36},{36... | collective-permute-start | bytes 2359304 | tf_op jit(solution)/shard_map/ppermute | solution.py:188
  238.9 5.2 %collective-permute-start.19 = (bf16[32,1024]{1,0:T(8,128)(2,1)S(1)}, bf16[32,1024]{1,0:T(8,128)(2,1)S(1)}, u32[]{:S(2)}, u32[]{:S(2)}) collective-permute-start(bf16[32,1024]{1,0:T(8,128)(2,1)S(1)} %reduce_sum.22), channel_id=1, source_target_pairs={{0,1},{1,0},{2,3},{3,2},{4,5},{5,4},{6,7},{7,6},{8,9},{9,8},{10,11... | collective-permute-start | bytes 196616 | tf_op jit(solution)/shard_map/ppermute | solution.py:188
  244.1 1.6 all-to-all-done.2
  247.1 8.8 %collective-permute-done.19 = bf16[32,1024]{1,0:T(8,128)(2,1)S(1)} collective-permute-done((bf16[32,1024]{1,0:T(8,128)(2,1)S(1)}, bf16[32,1024]{1,0:T(8,128)(2,1)S(1)}, u32[]{:S(2)}, u32[]{:S(2)}) %collective-permute-start.19) | collective-permute-done | bytes 65568 | tf_op jit(solution)/shard_map/ppermute | solution.py:188
  256.0 2.4 collective-permute-start.20
  258.4 2.3 fusion
  260.7 2.3 copy.19
  (98 shorter events, 24.0 us)
Async XLA Ops:
  0.6 0.9 copy-start
  0.6 28.8 %copy-start.14 = (bf16[512,3,256]{2,0,1:T(8,128)(2,1)S(1)}, bf16[512,3,256]{2,0,1:T(8,128)(2,1)}, u32[]{:S(2)}) copy-start(bf16[512,3,256]{2,0,1:T(8,128)(2,1)} %param.9) | copy-start | bytes 2359300
  1.8 9.6 %collective-permute-start = (bf16[8,4,512]{2,0,1:T(8,128)(2,1)S(1)}, bf16[8,4,512]{2,0,1:T(8,128)(2,1)S(1)}, u32[]{:S(2)}, u32[]{:S(2)}) collective-permute-start(bf16[8,4,512]{2,0,1:T(8,128)(2,1)S(1)} %get-tuple-element.42), channel_id=1, source_target_pairs={{0,32},{32,0},{1,33},{33,1},{2,34},{34,2},{3,35},{35,3},{4,36},{36... | collective-permute-start | bytes 98312 | tf_op jit(solution)/shard_map/ppermute | solution.py:188
  12.6 20.2 %all-to-all-start = ((bf16[16,32,1024]{2,1,0:T(8,128)(2,1)}), bf16[16,32,1024]{2,1,0:T(8,128)(2,1)S(1)}, u32[]{:S(2)}, u32[]{:S(2)}) async-start(bf16[16,32,1024]{2,1,0:T(8,128)(2,1)} %broadcast_in_dim.30), calls=%async_computation | async-start | bytes 2097152 | tf_op jit(solution)/shard_map/all_to_all | solution.py:241
  16.2 16.0 %collective-permute-start.5 = (bf16[32,1024]{1,0:T(8,128)(2,1)S(1)}, bf16[32,1024]{1,0:T(8,128)(2,1)S(1)}, u32[]{:S(2)}, u32[]{:S(2)}) collective-permute-start(bf16[32,1024]{1,0:T(8,128)(2,1)S(1)} %broadcast_in_dim.29), channel_id=1, source_target_pairs={{0,1},{1,0},{2,3},{3,2},{4,5},{5,4},{6,7},{7,6},{8,9},{9,8},{10,11... | collective-permute-start | bytes 196616 | tf_op jit(solution)/shard_map/ppermute | solution.py:188
  29.5 11.0 %collective-permute-start.1 = (bf16[3,512,256]{2,1,0:T(8,128)(2,1)S(1)}, bf16[3,512,256]{2,1,0:T(8,128)(2,1)}, u32[]{:S(2)}, u32[]{:S(2)}) collective-permute-start(bf16[3,512,256]{2,1,0:T(8,128)(2,1)S(1)} %bitcast.53), channel_id=1, source_target_pairs={{0,32},{32,0},{1,33},{33,1},{2,34},{34,2},{3,35},{35,3},{4,36},{36... | collective-permute-start | bytes 2359304 | tf_op jit(solution)/shard_map/ppermute | solution.py:188
  32.7 7.8 %copy-start.4 = (bf16[16,32,1024]{2,1,0:T(8,128)(2,1)}, bf16[16,32,1024]{2,1,0:T(8,128)(2,1)S(1)}, u32[]{:S(2)}) copy-start(bf16[16,32,1024]{2,1,0:T(8,128)(2,1)S(1)} %all-to-all-done) | copy-start | bytes 3145732
  34.0 21.1 %all-to-all-start.1 = ((bf16[16,32,1024]{2,1,0:T(8,128)(2,1)}), bf16[16,32,1024]{2,1,0:T(8,128)(2,1)S(1)}, u32[]{:S(2)}, u32[]{:S(2)}) async-start(bf16[16,32,1024]{2,1,0:T(8,128)(2,1)} %broadcast_in_dim.31), calls=%async_computation.1 | async-start | bytes 2097152 | tf_op jit(solution)/shard_map/all_to_all | solution.py:241
  45.0 19.8 %copy-start.12 = (f32[16,128]{1,0:T(8,128)S(1)}, f32[16,128]{1,0:T(8,128)}, u32[]{:S(2)}) copy-start(f32[16,128]{1,0:T(8,128)} %taps_ref.1) | copy-start | bytes 24580
  45.0 20.0 %copy-start.8 = (bf16[8,64,768]{2,1,0:T(8,128)(2,1)S(1)}, bf16[8,64,768]{2,1,0:T(8,128)(2,1)}, u32[]{:S(2)}) copy-start(bf16[8,64,768]{2,1,0:T(8,128)(2,1)} %shard_map.104) | copy-start | bytes 2359300
  46.1 18.9 %collective-permute-start.2 = (bf16[4,64,768]{2,1,0:T(8,128)(2,1)S(1)}, bf16[4,64,768]{2,1,0:T(8,128)(2,1)S(1)}, u32[]{:S(2)}, u32[]{:S(2)}) collective-permute-start(bf16[4,64,768]{2,1,0:T(8,128)(2,1)S(1)} %slice.105), channel_id=1, source_target_pairs={{0,64},{64,0},{128,192},{192,128},{256,320},{320,256},{384,448},{4... | collective-permute-start | bytes 1179656 | tf_op jit(solution)/shard_map/ppermute | solution.py:188
  55.1 1.0 copy-start.1
  60.6 51.7 %copy-start.13 = (f32[16]{0:T(128)S(1)}, f32[16]{0:T(128)}, u32[]{:S(2)}) copy-start(f32[16]{0:T(128)} %param.12) | copy-start | bytes 196
  61.6 11.1 %collective-permute-start.6 = (bf16[4,64,768]{2,1,0:T(8,128)(2,1)S(1)}, bf16[4,64,768]{2,1,0:T(8,128)(2,1)S(1)}, u32[]{:S(2)}, u32[]{:S(2)}) collective-permute-start(bf16[4,64,768]{2,1,0:T(8,128)(2,1)S(1)} %slice.111), channel_id=1, source_target_pairs={{0,64},{64,0},{128,192},{192,128},{256,320},{320,256},{384,448},{4... | collective-permute-start | bytes 1179656 | tf_op jit(solution)/shard_map/ppermute | solution.py:188
  65.1 10.7 %collective-permute-start.3 = (bf16[2,64,768]{2,1,0:T(8,128)(2,1)S(1)}, bf16[2,64,768]{2,1,0:T(8,128)(2,1)S(1)}, u32[]{:S(2)}, u32[]{:S(2)}) collective-permute-start(bf16[2,64,768]{2,1,0:T(8,128)(2,1)S(1)} %slice.107), channel_id=1, source_target_pairs={{0,128},{64,192},{128,0},{192,64},{256,384},{320,448},{384,256},{4... | collective-permute-start | bytes 589832 | tf_op jit(solution)/shard_map/ppermute | solution.py:188
  73.8 12.7 %collective-permute-start.7 = (bf16[2,64,768]{2,1,0:T(8,128)(2,1)S(1)}, bf16[2,64,768]{2,1,0:T(8,128)(2,1)S(1)}, u32[]{:S(2)}, u32[]{:S(2)}) collective-permute-start(bf16[2,64,768]{2,1,0:T(8,128)(2,1)S(1)} %slice.113), channel_id=1, source_target_pairs={{0,128},{64,192},{128,0},{192,64},{256,384},{320,448},{384,256},{4... | collective-permute-start | bytes 589832 | tf_op jit(solution)/shard_map/ppermute | solution.py:188
  75.9 23.3 %collective-permute-start.4 = (bf16[1,64,768]{2,1,0:T(8,128)(2,1)S(1)}, bf16[1,64,768]{2,1,0:T(8,128)(2,1)S(1)}, u32[]{:S(2)}, u32[]{:S(2)}) collective-permute-start(bf16[1,64,768]{2,1,0:T(8,128)(2,1)S(1)} %slice.109), channel_id=1, source_target_pairs={{0,256},{64,320},{128,384},{192,448},{256,0},{320,64},{384,128},{4... | collective-permute-start | bytes 294920 | tf_op jit(solution)/shard_map/ppermute | solution.py:188
  86.6 23.1 %collective-permute-start.8 = (bf16[1,64,768]{2,1,0:T(8,128)(2,1)S(1)}, bf16[1,64,768]{2,1,0:T(8,128)(2,1)S(1)}, u32[]{:S(2)}, u32[]{:S(2)}) collective-permute-start(bf16[1,64,768]{2,1,0:T(8,128)(2,1)S(1)} %slice.115), channel_id=1, source_target_pairs={{0,256},{64,320},{128,384},{192,448},{256,0},{320,64},{384,128},{4... | collective-permute-start | bytes 294920 | tf_op jit(solution)/shard_map/ppermute | solution.py:188
  99.2 13.8 %copy-start.10 = (bf16[1,64,768]{2,1,0:T(8,128)(2,1)}, bf16[1,64,768]{2,1,0:T(8,128)(2,1)S(1)}, u32[]{:S(2)}) copy-start(bf16[1,64,768]{2,1,0:T(8,128)(2,1)S(1)} %add_convert_fusion.5) | copy-start | bytes 294916
  109.7 3.3 %copy-start.11 = (bf16[1,64,768]{2,1,0:T(8,128)(2,1)}, bf16[1,64,768]{2,1,0:T(8,128)(2,1)S(1)}, u32[]{:S(2)}) copy-start(bf16[1,64,768]{2,1,0:T(8,128)(2,1)S(1)} %add_convert_fusion.4) | copy-start | bytes 294916
  109.7 3.3 %collective-permute-start.9 = (bf16[8,768]{1,0:T(8,128)(2,1)S(1)}, bf16[8,768]{1,0:T(8,128)(2,1)S(1)}, u32[]{:S(2)}, u32[]{:S(2)}) collective-permute-start(bf16[8,768]{1,0:T(8,128)(2,1)S(1)} %fusion.5), channel_id=1, source_target_pairs={{0,32},{32,64},{64,96},{96,128},{128,160},{160,192},{192,224},{224... | collective-permute-start | bytes 36872 | tf_op jit(solution)/shard_map/ppermute | solution.py:194
  113.0 0.6 copy-start.18
  115.6 8.9 %collective-permute-start.10 = (bf16[128,256]{1,0:T(8,128)(2,1)}, bf16[128,256]{1,0:T(8,128)(2,1)S(1)}, u32[]{:S(2)}, u32[]{:S(2)}) collective-permute-start(bf16[128,256]{1,0:T(8,128)(2,1)} %get-tuple-element.20.prod_ref), channel_id=1, source_target_pairs={{0,32},{32,64},{64,96},{96,128},{128,160},{160,192},{192,224},{224... | collective-permute-start | bytes 196616 | tf_op jit(solution)/shard_map/ppermute | solution.py:194
  119.2 5.8 %collective-permute-start.11 = (bf16[128,256]{1,0:T(8,128)(2,1)}, bf16[128,256]{1,0:T(8,128)(2,1)S(1)}, u32[]{:S(2)}, u32[]{:S(2)}) collective-permute-start(bf16[128,256]{1,0:T(8,128)(2,1)} %get-tuple-element.21.cg_ref), channel_id=1, source_target_pairs={{32,0},{64,32},{96,64},{128,96},{160,128},{192,160},{224,192},{256... | collective-permute-start | bytes 196616 | tf_op jit(solution)/shard_map/ppermute | solution.py:194
  124.5 0.6 copy-start.15
  125.0 0.6 copy-start.16
  129.6 5.1 %collective-permute-start.12 = (f32[8,768]{1,0:T(8,128)S(1)}, f32[8,768]{1,0:T(8,128)S(1)}, u32[]{:S(2)}, u32[]{:S(2)}) collective-permute-start(f32[8,768]{1,0:T(8,128)S(1)} %slice.97), channel_id=1, source_target_pairs={{32,0},{64,32},{96,64},{128,96},{160,128},{192,160},{224,192},{256... | collective-permute-start | bytes 73736 | tf_op jit(solution)/shard_map/ppermute | solution.py:194
  134.7 0.6 copy-start.17
  137.3 16.1 %collective-permute-start.16 = (bf16[1,64,768]{2,1,0:T(8,128)(2,1)}, bf16[1,64,768]{2,1,0:T(8,128)(2,1)S(1)}, u32[]{:S(2)}, u32[]{:S(2)}) collective-permute-start(bf16[1,64,768]{2,1,0:T(8,128)(2,1)} %bitcast.41), channel_id=1, source_target_pairs={{0,256},{64,320},{128,384},{192,448},{256,0},{320,64},{384,128},{4... | collective-permute-start | bytes 294920 | tf_op jit(solution)/shard_map/ppermute | solution.py:188
  154.3 10.7 %collective-permute-start.17 = (bf16[2,64,768]{2,1,0:T(8,128)(2,1)S(1)}, bf16[2,64,768]{2,1,0:T(8,128)(2,1)S(1)}, u32[]{:S(2)}, u32[]{:S(2)}) collective-permute-start(bf16[2,64,768]{2,1,0:T(8,128)(2,1)S(1)} %pad_maximum_fusion.5), channel_id=1, source_target_pairs={{0,128},{64,192},{128,0},{192,64},{256,384},{320,448},{384,256},{4... | collective-permute-start | bytes 589832 | tf_op jit(solution)/shard_map/ppermute | solution.py:188
  165.9 13.4 %collective-permute-start.18 = (bf16[4,64,768]{2,1,0:T(8,128)(2,1)S(1)}, bf16[4,64,768]{2,1,0:T(8,128)(2,1)S(1)}, u32[]{:S(2)}, u32[]{:S(2)}) collective-permute-start(bf16[4,64,768]{2,1,0:T(8,128)(2,1)S(1)} %pad_maximum_fusion.3), channel_id=1, source_target_pairs={{0,64},{64,0},{128,192},{192,128},{256,320},{320,256},{384,448},{4... | collective-permute-start | bytes 1179656 | tf_op jit(solution)/shard_map/ppermute | solution.py:188
  167.9 23.8 %collective-permute-start.13 = (bf16[1,64,768]{2,1,0:T(8,128)(2,1)}, bf16[1,64,768]{2,1,0:T(8,128)(2,1)S(1)}, u32[]{:S(2)}, u32[]{:S(2)}) collective-permute-start(bf16[1,64,768]{2,1,0:T(8,128)(2,1)} %bitcast.37), channel_id=1, source_target_pairs={{0,256},{64,320},{128,384},{192,448},{256,0},{320,64},{384,128},{4... | collective-permute-start | bytes 294920 | tf_op jit(solution)/shard_map/ppermute | solution.py:188
  181.2 10.6 %copy-start.6 = (bf16[64,768]{1,0:T(8,128)(2,1)S(1)}, bf16[64,768]{1,0:T(8,128)(2,1)}, u32[]{:S(2)}) copy-start(bf16[64,768]{1,0:T(8,128)(2,1)} %get-tuple-element.27) | copy-start | bytes 294916
  185.2 38.5 %all-to-all-start.3 = ((bf16[16,32,1024]{2,1,0:T(8,128)(2,1)}), bf16[16,32,1024]{2,1,0:T(8,128)(2,1)S(1)}, u32[]{:S(2)}, u32[]{:S(2)}) async-start(bf16[16,32,1024]{2,1,0:T(8,128)(2,1)} %bitcast.35), calls=%async_computation.3 | async-start | bytes 2097152 | tf_op jit(solution)/shard_map/all_to_all | solution.py:273
  191.7 14.7 %collective-permute-start.14 = (bf16[2,64,768]{2,1,0:T(8,128)(2,1)S(1)}, bf16[2,64,768]{2,1,0:T(8,128)(2,1)S(1)}, u32[]{:S(2)}, u32[]{:S(2)}) collective-permute-start(bf16[2,64,768]{2,1,0:T(8,128)(2,1)S(1)} %pad_maximum_fusion.4), channel_id=1, source_target_pairs={{0,128},{64,192},{128,0},{192,64},{256,384},{320,448},{384,256},{4... | collective-permute-start | bytes 589832 | tf_op jit(solution)/shard_map/ppermute | solution.py:188
  206.5 12.1 %collective-permute-start.15 = (bf16[4,64,768]{2,1,0:T(8,128)(2,1)S(1)}, bf16[4,64,768]{2,1,0:T(8,128)(2,1)S(1)}, u32[]{:S(2)}, u32[]{:S(2)}) collective-permute-start(bf16[4,64,768]{2,1,0:T(8,128)(2,1)S(1)} %pad_maximum_fusion.2), channel_id=1, source_target_pairs={{0,64},{64,0},{128,192},{192,128},{256,320},{320,256},{384,448},{4... | collective-permute-start | bytes 1179656 | tf_op jit(solution)/shard_map/ppermute | solution.py:188
  219.5 10.8 %copy-start.2 = (bf16[16,32,1024]{2,1,0:T(8,128)(2,1)S(1)}, bf16[16,32,1024]{2,1,0:T(8,128)(2,1)}, u32[]{:S(2)}) copy-start(bf16[16,32,1024]{2,1,0:T(8,128)(2,1)} %copy-done.1) | copy-start | bytes 3145732
  219.5 10.8 %copy-start.7 = (bf16[512,768]{1,0:T(8,128)(2,1)S(1)}, bf16[512,768]{1,0:T(8,128)(2,1)}, u32[]{:S(2)}) copy-start(bf16[512,768]{1,0:T(8,128)(2,1)} %get-tuple-element.32) | copy-start | bytes 2359300
  223.6 7.8 %copy-start.3 = (bf16[16,32,1024]{2,1,0:T(8,128)(2,1)}, bf16[16,32,1024]{2,1,0:T(8,128)(2,1)S(1)}, u32[]{:S(2)}) copy-start(bf16[16,32,1024]{2,1,0:T(8,128)(2,1)S(1)} %all-to-all-done.3) | copy-start | bytes 3145732
  223.6 22.1 %all-to-all-start.2 = ((bf16[16,32,1024]{2,1,0:T(8,128)(2,1)}), bf16[16,32,1024]{2,1,0:T(8,128)(2,1)}, u32[]{:S(2)}, u32[]{:S(2)}) async-start(bf16[16,32,1024]{2,1,0:T(8,128)(2,1)} %bitcast.36), calls=%async_computation.2 | async-start | bytes 2097152 | tf_op jit(solution)/shard_map/all_to_all | solution.py:273
  230.4 1.2 copy-start.5
  230.4 1.4 copy-start.9
  233.9 24.5 %collective-permute-start.21 = (bf16[512,768]{0,1:T(8,128)(2,1)}, bf16[512,768]{0,1:T(8,128)(2,1)}, u32[]{:S(2)}, u32[]{:S(2)}) collective-permute-start(bf16[512,768]{0,1:T(8,128)(2,1)} %slice.136), channel_id=1, source_target_pairs={{0,32},{32,0},{1,33},{33,1},{2,34},{34,2},{3,35},{35,3},{4,36},{36... | collective-permute-start | bytes 2359304 | tf_op jit(solution)/shard_map/ppermute | solution.py:188
  238.9 17.0 %collective-permute-start.19 = (bf16[32,1024]{1,0:T(8,128)(2,1)S(1)}, bf16[32,1024]{1,0:T(8,128)(2,1)S(1)}, u32[]{:S(2)}, u32[]{:S(2)}) collective-permute-start(bf16[32,1024]{1,0:T(8,128)(2,1)S(1)} %reduce_sum.22), channel_id=1, source_target_pairs={{0,1},{1,0},{2,3},{3,2},{4,5},{5,4},{6,7},{7,6},{8,9},{9,8},{10,11... | collective-permute-start | bytes 196616 | tf_op jit(solution)/shard_map/ppermute | solution.py:188
  256.0 7.0 %collective-permute-start.20 = (bf16[8,4,512]{2,0,1:T(8,128)(2,1)S(1)}, bf16[8,4,512]{2,0,1:T(8,128)(2,1)S(1)}, u32[]{:S(2)}, u32[]{:S(2)}) collective-permute-start(bf16[8,4,512]{2,0,1:T(8,128)(2,1)S(1)} %copy.23), channel_id=1, source_target_pairs={{0,32},{32,0},{1,33},{33,1},{2,34},{34,2},{3,35},{35,3},{4,36},{36... | collective-permute-start | bytes 98312 | tf_op jit(solution)/shard_map/ppermute | solution.py:188

commit v2 on v1

--- a/solution.py
+++ b/solution.py
@@ -16,12 +16,13 @@
 
 def call(body, outs, *args, scratch=()):
     whole = pl.BlockSpec(memory_space=pltpu.VMEM)
+    scalar = pl.BlockSpec(memory_space=pltpu.SMEM)
     many = isinstance(outs, (tuple, list))
     size = sum(math.prod(a.shape) * a.dtype.itemsize for a in args)
     return pl.pallas_call(
         body,
         out_shape=outs,
-        in_specs=[whole] * len(args),
+        in_specs=[scalar if a.shape == (1,) else whole for a in args],
         out_specs=[whole] * len(outs) if many else whole,
         scratch_shapes=list(scratch),
         cost_estimate=pl.CostEstimate(flops=10**9, bytes_accessed=size, transcendentals=0),
@@ -39,6 +40,10 @@
 
 def dot_nt(a, b):
     return lax.dot_general(a, b, (((1,), (1,)), ((), ())), preferred_element_type=F32)
+
+
+def dot_tn(a, b):
+    return lax.dot_general(a, b, (((0,), (0,)), ((), ())), preferred_element_type=F32)
 
 
 def bit_reversed(count):
@@ -85,30 +90,42 @@
             ref[rows, taps:] = jnp.where(near, 0.0, ring).astype(BF16)
 
 
-def project_body(pieces, members, x_ref, own_ref, peer_ref, out_ref):
-    rows, width = x_ref.shape
-    half = width // 2
+def project_body(pieces, members, core_ref, x_ref, own_ref, peer_ref, keep_ref, send_ref):
+    core = core_ref[0]
+    rows = x_ref.shape[1]
     order = row_order(pieces, members, rows // (pieces * members), False)
-    x = dot(order, x_ref[...]).astype(BF16)
+    mine = dot(order, x_ref[core]).astype(BF16)
+    theirs = dot(order, x_ref[1 - core]).astype(BF16)
     streams, _, channels = own_ref.shape
+    half = rows // 2
     for i in range(streams):
-        part = dot(x[:, :half], own_ref[i]) + dot(x[:, half:], peer_ref[i])
-        out_ref[:, :, i * channels : (i + 1) * channels] = part.astype(BF16).reshape(
-            members, rows // members, channels
-        )
-
-
-def back_body(pieces, members, g_ref, own_ref, peer_ref, out_ref, turned_ref):
+        cols = slice(i * channels, (i + 1) * channels)
+        part = (dot(mine, own_ref[i]) + dot(theirs, peer_ref[i])).astype(BF16)
+        keep_ref[:, :, cols] = part[:half].reshape(members // 2, rows // members, channels)
+        send_ref[:, :, cols] = part[half:].reshape(members // 2, rows // members, channels)
+
+
+def back_body(pieces, members, core_ref, g_ref, own_ref, peer_ref, out_ref, turned_ref):
+    core = core_ref[0]
     rows = g_ref.shape[0] * g_ref.shape[1]
     order = row_order(pieces, members, rows // (pieces * members), True)
-    streams, half, channels = own_ref.shape
+    streams, _, channels = own_ref.shape
     g = dot(order, g_ref[...].reshape(rows, streams * channels)).astype(BF16)
     turned_ref[...] = g
-    for side, ref in ((0, own_ref), (1, peer_ref)):
+    for place, ref in ((core, own_ref), (1 - core, peer_ref)):
         total = dot_nt(g[:, :channels], ref[0])
         for i in range(1, streams):
             total = total + dot_nt(g[:, i * channels : (i + 1) * channels], ref[i])
-        out_ref[:, side * half : (side + 1) * half] = total.astype(BF16)
+        out_ref[place] = total.astype(BF16)
+
+
+def weight_body(core_ref, x0_ref, x1_ref, g0_ref, g1_ref, own_ref, peer_ref):
+    core = core_ref[0]
+    streams, _, channels = own_ref.shape
+    for place, ref in ((core, own_ref), (1 - core, peer_ref)):
+        for i in range(streams):
+            cols = slice(i * channels, (i + 1) * channels)
+            ref[i] = (dot_tn(x0_ref[place], g0_ref[:, cols]) + dot_tn(x1_ref[place], g1_ref[:, cols])).astype(ref.dtype)
 
 
 def later(x, border, by):
@@ -130,7 +147,7 @@
 
 def gate_body(tokens, f0_ref, f1_ref, halo_ref, short_ref, up_ref, half_ref, q_ref, k_ref, v_ref, prod_ref, cg_ref):
     count = f0_ref.shape[0] * 2
-    order = token_order(half_ref[0, 0], tokens, count, False)
+    order = token_order(half_ref[0], tokens, count, False)
     features = dot(order, jnp.concatenate([f0_ref[...], f1_ref[...]], axis=0))
     channels = up_ref.shape[1]
     outs = (q_ref, k_ref, v_ref)
@@ -158,7 +175,7 @@
     return total
 
 
-def hyena_body(fwd_ref, bwd_ref, prod_ref, prev_ref, cg_ref, next_ref, q_ref, k_ref, v_ref, up_ref, skip_ref, out_ref, fg_ref):
+def hyena_body(fwd_ref, bwd_ref, prod_ref, prev_ref, cg_ref, next_ref, q_ref, k_ref, v_ref, up_ref, skip_ref, out_ref, fg_ref, head_ref):
     channels = up_ref.shape[1]
     up, q, k, v, skip = up_ref[...].astype(F32), q_ref[...], k_ref[...], v_ref[...], skip_ref[...]
     convolved = convolve(fwd_ref, prod_ref[...], prev_ref[...]) + skip * (k * v)
@@ -167,12 +184,13 @@
     back = convolve(bwd_ref, cg_ref[...], next_ref[...]) + skip * (up * q)
     fg_ref[:, channels : 2 * channels] = back * v
     fg_ref[:, 2 * channels :] = back * k
+    head_ref[...] = fg_ref[:8]
 
 
 def grad_body(tokens, fg_ref, head_ref, short_ref, half_ref, out0_ref, out1_ref):
     count, wide = fg_ref.shape
     channels = wide // 3
-    order = token_order(half_ref[0, 0], tokens, count, True)
+    order = token_order(half_ref[0], tokens, count, True)
     for i in range(3):
         cols = slice(i * channels, (i + 1) * channels)
         x, border = fg_ref[:, cols], head_ref[:, cols]
@@ -194,63 +212,71 @@
     return lax.ppermute(x, axis, [(i, i + by) for i in range(count) if 0 <= i + by < count])
 
 
-def line_scatter(x):
-    count, by = x.shape[0], 1
-    while count > 1:
+def line_scatter(keep, send):
+    count, by = keep.shape[0], 1
+    while True:
+        got = swap(send, "zl", by)
+        if count == 1:
+            return (keep[0].astype(F32) + got[0].astype(F32)).astype(BF16)
         half = count // 2
-        got = swap(x[half:], "zl", by)
-        x = (x[:half].astype(F32) + got.astype(F32)).astype(BF16)
+        send = (keep[half:].astype(F32) + got[half:].astype(F32)).astype(BF16)
+        keep = (keep[:half].astype(F32) + got[:half].astype(F32)).astype(BF16)
         count, by = half, by * 2
-    return x[0]
-
-
-def line_gather(x):
+
+
+def line_gather(x, tie=None):
     x = x[None]
     by = lax.axis_size("zl") // 2
     while by:
+        if by == 1 and tie is not None:
+            x, tie = lax.optimization_barrier((x, tie))
         x = jnp.concatenate([x, swap(x, "zl", by)], axis=0)
         by //= 2
-    return x
+    return x if tie is None else (x, tie)
 
 
 def shards(inputs, featurizer, short_filter, long_filter, decay_rate, skip_gain, output_grad):
     tokens, blocks, rows = inputs.shape
     members = lax.axis_size("zl")
     pieces = lax.axis_size("x") * lax.axis_size("y")
+    lines = members * tokens
     channels = featurizer.shape[2]
     wide = 3 * channels
     count = output_grad.shape[0]
     zl, core, zh = lax.axis_index("zl"), lax.axis_index("core"), lax.axis_index("zh")
-    short_filter = short_filter.astype(F32)
-
+    here = core.astype(jnp.int32).reshape(1)
+    half = zh.astype(jnp.int32).reshape(1)
+
+    order = jnp.array(bit_reversed(members), jnp.int32) ^ zl
+    block = (order[None, :] * 2 + jnp.arange(2, dtype=jnp.int32)[:, None]).reshape(-1, 1)
+    source = (jnp.arange(tokens, dtype=jnp.int32)[None, :] * blocks + block).reshape(-1, 1)
+    pick = (source == jnp.arange(tokens * blocks, dtype=jnp.int32)[None, :]).astype(BF16)
+    local = dot(pick, inputs.reshape(tokens * blocks, rows)).astype(BF16).reshape(2, 1, lines, rows)
+
+    def exchange(x):
+        x = lax.all_to_all(x.reshape(2 * pieces, lines, rows), ("core", "x", "y"), 0, 0, tiled=True)
+        return x.reshape(2, pieces, lines, rows)
+
+    def spread(x):
+        return exchange(jnp.broadcast_to(x, (2, pieces, lines, rows))).reshape(2, pieces * lines, rows)
+
+    x_near = spread(local)
+    far = swap(local, "zh")
     w_own = featurizer.transpose(1, 0, 2)
     w_peer = swap(w_own, "core")
     rolled = jnp.roll(long_filter[:, ::-1], 1, axis=1)
     matrix = shape((long_filter.shape[0] * count, 2 * count), BF16)
     t_fwd, t_bwd = call(toeplitz_body, (matrix, matrix), long_filter, rolled, decay_rate[:, None])
-
-    order = jnp.array(bit_reversed(members), jnp.int32)
-    wanted = (((order ^ zl) * 2)[None, :] + (jnp.arange(2, dtype=jnp.int32) ^ core)[:, None]).reshape(-1)
-    pick = (wanted[:, None] == jnp.arange(blocks, dtype=jnp.int32)[None, :]).astype(BF16)
-    sorted_in = jnp.einsum("kb,tbd->ktd", pick, inputs, preferred_element_type=F32).astype(BF16)
-    mine, other = sorted_in[:members], sorted_in[members:]
-    local = jnp.concatenate([mine, swap(other, "core")], axis=2).reshape(members * tokens, 2 * rows)
-
-    def spread(x):
-        wider = jnp.broadcast_to(x[None], (pieces, *x.shape))
-        return lax.all_to_all(wider, ("x", "y"), 0, 0, tiled=True).reshape(-1, x.shape[1])
-
-    far = swap(local, "zh")
+    x_near, t_fwd, t_bwd = lax.optimization_barrier((x_near, t_fwd, t_bwd))
+
     project = functools.partial(project_body, pieces, members)
-    part_shape = shape((members, pieces * tokens, wide), BF16)
-    x_near = spread(local)
-    f_near = line_scatter(call(project, part_shape, x_near, w_own, w_peer))
+    part_shape = (shape((members // 2, pieces * tokens, wide), BF16),) * 2
+    f_near = line_scatter(*call(project, part_shape, here, x_near, w_own, w_peer))
     x_far = spread(far)
-    f_far = line_scatter(call(project, part_shape, x_far, w_own, w_peer))
+    f_far = line_scatter(*call(project, part_shape, here, x_far, w_own, w_peer))
 
     last = jnp.where(zh == 1, f_near[-8:], f_far[-8:])
     halo = shifted(last, 1)
-    half = zh.astype(jnp.int32).reshape(1, 1)
     upstream = output_grad.reshape(count, channels)
     plane = shape((count, channels), F32)
     thin = shape((count, channels), BF16)
@@ -258,34 +284,30 @@
         functools.partial(gate_body, tokens), (plane, plane, plane, thin, thin), f_near, f_far, halo, short_filter, upstream, half
     )
     prev, nxt = shifted(prod, 1), shifted(cg, -1)
-    hyena, fg = call(
+    hyena, fg, head = call(
         hyena_body,
-        (thin, shape((count, wide), F32)),
+        (thin, shape((count, wide), F32), shape((8, wide), F32)),
         t_fwd, t_bwd, prod, prev, cg, nxt, q, k, v, upstream, skip_gain[None, :],
     )
-    head = shifted(fg[:8], -1)
+    head = shifted(head, -1)
     piece_shape = shape((count // 2, wide), BF16)
     g_near, g_far = call(functools.partial(grad_body, tokens), (piece_shape, piece_shape), fg, head, short_filter, half)
     back = functools.partial(back_body, pieces, members)
-    back_shapes = (shape((members * pieces * tokens, 2 * rows), BF16), shape((members * pieces * tokens, wide), BF16))
+    back_shapes = (shape((2, pieces * lines, rows), BF16), shape((pieces * lines, wide), BF16))
 
     def collect(x):
-        x = lax.all_to_all(x.reshape(pieces, members * tokens, 2 * rows), ("x", "y"), 0, 0, tiled=True)
-        return jnp.sum(x.astype(F32), axis=0)
-
-    d_far, turned_far = call(back, back_shapes, line_gather(g_far), w_own, w_peer)
-    sent = swap(collect(d_far).astype(BF16), "zh")
-    d_near, turned_near = call(back, back_shapes, line_gather(g_near), w_own, w_peer)
-    total = (collect(d_near) + sent.astype(F32)).astype(BF16).reshape(members, tokens, 2 * rows)
-    both = jnp.concatenate([total[:, :, :rows], swap(total[:, :, rows:], "core")], axis=0)
-    input_grad = jnp.einsum("kb,ktd->tbd", pick, both, preferred_element_type=F32).astype(BF16)
-
-    def outer(x, g):
-        return lax.dot_general(x, g, (((0,), (0,)), ((), ())), preferred_element_type=F32)
-
-    w_grad = outer(x_near, turned_near) + outer(x_far, turned_far)
-    w_far = swap(w_grad[rows:].astype(BF16), "core")
-    weight_grad = (w_grad[:rows] + w_far.astype(F32)).astype(BF16).reshape(featurizer.shape)
+        return jnp.sum(exchange(x).astype(F32), axis=1)
+
+    d_far, turned_far = call(back, back_shapes, here, line_gather(g_far), w_own, w_peer)
+    s_far = collect(d_far).astype(BF16)
+    all_near, s_far = line_gather(g_near, s_far)
+    sent = swap(s_far, "zh")
+    d_near, turned_near = call(back, back_shapes, here, all_near, w_own, w_peer)
+    weight_shape = (3, rows, channels)
+    w_grad, w_far = call(weight_body, (shape(weight_shape, F32), shape(weight_shape, BF16)), here, x_near, x_far, turned_near, turned_far)
+    weight_grad = (w_grad + swap(w_far, "core").astype(F32)).astype(BF16).transpose(1, 0, 2)
+    total = (collect(d_near) + sent.astype(F32)).astype(BF16).reshape(2 * lines, rows)
+    input_grad = dot_tn(pick, total).astype(BF16).reshape(inputs.shape)
     return (hyena.reshape(output_grad.shape), input_grad, weight_grad)
 
 

time: 265 us -> 270 us (1.019)
  waiting for transfers between devices: 85.3 us -> 105 us
  starting transfers between devices: 121 us -> 114 us
  local copies, waits for them, and re-layouts: 12.9 us -> 6.37 us
  Pallas kernels: 27.6 us -> 32.2 us
  other arithmetic: 12.7 us -> 9.67 us
    ppermute x18 -> x16, starting transfers between devices: 88.3 us -> 71.8 us  [swap(): lax.ppermute(x, axis, [(i, i ^ by) for i in range(lax.axis_size(axis))])]
    ppermute x18 -> x16, waiting for transfers between devices: 73.1 us -> 88.9 us  [swap(): lax.ppermute(x, axis, [(i, i ^ by) for i in range(lax.axis_size(axis))])]
    all_to_all x4, starting transfers between devices: 23.4 us -> 32.5 us  [exchange(): lax.all_to_all(x.reshape(2 * pieces, lines, rows), ('core', 'x', 'y'), 0,...]
    ppermute x4, waiting for transfers between devices: 3.72 us -> 8.42 us  [shifted(): lax.ppermute(x, axis, [(i, i + by) for i in range(count) if 0 <= i + by <...]
    pallas_call x8 -> x9, Pallas kernels: 27.6 us -> 32.2 us  [call(): pl.pallas_call(body, out_shape=outs, in_specs=[scalar if a.shape == (1,)...]
    slice x10 -> x0, local copies, waits for them, and re-layouts: 3.95 us -> none  [the longest x6 2.18 us: line_scatter(): got = swap(x[half:], 'zl', by)]
    unnamed x41 -> x30, local copies, waits for them, and re-layouts: 5.55 us -> 3 us
  transfers between devices with their start and end apart: 26 -> 24, of which waited for: 14 -> 15; matrix products, arithmetic and copies ran while one was open for 7% -> 2% of each run, Pallas kernels for 8% -> 5%
where the time goes in v2:
time: 270 us; the launch traced here: 269 us
  starting transfers between devices  114 us (42%)
  waiting for transfers between devices  105 us (39%)
  Pallas kernels  32.2 us (12%)
  other arithmetic  9.67 us (4%)
  local copies, waits for them, and re-layouts  6.37 us (2%)
    ppermute x16, waiting for transfers between devices, swap(): lax.ppermute(x, axis, [(i, i ^ by) for i in range(lax.axis_size(axis))])  88.9 us
    ppermute x16, starting transfers between devices, swap(): lax.ppermute(x, axis, [(i, i ^ by) for i in range(lax.axis_size(axis))])  71.8 us
    all_to_all x4, starting transfers between devices, exchange(): lax.all_to_all(x.reshape(2 * pieces, lines, rows), ('core', 'x', 'y'), 0,...  32.5 us
    pallas_call x9, Pallas kernels, call(): pl.pallas_call(body, out_shape=outs, in_specs=[scalar if a.shape == (1,)...  32.2 us
    ppermute x4, starting transfers between devices, shifted(): lax.ppermute(x, axis, [(i, i + by) for i in range(count) if 0 <= i + by <...  9.6 us
    ppermute x4, waiting for transfers between devices, shifted(): lax.ppermute(x, axis, [(i, i + by) for i in range(count) if 0 <= i + by <...  8.42 us
    all_to_all x4, waiting for transfers between devices, exchange(): lax.all_to_all(x.reshape(2 * pieces, lines, rows), ('core', 'x', 'y'), 0,...  7.27 us
  transfers between devices with their start and end apart: 24, of which 15 were waited for; matrix products, arithmetic and copies ran while one was open for 2% of the time, Pallas kernels for 5%

profile of v2, /device:TPU:1, one launch (start us, length us, event | category | flops | bytes accessed | tf_op | source)
XLA Modules:
  0.0 268.9 jit_solution(8832923818844587901)
XLA Ops:
  2.9 10.5 %all-to-all-start = ((bf16[32,32,512]{2,1,0:T(8,128)(2,1)}), bf16[32,32,512]{2,1,0:T(8,128)(2,1)S(1)}, u32[]{:S(2)}, u32[]{:S(2)}) async-start(bf16[32,32,512]{2,1,0:T(8,128)(2,1)} %bitcast.2), calls=%async_computation | async-start | bytes 2097152 | tf_op jit(solution)/shard_map/all_to_all | solution.py:257
  13.5 13.5 %collective-permute-start.4 = (bf16[2,1,32,512]{3,2,0,1:T(8,128)(2,1)S(1)}, bf16[2,1,32,512]{3,2,0,1:T(8,128)(2,1)S(1)}, u32[]{:S(2)}, u32[]{:S(2)}) collective-permute-start(bf16[2,1,32,512]{3,2,0,1:T(8,128)(2,1)S(1)} %bitcast.50), channel_id=1, source_target_pairs={{0,1},{1,0},{2,3},{3,2},{4,5},{5,4},{6,7},{7,6},{8,9},{9,8},{10,11... | collective-permute-start | bytes 196616 | tf_op jit(solution)/shard_map/ppermute | solution.py:206
  27.0 2.4 collective-permute-start
  30.0 1.2 broadcast_in_dim.34
  31.4 7.4 %all-to-all-start.1 = ((bf16[32,32,512]{2,1,0:T(8,128)(2,1)}), bf16[32,32,512]{2,1,0:T(8,128)(2,1)S(1)}, u32[]{:S(2)}, u32[]{:S(2)}) async-start(bf16[32,32,512]{2,1,0:T(8,128)(2,1)} %bitcast.10), calls=%async_computation.1 | async-start | bytes 2097152 | tf_op jit(solution)/shard_map/all_to_all | solution.py:257
  40.2 3.4 %shard_map.103 = (bf16[2048,256]{1,0:T(8,128)(2,1)}, bf16[2048,256]{1,0:T(8,128)(2,1)}) custom-call(f32[16,128]{1,0:T(8,128)} %taps_ref.1, f32[16,128]{1,0:T(8,128)} %pad_maximum_fusion.6.rev_ref, f32[16,1]{1,0:T(8,128)} %copy.12.decay_ref), custom_call_target="tpu_custom_call" | custom-call | flops 1000000000 | bytes 16448 | tf_op jit(solution)/shard_map/pallas_call | solution.py:22
  43.6 4.4 %shard_map.104 = (bf16[4,64,768]{2,1,0:T(8,128)(2,1)}, bf16[4,64,768]{2,1,0:T(8,128)(2,1)}) custom-call(s32[1]{0:T(128)} %bitcast.5.core_ref, bf16[2,512,512]{2,1,0:T(8,128)(2,1)} %bitcast.36, bf16[3,512,256]{2,1,0:T(8,128)(2,1)} %bitcast.58, bf16[3,512,256]{2,1,0:T(8,128)(2,1)} %collective-permute-done.peer_ref), custom_call_target="tpu_custom_call" | custom-call | flops 1000000000 | bytes 2621444 | tf_op jit(solution)/shard_map/pallas_call | solution.py:22
  48.0 3.9 %collective-permute-start.1 = (bf16[4,64,768]{2,1,0:T(8,128)(2,1)}, bf16[4,64,768]{2,1,0:T(8,128)(2,1)S(1)}, u32[]{:S(2)}, u32[]{:S(2)}) collective-permute-start(bf16[4,64,768]{2,1,0:T(8,128)(2,1)} %get-tuple-element.36), channel_id=1, source_target_pairs={{0,64},{64,0},{128,192},{192,128},{256,320},{320,256},{384,448},{4... | collective-permute-start | bytes 1179656 | tf_op jit(solution)/shard_map/ppermute | solution.py:206
  52.0 3.1 %all-to-all-done.1 = bf16[32,32,512]{2,1,0:T(8,128)(2,1)S(1)} async-done(((bf16[32,32,512]{2,1,0:T(8,128)(2,1)}), bf16[32,32,512]{2,1,0:T(8,128)(2,1)S(1)}, u32[]{:S(2)}, u32[]{:S(2)}) %all-to-all-start.1) | async-done | bytes 1048608 | tf_op jit(solution)/shard_map/all_to_all | solution.py:257
  56.0 4.5 %shard_map.105 = (bf16[4,64,768]{2,1,0:T(8,128)(2,1)}, bf16[4,64,768]{2,1,0:T(8,128)(2,1)}) custom-call(s32[1]{0:T(128)} %bitcast.5.core_ref, bf16[2,512,512]{2,1,0:T(8,128)(2,1)} %bitcast.38, bf16[3,512,256]{2,1,0:T(8,128)(2,1)} %bitcast.59, bf16[3,512,256]{2,1,0:T(8,128)(2,1)} %collective-permute-done.peer_ref), custom_call_target="tpu_custom_call" | custom-call | flops 1000000000 | bytes 2621444 | tf_op jit(solution)/shard_map/pallas_call | solution.py:22
  60.5 3.9 %collective-permute-start.5 = (bf16[4,64,768]{2,1,0:T(8,128)(2,1)}, bf16[4,64,768]{2,1,0:T(8,128)(2,1)S(1)}, u32[]{:S(2)}, u32[]{:S(2)}) collective-permute-start(bf16[4,64,768]{2,1,0:T(8,128)(2,1)} %get-tuple-element.38), channel_id=1, source_target_pairs={{0,64},{64,0},{128,192},{192,128},{256,320},{320,256},{384,448},{4... | collective-permute-start | bytes 1179656 | tf_op jit(solution)/shard_map/ppermute | solution.py:206
  64.5 3.0 %collective-permute-start.2 = (bf16[2,64,768]{2,1,0:T(8,128)(2,1)S(1)}, bf16[2,64,768]{2,1,0:T(8,128)(2,1)S(1)}, u32[]{:S(2)}, u32[]{:S(2)}) collective-permute-start(bf16[2,64,768]{2,1,0:T(8,128)(2,1)S(1)} %get-tuple-element.60), channel_id=1, source_target_pairs={{0,128},{64,192},{128,0},{192,64},{256,384},{320,448},{384,256},{4... | collective-permute-start | bytes 589832 | tf_op jit(solution)/shard_map/ppermute | solution.py:206
  67.6 9.4 %collective-permute-done.5 = bf16[4,64,768]{2,1,0:T(8,128)(2,1)S(1)} collective-permute-done((bf16[4,64,768]{2,1,0:T(8,128)(2,1)}, bf16[4,64,768]{2,1,0:T(8,128)(2,1)S(1)}, u32[]{:S(2)}, u32[]{:S(2)}) %collective-permute-start.5) | collective-permute-done | bytes 393248 | tf_op jit(solution)/shard_map/ppermute | solution.py:206
  78.1 2.4 collective-permute-start.6
  80.5 7.2 %collective-permute-start.3 = (bf16[1,64,768]{2,1,0:T(8,128)(2,1)S(1)}, bf16[1,64,768]{2,1,0:T(8,128)(2,1)S(1)}, u32[]{:S(2)}, u32[]{:S(2)}) collective-permute-start(bf16[1,64,768]{2,1,0:T(8,128)(2,1)S(1)} %add_convert_fusion.9), channel_id=1, source_target_pairs={{0,256},{64,320},{128,384},{192,448},{256,0},{320,64},{384,128},{4... | collective-permute-start | bytes 294920 | tf_op jit(solution)/shard_map/ppermute | solution.py:206
  87.7 7.3 %collective-permute-done.6 = bf16[2,64,768]{2,1,0:T(8,128)(2,1)S(1)} collective-permute-done((bf16[2,64,768]{2,1,0:T(8,128)(2,1)S(1)}, bf16[2,64,768]{2,1,0:T(8,128)(2,1)S(1)}, u32[]{:S(2)}, u32[]{:S(2)}) %collective-permute-start.6) | collective-permute-done | bytes 196640 | tf_op jit(solution)/shard_map/ppermute | solution.py:206
  95.0 6.2 %collective-permute-start.7 = (bf16[1,64,768]{2,1,0:T(8,128)(2,1)S(1)}, bf16[1,64,768]{2,1,0:T(8,128)(2,1)S(1)}, u32[]{:S(2)}, u32[]{:S(2)}) collective-permute-start(bf16[1,64,768]{2,1,0:T(8,128)(2,1)S(1)} %add_convert_fusion.6), channel_id=1, source_target_pairs={{0,256},{64,320},{128,384},{192,448},{256,0},{320,64},{384,128},{4... | collective-permute-start | bytes 294920 | tf_op jit(solution)/shard_map/ppermute | solution.py:206
  101.3 8.9 %collective-permute-done.7 = bf16[1,64,768]{2,1,0:T(8,128)(2,1)S(1)} collective-permute-done((bf16[1,64,768]{2,1,0:T(8,128)(2,1)S(1)}, bf16[1,64,768]{2,1,0:T(8,128)(2,1)S(1)}, u32[]{:S(2)}, u32[]{:S(2)}) %collective-permute-start.7) | collective-permute-done | bytes 98336 | tf_op jit(solution)/shard_map/ppermute | solution.py:206
  110.2 1.9 collective-permute-start.8
  113.9 2.0 shard_map.106
  115.9 3.8 %collective-permute-start.9 = (bf16[128,256]{1,0:T(8,128)(2,1)}, bf16[128,256]{1,0:T(8,128)(2,1)S(1)}, u32[]{:S(2)}, u32[]{:S(2)}) collective-permute-start(bf16[128,256]{1,0:T(8,128)(2,1)} %get-tuple-element.39.prod_ref), channel_id=1, source_target_pairs={{0,32},{32,64},{64,96},{96,128},{128,160},{160,192},{192,224},{224... | collective-permute-start | bytes 196616 | tf_op jit(solution)/shard_map/ppermute | solution.py:212
  119.7 1.9 collective-permute-start.10
  121.7 3.8 %collective-permute-done.10.next_ref = bf16[128,256]{1,0:T(8,128)(2,1)S(1)} collective-permute-done((bf16[128,256]{1,0:T(8,128)(2,1)}, bf16[128,256]{1,0:T(8,128)(2,1)S(1)}, u32[]{:S(2)}, u32[]{:S(2)}) %collective-permute-start.10) | collective-permute-done | bytes 65568 | tf_op jit(solution)/shard_map/ppermute | solution.py:212
  126.2 3.2 %shard_map.107 = (bf16[128,256]{1,0:T(8,128)(2,1)}, f32[128,768]{1,0:T(8,128)}, f32[8,768]{1,0:T(8,128)}) custom-call(bf16[2048,256]{1,0:T(8,128)(2,1)} %get-tuple-element.32.fwd_ref, bf16[2048,256]{1,0:T(8,128)(2,1)} %get-tuple-element.33.bwd_ref, bf16[128,256]{1,0:T(8,128)(2,1)} %get-tuple-element.39.prod_ref, bf16[128,256]{1,0:T(8,128)(2,1)} %copy-done.11, ...), custom_call_target="tpu_custom_call" | custom-call | flops 1000000000 | bytes 2819072 | tf_op jit(solution)/shard_map/pallas_call | solution.py:22
  129.4 1.9 collective-permute-start.11
  131.3 3.4 %collective-permute-done.11.head_ref = f32[8,768]{1,0:T(8,128)S(1)} collective-permute-done((f32[8,768]{1,0:T(8,128)}, f32[8,768]{1,0:T(8,128)S(1)}, u32[]{:S(2)}, u32[]{:S(2)}) %collective-permute-start.11) | collective-permute-done | bytes 24608 | tf_op jit(solution)/shard_map/ppermute | solution.py:212
  135.3 2.0 shard_map.108
  137.3 2.2 collective-permute-start.14
  139.5 12.1 %collective-permute-done.14 = bf16[1,64,768]{2,1,0:T(8,128)(2,1)S(1)} collective-permute-done((bf16[1,64,768]{2,1,0:T(8,128)(2,1)}, bf16[1,64,768]{2,1,0:T(8,128)(2,1)S(1)}, u32[]{:S(2)}, u32[]{:S(2)}) %collective-permute-start.14) | collective-permute-done | bytes 98336 | tf_op jit(solution)/shard_map/ppermute | solution.py:206
  152.6 1.9 collective-permute-start.15
  154.5 9.3 %collective-permute-done.15 = bf16[2,64,768]{2,1,0:T(8,128)(2,1)S(1)} collective-permute-done((bf16[2,64,768]{2,1,0:T(8,128)(2,1)S(1)}, bf16[2,64,768]{2,1,0:T(8,128)(2,1)S(1)}, u32[]{:S(2)}, u32[]{:S(2)}) %collective-permute-start.15) | collective-permute-done | bytes 196640 | tf_op jit(solution)/shard_map/ppermute | solution.py:206
  164.7 1.9 collective-permute-start.16
  166.6 10.2 %collective-permute-done.16 = bf16[4,64,768]{2,1,0:T(8,128)(2,1)S(1)} collective-permute-done((bf16[4,64,768]{2,1,0:T(8,128)(2,1)S(1)}, bf16[4,64,768]{2,1,0:T(8,128)(2,1)S(1)}, u32[]{:S(2)}, u32[]{:S(2)}) %collective-permute-start.16) | collective-permute-done | bytes 393248 | tf_op jit(solution)/shard_map/ppermute | solution.py:206
  176.8 1.9 pad_maximum_fusion.g_ref
  178.6 4.0 %shard_map.109 = (bf16[2,512,512]{2,1,0:T(8,128)(2,1)}, bf16[512,768]{1,0:T(8,128)(2,1)}) custom-call(s32[1]{0:T(128)} %bitcast.5.core_ref, bf16[8,64,768]{2,1,0:T(8,128)(2,1)} %pad_maximum_fusion.g_ref, bf16[3,512,256]{2,1,0:T(8,128)(2,1)} %bitcast.60, bf16[3,512,256]{2,1,0:T(8,128)(2,1)} %collective-permute-done.peer_ref), custom_call_target="tpu_custom_call" | custom-call | flops 1000000000 | bytes 2359300 | tf_op jit(solution)/shard_map/pallas_call | solution.py:22
  182.7 7.4 %all-to-all-start.2 = ((bf16[32,32,512]{2,1,0:T(8,128)(2,1)}), bf16[32,32,512]{2,1,0:T(8,128)(2,1)S(1)}, u32[]{:S(2)}, u32[]{:S(2)}) async-start(bf16[32,32,512]{2,1,0:T(8,128)(2,1)} %bitcast.41), calls=%async_computation.2 | async-start | bytes 2097152 | tf_op jit(solution)/shard_map/all_to_all | solution.py:257
  190.1 4.3 %collective-permute-start.12 = (bf16[1,64,768]{2,1,0:T(8,128)(2,1)S(1)}, bf16[1,64,768]{2,1,0:T(8,128)(2,1)S(1)}, u32[]{:S(2)}, u32[]{:S(2)}) collective-permute-start(bf16[1,64,768]{2,1,0:T(8,128)(2,1)S(1)} %bitcast.46), channel_id=1, source_target_pairs={{0,256},{64,320},{128,384},{192,448},{256,0},{320,64},{384,128},{4... | collective-permute-start | bytes 294920 | tf_op jit(solution)/shard_map/ppermute | solution.py:206
  194.5 12.2 %collective-permute-done.12 = bf16[1,64,768]{2,1,0:T(8,128)(2,1)S(1)} collective-permute-done((bf16[1,64,768]{2,1,0:T(8,128)(2,1)S(1)}, bf16[1,64,768]{2,1,0:T(8,128)(2,1)S(1)}, u32[]{:S(2)}, u32[]{:S(2)}) %collective-permute-start.12) | collective-permute-done | bytes 98336 | tf_op jit(solution)/shard_map/ppermute | solution.py:206
  206.7 1.9 collective-permute-start.13
  208.7 9.5 %collective-permute-done.13 = bf16[2,64,768]{2,1,0:T(8,128)(2,1)S(1)} collective-permute-done((bf16[2,64,768]{2,1,0:T(8,128)(2,1)S(1)}, bf16[2,64,768]{2,1,0:T(8,128)(2,1)S(1)}, u32[]{:S(2)}, u32[]{:S(2)}) %collective-permute-start.13) | collective-permute-done | bytes 196640 | tf_op jit(solution)/shard_map/ppermute | solution.py:206
  218.4 2.1 collective-permute-start.17
  220.5 10.0 %collective-permute-done.17 = bf16[4,64,768]{2,1,0:T(8,128)(2,1)S(1)} collective-permute-done((bf16[4,64,768]{2,1,0:T(8,128)(2,1)S(1)}, bf16[4,64,768]{2,1,0:T(8,128)(2,1)S(1)}, u32[]{:S(2)}, u32[]{:S(2)}) %collective-permute-start.17) | collective-permute-done | bytes 393248 | tf_op jit(solution)/shard_map/ppermute | solution.py:206
  231.4 4.0 %shard_map.110 = (bf16[2,512,512]{2,1,0:T(8,128)(2,1)}, bf16[512,768]{1,0:T(8,128)(2,1)}) custom-call(s32[1]{0:T(128)} %bitcast.5.core_ref, bf16[8,64,768]{2,1,0:T(8,128)(2,1)} %pad_maximum_fusion.1.g_ref, bf16[3,512,256]{2,1,0:T(8,128)(2,1)} %bitcast.61, bf16[3,512,256]{2,1,0:T(8,128)(2,1)} %collective-permute-done.peer_ref), custom_call_target="tpu_custom_call" | custom-call | flops 1000000000 | bytes 2359300 | tf_op jit(solution)/shard_map/pallas_call | solution.py:22
  235.5 4.7 %shard_map.111 = (f32[3,512,256]{2,1,0:T(8,128)}, bf16[3,512,256]{2,1,0:T(8,128)(2,1)}) custom-call(s32[1]{0:T(128)} %bitcast.5.core_ref, bf16[2,512,512]{2,1,0:T(8,128)(2,1)} %bitcast.37, bf16[2,512,512]{2,1,0:T(8,128)(2,1)} %bitcast.39, bf16[512,768]{1,0:T(8,128)(2,1)} %get-tuple-element.53.g0_ref, bf16[512,768]{1,0:T(8,128)(2,1)} %get-tuple-element.54.g1_ref), custom_call_target="tpu_custom_call" | custom-call | flops 1000000000 | bytes 3670020 | tf_op jit(solution)/shard_map/pallas_call | solution.py:22
  240.2 3.4 %collective-permute-start.19 = (bf16[3,512,256]{2,1,0:T(8,128)(2,1)}, bf16[3,512,256]{2,1,0:T(8,128)(2,1)S(1)}, u32[]{:S(2)}, u32[]{:S(2)}) collective-permute-start(bf16[3,512,256]{2,1,0:T(8,128)(2,1)} %get-tuple-element.56), channel_id=1, source_target_pairs={{0,32},{32,0},{1,33},{33,1},{2,34},{34,2},{3,35},{35,3},{4,36},{36... | collective-permute-start | bytes 2359304 | tf_op jit(solution)/shard_map/ppermute | solution.py:206
  243.6 7.1 %all-to-all-start.3 = ((bf16[32,32,512]{2,1,0:T(8,128)(2,1)}), bf16[32,32,512]{2,1,0:T(8,128)(2,1)S(1)}, u32[]{:S(2)}, u32[]{:S(2)}) async-start(bf16[32,32,512]{2,1,0:T(8,128)(2,1)} %bitcast.40), calls=%async_computation.3 | async-start | bytes 2097152 | tf_op jit(solution)/shard_map/all_to_all | solution.py:257
  250.7 11.6 %collective-permute-start.18 = (bf16[2,32,512]{2,1,0:T(8,128)(2,1)S(1)}, bf16[2,32,512]{2,1,0:T(8,128)(2,1)}, u32[]{:S(2)}, u32[]{:S(2)}) collective-permute-start(bf16[2,32,512]{2,1,0:T(8,128)(2,1)S(1)} %bitcast_reduce_fusion), channel_id=1, source_target_pairs={{0,1},{1,0},{2,3},{3,2},{4,5},{5,4},{6,7},{7,6},{8,9},{9,8},{10,11... | collective-permute-start | bytes 196616 | tf_op jit(solution)/shard_map/ppermute | solution.py:206
  263.4 3.6 %all-to-all-done.3 = bf16[32,32,512]{2,1,0:T(8,128)(2,1)S(1)} async-done(((bf16[32,32,512]{2,1,0:T(8,128)(2,1)}), bf16[32,32,512]{2,1,0:T(8,128)(2,1)S(1)}, u32[]{:S(2)}, u32[]{:S(2)}) %all-to-all-start.3) | async-done | bytes 1048608 | tf_op jit(solution)/shard_map/all_to_all | solution.py:257
  (70 shorter events, 15.8 us)
Async XLA Ops:
  0.6 1.0 copy-start
  1.8 25.2 %copy-start.10 = (bf16[512,3,256]{2,0,1:T(8,128)(2,1)S(1)}, bf16[512,3,256]{2,0,1:T(8,128)(2,1)}, u32[]{:S(2)}) copy-start(bf16[512,3,256]{2,0,1:T(8,128)(2,1)} %param.9) | copy-start | bytes 2359300
  2.9 27.1 %all-to-all-start = ((bf16[32,32,512]{2,1,0:T(8,128)(2,1)}), bf16[32,32,512]{2,1,0:T(8,128)(2,1)S(1)}, u32[]{:S(2)}, u32[]{:S(2)}) async-start(bf16[32,32,512]{2,1,0:T(8,128)(2,1)} %bitcast.2), calls=%async_computation | async-start | bytes 2097152 | tf_op jit(solution)/shard_map/all_to_all | solution.py:257
  13.5 16.0 %collective-permute-start.4 = (bf16[2,1,32,512]{3,2,0,1:T(8,128)(2,1)S(1)}, bf16[2,1,32,512]{3,2,0,1:T(8,128)(2,1)S(1)}, u32[]{:S(2)}, u32[]{:S(2)}) collective-permute-start(bf16[2,1,32,512]{3,2,0,1:T(8,128)(2,1)S(1)} %bitcast.50), channel_id=1, source_target_pairs={{0,1},{1,0},{2,3},{3,2},{4,5},{5,4},{6,7},{7,6},{8,9},{9,8},{10,11... | collective-permute-start | bytes 196616 | tf_op jit(solution)/shard_map/ppermute | solution.py:206
  27.0 16.6 %collective-permute-start = (bf16[3,512,256]{2,1,0:T(8,128)(2,1)S(1)}, bf16[3,512,256]{2,1,0:T(8,128)(2,1)}, u32[]{:S(2)}, u32[]{:S(2)}) collective-permute-start(bf16[3,512,256]{2,1,0:T(8,128)(2,1)S(1)} %bitcast.62), channel_id=1, source_target_pairs={{0,32},{32,0},{1,33},{33,1},{2,34},{34,2},{3,35},{35,3},{4,36},{36... | collective-permute-start | bytes 2359304 | tf_op jit(solution)/shard_map/ppermute | solution.py:206
  30.0 1.4 copy-start.2
  30.0 8.7 %copy-start.8 = (f32[16,128]{1,0:T(8,128)S(1)}, f32[16,128]{1,0:T(8,128)}, u32[]{:S(2)}) copy-start(f32[16,128]{1,0:T(8,128)} %taps_ref.1) | copy-start | bytes 24580
  30.0 8.9 %copy-start.9 = (f32[16]{0:T(128)S(1)}, f32[16]{0:T(128)}, u32[]{:S(2)}) copy-start(f32[16]{0:T(128)} %param.12) | copy-start | bytes 196
  31.4 23.7 %all-to-all-start.1 = ((bf16[32,32,512]{2,1,0:T(8,128)(2,1)}), bf16[32,32,512]{2,1,0:T(8,128)(2,1)S(1)}, u32[]{:S(2)}, u32[]{:S(2)}) async-start(bf16[32,32,512]{2,1,0:T(8,128)(2,1)} %bitcast.10), calls=%async_computation.1 | async-start | bytes 2097152 | tf_op jit(solution)/shard_map/all_to_all | solution.py:257
  48.0 16.4 %collective-permute-start.1 = (bf16[4,64,768]{2,1,0:T(8,128)(2,1)}, bf16[4,64,768]{2,1,0:T(8,128)(2,1)S(1)}, u32[]{:S(2)}, u32[]{:S(2)}) collective-permute-start(bf16[4,64,768]{2,1,0:T(8,128)(2,1)} %get-tuple-element.36), channel_id=1, source_target_pairs={{0,64},{64,0},{128,192},{192,128},{256,320},{320,256},{384,448},{4... | collective-permute-start | bytes 1179656 | tf_op jit(solution)/shard_map/ppermute | solution.py:206
  55.0 1.0 copy-start.3
  56.0 8.4 %copy-start.5 = (bf16[4,64,768]{2,1,0:T(8,128)(2,1)S(1)}, bf16[4,64,768]{2,1,0:T(8,128)(2,1)}, u32[]{:S(2)}) copy-start(bf16[4,64,768]{2,1,0:T(8,128)(2,1)} %get-tuple-element.35) | copy-start | bytes 1179652
  60.5 16.5 %collective-permute-start.5 = (bf16[4,64,768]{2,1,0:T(8,128)(2,1)}, bf16[4,64,768]{2,1,0:T(8,128)(2,1)S(1)}, u32[]{:S(2)}, u32[]{:S(2)}) collective-permute-start(bf16[4,64,768]{2,1,0:T(8,128)(2,1)} %get-tuple-element.38), channel_id=1, source_target_pairs={{0,64},{64,0},{128,192},{192,128},{256,320},{320,256},{384,448},{4... | collective-permute-start | bytes 1179656 | tf_op jit(solution)/shard_map/ppermute | solution.py:206
  64.5 15.9 %collective-permute-start.2 = (bf16[2,64,768]{2,1,0:T(8,128)(2,1)S(1)}, bf16[2,64,768]{2,1,0:T(8,128)(2,1)S(1)}, u32[]{:S(2)}, u32[]{:S(2)}) collective-permute-start(bf16[2,64,768]{2,1,0:T(8,128)(2,1)S(1)} %get-tuple-element.60), channel_id=1, source_target_pairs={{0,128},{64,192},{128,0},{192,64},{256,384},{320,448},{384,256},{4... | collective-permute-start | bytes 589832 | tf_op jit(solution)/shard_map/ppermute | solution.py:206
  78.1 16.9 %collective-permute-start.6 = (bf16[2,64,768]{2,1,0:T(8,128)(2,1)S(1)}, bf16[2,64,768]{2,1,0:T(8,128)(2,1)S(1)}, u32[]{:S(2)}, u32[]{:S(2)}) collective-permute-start(bf16[2,64,768]{2,1,0:T(8,128)(2,1)S(1)} %get-tuple-element.58), channel_id=1, source_target_pairs={{0,128},{64,192},{128,0},{192,64},{256,384},{320,448},{384,256},{4... | collective-permute-start | bytes 589832 | tf_op jit(solution)/shard_map/ppermute | solution.py:206
  80.5 20.7 %collective-permute-start.3 = (bf16[1,64,768]{2,1,0:T(8,128)(2,1)S(1)}, bf16[1,64,768]{2,1,0:T(8,128)(2,1)S(1)}, u32[]{:S(2)}, u32[]{:S(2)}) collective-permute-start(bf16[1,64,768]{2,1,0:T(8,128)(2,1)S(1)} %add_convert_fusion.9), channel_id=1, source_target_pairs={{0,256},{64,320},{128,384},{192,448},{256,0},{320,64},{384,128},{4... | collective-permute-start | bytes 294920 | tf_op jit(solution)/shard_map/ppermute | solution.py:206
  95.0 15.1 %collective-permute-start.7 = (bf16[1,64,768]{2,1,0:T(8,128)(2,1)S(1)}, bf16[1,64,768]{2,1,0:T(8,128)(2,1)S(1)}, u32[]{:S(2)}, u32[]{:S(2)}) collective-permute-start(bf16[1,64,768]{2,1,0:T(8,128)(2,1)S(1)} %add_convert_fusion.6), channel_id=1, source_target_pairs={{0,256},{64,320},{128,384},{192,448},{256,0},{320,64},{384,128},{4... | collective-permute-start | bytes 294920 | tf_op jit(solution)/shard_map/ppermute | solution.py:206
  101.3 12.1 %copy-start.6 = (bf16[1,64,768]{2,1,0:T(8,128)(2,1)}, bf16[1,64,768]{2,1,0:T(8,128)(2,1)S(1)}, u32[]{:S(2)}) copy-start(bf16[1,64,768]{2,1,0:T(8,128)(2,1)S(1)} %add_convert_fusion.8) | copy-start | bytes 294916
  110.2 3.1 %copy-start.7 = (bf16[1,64,768]{2,1,0:T(8,128)(2,1)}, bf16[1,64,768]{2,1,0:T(8,128)(2,1)S(1)}, u32[]{:S(2)}) copy-start(bf16[1,64,768]{2,1,0:T(8,128)(2,1)S(1)} %add_convert_fusion.5) | copy-start | bytes 294916
  110.2 3.1 %collective-permute-start.8 = (bf16[8,768]{1,0:T(8,128)(2,1)S(1)}, bf16[8,768]{1,0:T(8,128)(2,1)S(1)}, u32[]{:S(2)}, u32[]{:S(2)}) collective-permute-start(bf16[8,768]{1,0:T(8,128)(2,1)S(1)} %fusion.3), channel_id=1, source_target_pairs={{0,32},{32,64},{64,96},{96,128},{128,160},{160,192},{192,224},{224... | collective-permute-start | bytes 36872 | tf_op jit(solution)/shard_map/ppermute | solution.py:212
  113.3 0.6 copy-start.14
  115.9 5.8 %collective-permute-start.9 = (bf16[128,256]{1,0:T(8,128)(2,1)}, bf16[128,256]{1,0:T(8,128)(2,1)S(1)}, u32[]{:S(2)}, u32[]{:S(2)}) collective-permute-start(bf16[128,256]{1,0:T(8,128)(2,1)} %get-tuple-element.39.prod_ref), channel_id=1, source_target_pairs={{0,32},{32,64},{64,96},{96,128},{128,160},{160,192},{192,224},{224... | collective-permute-start | bytes 196616 | tf_op jit(solution)/shard_map/ppermute | solution.py:212
  119.7 5.8 %collective-permute-start.10 = (bf16[128,256]{1,0:T(8,128)(2,1)}, bf16[128,256]{1,0:T(8,128)(2,1)S(1)}, u32[]{:S(2)}, u32[]{:S(2)}) collective-permute-start(bf16[128,256]{1,0:T(8,128)(2,1)} %get-tuple-element.40.cg_ref), channel_id=1, source_target_pairs={{32,0},{64,32},{96,64},{128,96},{160,128},{192,160},{224,192},{256... | collective-permute-start | bytes 196616 | tf_op jit(solution)/shard_map/ppermute | solution.py:212
  121.7 3.9 %copy-start.11 = (bf16[128,256]{1,0:T(8,128)(2,1)}, bf16[128,256]{1,0:T(8,128)(2,1)S(1)}, u32[]{:S(2)}) copy-start(bf16[128,256]{1,0:T(8,128)(2,1)S(1)} %collective-permute-done.9.prev_ref) | copy-start | bytes 196612
  125.5 0.6 copy-start.12
  129.4 5.3 %collective-permute-start.11 = (f32[8,768]{1,0:T(8,128)}, f32[8,768]{1,0:T(8,128)S(1)}, u32[]{:S(2)}, u32[]{:S(2)}) collective-permute-start(f32[8,768]{1,0:T(8,128)} %get-tuple-element.46), channel_id=1, source_target_pairs={{32,0},{64,32},{96,64},{128,96},{160,128},{192,160},{224,192},{256... | collective-permute-start | bytes 73736 | tf_op jit(solution)/shard_map/ppermute | solution.py:212
  134.7 0.6 copy-start.13
  137.3 14.4 %collective-permute-start.14 = (bf16[1,64,768]{2,1,0:T(8,128)(2,1)}, bf16[1,64,768]{2,1,0:T(8,128)(2,1)S(1)}, u32[]{:S(2)}, u32[]{:S(2)}) collective-permute-start(bf16[1,64,768]{2,1,0:T(8,128)(2,1)} %bitcast.42), channel_id=1, source_target_pairs={{0,256},{64,320},{128,384},{192,448},{256,0},{320,64},{384,128},{4... | collective-permute-start | bytes 294920 | tf_op jit(solution)/shard_map/ppermute | solution.py:206
  152.6 11.2 %collective-permute-start.15 = (bf16[2,64,768]{2,1,0:T(8,128)(2,1)S(1)}, bf16[2,64,768]{2,1,0:T(8,128)(2,1)S(1)}, u32[]{:S(2)}, u32[]{:S(2)}) collective-permute-start(bf16[2,64,768]{2,1,0:T(8,128)(2,1)S(1)} %pad_maximum_fusion.5), channel_id=1, source_target_pairs={{0,128},{64,192},{128,0},{192,64},{256,384},{320,448},{384,256},{4... | collective-permute-start | bytes 589832 | tf_op jit(solution)/shard_map/ppermute | solution.py:206
  164.7 12.1 %collective-permute-start.16 = (bf16[4,64,768]{2,1,0:T(8,128)(2,1)S(1)}, bf16[4,64,768]{2,1,0:T(8,128)(2,1)S(1)}, u32[]{:S(2)}, u32[]{:S(2)}) collective-permute-start(bf16[4,64,768]{2,1,0:T(8,128)(2,1)S(1)} %pad_maximum_fusion.3), channel_id=1, source_target_pairs={{0,64},{64,0},{128,192},{192,128},{256,320},{320,256},{384,448},{4... | collective-permute-start | bytes 1179656 | tf_op jit(solution)/shard_map/ppermute | solution.py:206
  182.7 7.4 %copy-start.4 = (bf16[64,768]{1,0:T(8,128)(2,1)S(1)}, bf16[64,768]{1,0:T(8,128)(2,1)}, u32[]{:S(2)}) copy-start(bf16[64,768]{1,0:T(8,128)(2,1)} %get-tuple-element.47) | copy-start | bytes 294916
  182.7 35.6 %all-to-all-start.2 = ((bf16[32,32,512]{2,1,0:T(8,128)(2,1)}), bf16[32,32,512]{2,1,0:T(8,128)(2,1)S(1)}, u32[]{:S(2)}, u32[]{:S(2)}) async-start(bf16[32,32,512]{2,1,0:T(8,128)(2,1)} %bitcast.41), calls=%async_computation.2 | async-start | bytes 2097152 | tf_op jit(solution)/shard_map/all_to_all | solution.py:257
  190.1 16.6 %collective-permute-start.12 = (bf16[1,64,768]{2,1,0:T(8,128)(2,1)S(1)}, bf16[1,64,768]{2,1,0:T(8,128)(2,1)S(1)}, u32[]{:S(2)}, u32[]{:S(2)}) collective-permute-start(bf16[1,64,768]{2,1,0:T(8,128)(2,1)S(1)} %bitcast.46), channel_id=1, source_target_pairs={{0,256},{64,320},{128,384},{192,448},{256,0},{320,64},{384,128},{4... | collective-permute-start | bytes 294920 | tf_op jit(solution)/shard_map/ppermute | solution.py:206
  206.7 11.4 %collective-permute-start.13 = (bf16[2,64,768]{2,1,0:T(8,128)(2,1)S(1)}, bf16[2,64,768]{2,1,0:T(8,128)(2,1)S(1)}, u32[]{:S(2)}, u32[]{:S(2)}) collective-permute-start(bf16[2,64,768]{2,1,0:T(8,128)(2,1)S(1)} %pad_maximum_fusion.4), channel_id=1, source_target_pairs={{0,128},{64,192},{128,0},{192,64},{256,384},{320,448},{384,256},{4... | collective-permute-start | bytes 589832 | tf_op jit(solution)/shard_map/ppermute | solution.py:206
  218.4 12.1 %collective-permute-start.17 = (bf16[4,64,768]{2,1,0:T(8,128)(2,1)S(1)}, bf16[4,64,768]{2,1,0:T(8,128)(2,1)S(1)}, u32[]{:S(2)}, u32[]{:S(2)}) collective-permute-start(bf16[4,64,768]{2,1,0:T(8,128)(2,1)S(1)} %pad_maximum_fusion.2), channel_id=1, source_target_pairs={{0,64},{64,0},{128,192},{192,128},{256,320},{320,256},{384,448},{4... | collective-permute-start | bytes 1179656 | tf_op jit(solution)/shard_map/ppermute | solution.py:206
  240.2 22.1 %copy-start.1 = (f32[3,512,256]{2,1,0:T(8,128)S(1)}, f32[3,512,256]{2,1,0:T(8,128)}, u32[]{:S(2)}) copy-start(f32[3,512,256]{2,1,0:T(8,128)} %get-tuple-element.55) | copy-start | bytes 4718596
  240.2 22.1 %collective-permute-start.19 = (bf16[3,512,256]{2,1,0:T(8,128)(2,1)}, bf16[3,512,256]{2,1,0:T(8,128)(2,1)S(1)}, u32[]{:S(2)}, u32[]{:S(2)}) collective-permute-start(bf16[3,512,256]{2,1,0:T(8,128)(2,1)} %get-tuple-element.56), channel_id=1, source_target_pairs={{0,32},{32,0},{1,33},{33,1},{2,34},{34,2},{3,35},{35,3},{4,36},{36... | collective-permute-start | bytes 2359304 | tf_op jit(solution)/shard_map/ppermute | solution.py:206
  243.6 23.5 %all-to-all-start.3 = ((bf16[32,32,512]{2,1,0:T(8,128)(2,1)}), bf16[32,32,512]{2,1,0:T(8,128)(2,1)S(1)}, u32[]{:S(2)}, u32[]{:S(2)}) async-start(bf16[32,32,512]{2,1,0:T(8,128)(2,1)} %bitcast.40), calls=%async_computation.3 | async-start | bytes 2097152 | tf_op jit(solution)/shard_map/all_to_all | solution.py:257
  250.7 16.4 %collective-permute-start.18 = (bf16[2,32,512]{2,1,0:T(8,128)(2,1)S(1)}, bf16[2,32,512]{2,1,0:T(8,128)(2,1)}, u32[]{:S(2)}, u32[]{:S(2)}) collective-permute-start(bf16[2,32,512]{2,1,0:T(8,128)(2,1)S(1)} %bitcast_reduce_fusion), channel_id=1, source_target_pairs={{0,1},{1,0},{2,3},{3,2},{4,5},{5,4},{6,7},{7,6},{8,9},{9,8},{10,11... | collective-permute-start | bytes 196616 | tf_op jit(solution)/shard_map/ppermute | solution.py:206

commit v3 on v2

--- a/solution.py
+++ b/solution.py
@@ -73,7 +73,10 @@
     return jnp.where(c == relative * (count // 2) + piece * tokens + token, 1.0, 0.0).astype(BF16)
 
 
-def toeplitz_body(taps_ref, rev_ref, decay_ref, fwd_ref, bwd_ref):
+def prepare_body(pieces, members, taps_ref, rev_ref, decay_ref, fwd_ref, bwd_ref, turn_ref, unturn_ref):
+    tokens = turn_ref.shape[0] // (pieces * members)
+    turn_ref[...] = row_order(pieces, members, tokens, False)
+    unturn_ref[...] = row_order(pieces, members, tokens, True)
     filters, taps = taps_ref.shape
     lag = lax.broadcasted_iota(jnp.int32, (1, taps), 1)
     back = jnp.where(lag == 0, 0, taps - lag)
@@ -90,10 +93,10 @@
             ref[rows, taps:] = jnp.where(near, 0.0, ring).astype(BF16)
 
 
-def project_body(pieces, members, core_ref, x_ref, own_ref, peer_ref, keep_ref, send_ref):
+def project_body(members, core_ref, order_ref, x_ref, own_ref, peer_ref, keep_ref, send_ref):
     core = core_ref[0]
     rows = x_ref.shape[1]
-    order = row_order(pieces, members, rows // (pieces * members), False)
+    order = order_ref[...]
     mine = dot(order, x_ref[core]).astype(BF16)
     theirs = dot(order, x_ref[1 - core]).astype(BF16)
     streams, _, channels = own_ref.shape
@@ -105,12 +108,12 @@
         send_ref[:, :, cols] = part[half:].reshape(members // 2, rows // members, channels)
 
 
-def back_body(pieces, members, core_ref, g_ref, own_ref, peer_ref, out_ref, turned_ref):
+def back_body(core_ref, order_ref, *refs):
+    *g_refs, own_ref, peer_ref, out_ref, turned_ref = refs
     core = core_ref[0]
-    rows = g_ref.shape[0] * g_ref.shape[1]
-    order = row_order(pieces, members, rows // (pieces * members), True)
     streams, _, channels = own_ref.shape
-    g = dot(order, g_ref[...].reshape(rows, streams * channels)).astype(BF16)
+    gathered = jnp.concatenate([ref[...].reshape(-1, streams * channels) for ref in g_refs], axis=0)
+    g = dot(order_ref[...], gathered).astype(BF16)
     turned_ref[...] = g
     for place, ref in ((core, own_ref), (1 - core, peer_ref)):
         total = dot_nt(g[:, :channels], ref[0])
@@ -224,18 +227,17 @@
         count, by = half, by * 2
 
 
-def line_gather(x, tie=None):
-    x = x[None]
+def line_gather(x):
+    parts = [x[None]]
     by = lax.axis_size("zl") // 2
     while by:
-        if by == 1 and tie is not None:
-            x, tie = lax.optimization_barrier((x, tie))
-        x = jnp.concatenate([x, swap(x, "zl", by)], axis=0)
+        so_far = jnp.concatenate(parts, axis=0) if len(parts) > 1 else parts[0]
+        parts.append(swap(so_far, "zl", by))
         by //= 2
-    return x if tie is None else (x, tie)
-
-
-def shards(inputs, featurizer, short_filter, long_filter, decay_rate, skip_gain, output_grad):
+    return parts
+
+
+def layer(inputs, featurizer, short_filter, long_filter, decay_rate, skip_gain, output_grad):
     tokens, blocks, rows = inputs.shape
     members = lax.axis_size("zl")
     pieces = lax.axis_size("x") * lax.axis_size("y")
@@ -261,19 +263,25 @@
         return exchange(jnp.broadcast_to(x, (2, pieces, lines, rows))).reshape(2, pieces * lines, rows)
 
     x_near = spread(local)
-    far = swap(local, "zh")
+    far = swap(local, "zh", 1)
     w_own = featurizer.transpose(1, 0, 2)
     w_peer = swap(w_own, "core")
     rolled = jnp.roll(long_filter[:, ::-1], 1, axis=1)
     matrix = shape((long_filter.shape[0] * count, 2 * count), BF16)
-    t_fwd, t_bwd = call(toeplitz_body, (matrix, matrix), long_filter, rolled, decay_rate[:, None])
-    x_near, t_fwd, t_bwd = lax.optimization_barrier((x_near, t_fwd, t_bwd))
-
-    project = functools.partial(project_body, pieces, members)
+    square = shape((pieces * lines, pieces * lines), BF16)
+    t_fwd, t_bwd, turn, unturn = call(
+        functools.partial(prepare_body, pieces, members),
+        (matrix, matrix, square, square),
+        long_filter, rolled, decay_rate[:, None],
+    )
+
+    project = functools.partial(project_body, members)
     part_shape = (shape((members // 2, pieces * tokens, wide), BF16),) * 2
-    f_near = line_scatter(*call(project, part_shape, here, x_near, w_own, w_peer))
+    parts = call(project, part_shape, here, turn, x_near, w_own, w_peer)
+    f_near = line_scatter(*parts)
     x_far = spread(far)
-    f_far = line_scatter(*call(project, part_shape, here, x_far, w_own, w_peer))
+    parts = call(project, part_shape, here, turn, x_far, w_own, w_peer)
+    f_far = line_scatter(*parts)
 
     last = jnp.where(zh == 1, f_near[-8:], f_far[-8:])
     halo = shifted(last, 1)
@@ -292,17 +300,15 @@
     head = shifted(head, -1)
     piece_shape = shape((count // 2, wide), BF16)
     g_near, g_far = call(functools.partial(grad_body, tokens), (piece_shape, piece_shape), fg, head, short_filter, half)
-    back = functools.partial(back_body, pieces, members)
     back_shapes = (shape((2, pieces * lines, rows), BF16), shape((pieces * lines, wide), BF16))
 
     def collect(x):
-        return jnp.sum(exchange(x).astype(F32), axis=1)
-
-    d_far, turned_far = call(back, back_shapes, here, line_gather(g_far), w_own, w_peer)
-    s_far = collect(d_far).astype(BF16)
-    all_near, s_far = line_gather(g_near, s_far)
-    sent = swap(s_far, "zh")
-    d_near, turned_near = call(back, back_shapes, here, all_near, w_own, w_peer)
+        x = exchange(x)
+        return jnp.sum(x.astype(F32), axis=1)
+
+    d_far, turned_far = call(back_body, back_shapes, here, unturn, *line_gather(g_far), w_own, w_peer)
+    sent = swap(collect(d_far).astype(BF16), "zh", 1)
+    d_near, turned_near = call(back_body, back_shapes, here, unturn, *line_gather(g_near), w_own, w_peer)
     weight_shape = (3, rows, channels)
     w_grad, w_far = call(weight_body, (shape(weight_shape, F32), shape(weight_shape, BF16)), here, x_near, x_far, turned_near, turned_far)
     weight_grad = (w_grad + swap(w_far, "core").astype(F32)).astype(BF16).transpose(1, 0, 2)
@@ -318,4 +324,4 @@
     f, t = ("zl", "core"), ("x", "y", "zh")
     in_specs = (P(t, None, f), P(f, None, t), P(None, None, t), P(t, None), P(t), P(t), P(None, f, t))
     out_specs = (P(None, f, t), P(t, None, f), P(f, None, t))
-    return jax.shard_map(shards, mesh=fine, in_specs=in_specs, out_specs=out_specs, check_vma=False)
+    return jax.shard_map(layer, mesh=fine, in_specs=in_specs, out_specs=out_specs, check_vma=False)

time: 270 us -> 254 us (0.941); the launches traced: 269 us -> 250 us
  waiting for transfers between devices: 105 us -> 74.4 us
  starting transfers between devices: 114 us -> 124 us
    ppermute x16, waiting for transfers between devices: 88.9 us -> 60.7 us  [swap(): lax.ppermute(x, axis, [(i, i ^ by) for i in range(lax.axis_size(axis))])]
    ppermute x16, starting transfers between devices: 71.8 us -> 80.4 us  [swap(): lax.ppermute(x, axis, [(i, i ^ by) for i in range(lax.axis_size(axis))])]
  transfers between devices with their start and end apart: 24 -> 24, of which waited for: 15 -> 14; matrix products, arithmetic and copies ran while one was open for 2% -> 3% of each run, Pallas kernels for 5% -> 10%
where the time goes in v3:
time: 254 us; the launch traced here: 250 us
  starting transfers between devices  124 us (49%)
  waiting for transfers between devices  74.4 us (29%)
  Pallas kernels  33.4 us (13%)
  other arithmetic  8.47 us (3%)
  local copies, waits for them, and re-layouts  7.78 us (3%)
    ppermute x16, starting transfers between devices, swap(): lax.ppermute(x, axis, [(i, i ^ by) for i in range(lax.axis_size(axis))])  80.4 us
    ppermute x16, waiting for transfers between devices, swap(): lax.ppermute(x, axis, [(i, i ^ by) for i in range(lax.axis_size(axis))])  60.7 us
    all_to_all x4, starting transfers between devices, exchange(): lax.all_to_all(x.reshape(2 * pieces, lines, rows), ('core', 'x', 'y'), 0,...  33.6 us
    pallas_call x9, Pallas kernels, call(): pl.pallas_call(body, out_shape=outs, in_specs=[scalar if a.shape == (1,)...  33.4 us
    ppermute x4, starting transfers between devices, shifted(): lax.ppermute(x, axis, [(i, i + by) for i in range(count) if 0 <= i + by <...  9.6 us
    ppermute x4, waiting for transfers between devices, shifted(): lax.ppermute(x, axis, [(i, i + by) for i in range(count) if 0 <= i + by <...  8.42 us
    all_to_all x4, waiting for transfers between devices, exchange(): lax.all_to_all(x.reshape(2 * pieces, lines, rows), ('core', 'x', 'y'), 0,...  5.31 us
  transfers between devices with their start and end apart: 24, of which 14 were waited for; matrix products, arithmetic and copies ran while one was open for 3% of the time, Pallas kernels for 10%

profile of v3, /device:TPU:1, one launch (start us, length us, event | category | flops | bytes accessed | tf_op | source)
XLA Modules:
  0.0 249.9 jit_solution(266842783062388790)
XLA Ops:
  1.8 1.1 broadcast_in_dim.32
  2.9 10.5 %all-to-all-start = ((bf16[32,32,512]{2,1,0:T(8,128)(2,1)}), bf16[32,32,512]{2,1,0:T(8,128)(2,1)S(1)}, u32[]{:S(2)}, u32[]{:S(2)}) async-start(bf16[32,32,512]{2,1,0:T(8,128)(2,1)} %bitcast.4), calls=%async_computation | async-start | bytes 2097152 | tf_op jit(solution)/shard_map/all_to_all | solution.py:259
  13.5 13.5 %collective-permute-start.4 = (bf16[2,1,32,512]{3,2,0,1:T(8,128)(2,1)S(1)}, bf16[2,1,32,512]{3,2,0,1:T(8,128)(2,1)S(1)}, u32[]{:S(2)}, u32[]{:S(2)}) collective-permute-start(bf16[2,1,32,512]{3,2,0,1:T(8,128)(2,1)S(1)} %bitcast.50), channel_id=1, source_target_pairs={{0,1},{1,0},{2,3},{3,2},{4,5},{5,4},{6,7},{7,6},{8,9},{9,8},{10,11... | collective-permute-start | bytes 196616 | tf_op jit(solution)/shard_map/ppermute | solution.py:209
  27.0 2.4 collective-permute-start
  30.0 1.2 broadcast_in_dim.34
  31.3 7.4 %all-to-all-start.1 = ((bf16[32,32,512]{2,1,0:T(8,128)(2,1)}), bf16[32,32,512]{2,1,0:T(8,128)(2,1)S(1)}, u32[]{:S(2)}, u32[]{:S(2)}) async-start(bf16[32,32,512]{2,1,0:T(8,128)(2,1)} %bitcast.10), calls=%async_computation.1 | async-start | bytes 2097152 | tf_op jit(solution)/shard_map/all_to_all | solution.py:259
  40.2 3.7 %shard_map.103 = (bf16[2048,256]{1,0:T(8,128)(2,1)}, bf16[2048,256]{1,0:T(8,128)(2,1)}, bf16[512,512]{1,0:T(8,128)(2,1)}, bf16[512,512]{1,0:T(8,128)(2,1)}) custom-call(f32[16,128]{1,0:T(8,128)} %taps_ref.1, f32[16,128]{1,0:T(8,128)} %pad_maximum_fusion.4.rev_ref, f32[16,1]{1,0:T(8,128)} %copy.12.decay_ref), custom_call_target="tpu_custom_call" | custom-call | flops 1000000000 | bytes 16448 | tf_op jit(solution)/shard_map/pallas_call | solution.py:22
  43.9 4.6 %shard_map.104 = (bf16[4,64,768]{2,1,0:T(8,128)(2,1)}, bf16[4,64,768]{2,1,0:T(8,128)(2,1)}) custom-call(s32[1]{0:T(128)} %bitcast.1.core_ref, bf16[512,512]{1,0:T(8,128)(2,1)} %get-tuple-element.29.order_ref, bf16[2,512,512]{2,1,0:T(8,128)(2,1)} %bitcast.36, bf16[3,512,256]{2,1,0:T(8,128)(2,1)} %bitcast.6.own_ref.refs_4_, ...), custom_call_target="tpu_custom_call" | custom-call | flops 1000000000 | bytes 3145732 | tf_op jit(solution)/shard_map/pallas_call | solution.py:22
  48.5 3.9 %collective-permute-start.1 = (bf16[4,64,768]{2,1,0:T(8,128)(2,1)}, bf16[4,64,768]{2,1,0:T(8,128)(2,1)S(1)}, u32[]{:S(2)}, u32[]{:S(2)}) collective-permute-start(bf16[4,64,768]{2,1,0:T(8,128)(2,1)} %get-tuple-element.31), channel_id=1, source_target_pairs={{0,64},{64,0},{128,192},{192,128},{256,320},{320,256},{384,448},{4... | collective-permute-start | bytes 1179656 | tf_op jit(solution)/shard_map/ppermute | solution.py:209
  52.4 2.5 %all-to-all-done.1 = bf16[32,32,512]{2,1,0:T(8,128)(2,1)S(1)} async-done(((bf16[32,32,512]{2,1,0:T(8,128)(2,1)}), bf16[32,32,512]{2,1,0:T(8,128)(2,1)S(1)}, u32[]{:S(2)}, u32[]{:S(2)}) %all-to-all-start.1) | async-done | bytes 1048608 | tf_op jit(solution)/shard_map/all_to_all | solution.py:259
  56.0 4.6 %shard_map.105 = (bf16[4,64,768]{2,1,0:T(8,128)(2,1)}, bf16[4,64,768]{2,1,0:T(8,128)(2,1)}) custom-call(s32[1]{0:T(128)} %bitcast.1.core_ref, bf16[512,512]{1,0:T(8,128)(2,1)} %get-tuple-element.29.order_ref, bf16[2,512,512]{2,1,0:T(8,128)(2,1)} %bitcast.38, bf16[3,512,256]{2,1,0:T(8,128)(2,1)} %bitcast.6.own_ref.refs_4_, ...), custom_call_target="tpu_custom_call" | custom-call | flops 1000000000 | bytes 3145732 | tf_op jit(solution)/shard_map/pallas_call | solution.py:22
  60.6 3.9 %collective-permute-start.5 = (bf16[4,64,768]{2,1,0:T(8,128)(2,1)}, bf16[4,64,768]{2,1,0:T(8,128)(2,1)S(1)}, u32[]{:S(2)}, u32[]{:S(2)}) collective-permute-start(bf16[4,64,768]{2,1,0:T(8,128)(2,1)} %get-tuple-element.33), channel_id=1, source_target_pairs={{0,64},{64,0},{128,192},{192,128},{256,320},{320,256},{384,448},{4... | collective-permute-start | bytes 1179656 | tf_op jit(solution)/shard_map/ppermute | solution.py:209
  64.6 2.5 collective-permute-start.2
  67.1 9.9 %collective-permute-done.5 = bf16[4,64,768]{2,1,0:T(8,128)(2,1)S(1)} collective-permute-done((bf16[4,64,768]{2,1,0:T(8,128)(2,1)}, bf16[4,64,768]{2,1,0:T(8,128)(2,1)S(1)}, u32[]{:S(2)}, u32[]{:S(2)}) %collective-permute-start.5) | collective-permute-done | bytes 393248 | tf_op jit(solution)/shard_map/ppermute | solution.py:209
  78.2 1.9 collective-permute-start.6
  80.1 7.6 %collective-permute-start.3 = (bf16[1,64,768]{2,1,0:T(8,128)(2,1)S(1)}, bf16[1,64,768]{2,1,0:T(8,128)(2,1)S(1)}, u32[]{:S(2)}, u32[]{:S(2)}) collective-permute-start(bf16[1,64,768]{2,1,0:T(8,128)(2,1)S(1)} %add_convert_fusion.9), channel_id=1, source_target_pairs={{0,256},{64,320},{128,384},{192,448},{256,0},{320,64},{384,128},{4... | collective-permute-start | bytes 294920 | tf_op jit(solution)/shard_map/ppermute | solution.py:209
  87.8 6.6 %collective-permute-done.6 = bf16[2,64,768]{2,1,0:T(8,128)(2,1)S(1)} collective-permute-done((bf16[2,64,768]{2,1,0:T(8,128)(2,1)S(1)}, bf16[2,64,768]{2,1,0:T(8,128)(2,1)S(1)}, u32[]{:S(2)}, u32[]{:S(2)}) %collective-permute-start.6) | collective-permute-done | bytes 196640 | tf_op jit(solution)/shard_map/ppermute | solution.py:209
  94.4 6.9 %collective-permute-start.7 = (bf16[1,64,768]{2,1,0:T(8,128)(2,1)S(1)}, bf16[1,64,768]{2,1,0:T(8,128)(2,1)S(1)}, u32[]{:S(2)}, u32[]{:S(2)}) collective-permute-start(bf16[1,64,768]{2,1,0:T(8,128)(2,1)S(1)} %add_convert_fusion.6), channel_id=1, source_target_pairs={{0,256},{64,320},{128,384},{192,448},{256,0},{320,64},{384,128},{4... | collective-permute-start | bytes 294920 | tf_op jit(solution)/shard_map/ppermute | solution.py:209
  101.3 8.5 %collective-permute-done.7 = bf16[1,64,768]{2,1,0:T(8,128)(2,1)S(1)} collective-permute-done((bf16[1,64,768]{2,1,0:T(8,128)(2,1)S(1)}, bf16[1,64,768]{2,1,0:T(8,128)(2,1)S(1)}, u32[]{:S(2)}, u32[]{:S(2)}) %collective-permute-start.7) | collective-permute-done | bytes 98336 | tf_op jit(solution)/shard_map/ppermute | solution.py:209
  109.9 1.9 collective-permute-start.8
  111.9 1.1 collective-permute-done.8.halo_ref
  113.6 2.0 shard_map.106
  115.6 3.9 %collective-permute-start.9 = (bf16[128,256]{1,0:T(8,128)(2,1)}, bf16[128,256]{1,0:T(8,128)(2,1)S(1)}, u32[]{:S(2)}, u32[]{:S(2)}) collective-permute-start(bf16[128,256]{1,0:T(8,128)(2,1)} %get-tuple-element.34.prod_ref), channel_id=1, source_target_pairs={{0,32},{32,64},{64,96},{96,128},{128,160},{160,192},{192,224},{224... | collective-permute-start | bytes 196616 | tf_op jit(solution)/shard_map/ppermute | solution.py:215
  119.5 1.9 collective-permute-start.10
  121.4 3.8 %collective-permute-done.10.next_ref = bf16[128,256]{1,0:T(8,128)(2,1)S(1)} collective-permute-done((bf16[128,256]{1,0:T(8,128)(2,1)}, bf16[128,256]{1,0:T(8,128)(2,1)S(1)}, u32[]{:S(2)}, u32[]{:S(2)}) %collective-permute-start.10) | collective-permute-done | bytes 65568 | tf_op jit(solution)/shard_map/ppermute | solution.py:215
  125.9 3.2 %shard_map.107 = (bf16[128,256]{1,0:T(8,128)(2,1)}, f32[128,768]{1,0:T(8,128)}, f32[8,768]{1,0:T(8,128)}) custom-call(bf16[2048,256]{1,0:T(8,128)(2,1)} %get-tuple-element.27.fwd_ref, bf16[2048,256]{1,0:T(8,128)(2,1)} %get-tuple-element.28.bwd_ref, bf16[128,256]{1,0:T(8,128)(2,1)} %get-tuple-element.34.prod_ref, bf16[128,256]{1,0:T(8,128)(2,1)} %copy-done.15, ...), custom_call_target="tpu_custom_call" | custom-call | flops 1000000000 | bytes 2819072 | tf_op jit(solution)/shard_map/pallas_call | solution.py:22
  129.1 1.9 collective-permute-start.11
  131.0 3.4 %collective-permute-done.11.head_ref = f32[8,768]{1,0:T(8,128)S(1)} collective-permute-done((f32[8,768]{1,0:T(8,128)}, f32[8,768]{1,0:T(8,128)S(1)}, u32[]{:S(2)}, u32[]{:S(2)}) %collective-permute-start.11) | collective-permute-done | bytes 24608 | tf_op jit(solution)/shard_map/ppermute | solution.py:215
  135.0 2.0 shard_map.108
  137.0 2.6 %collective-permute-start.15 = (bf16[1,64,768]{2,1,0:T(8,128)(2,1)}, bf16[1,64,768]{2,1,0:T(8,128)(2,1)S(1)}, u32[]{:S(2)}, u32[]{:S(2)}) collective-permute-start(bf16[1,64,768]{2,1,0:T(8,128)(2,1)} %bitcast.45), channel_id=1, source_target_pairs={{0,256},{64,320},{128,384},{192,448},{256,0},{320,64},{384,128},{4... | collective-permute-start | bytes 294920 | tf_op jit(solution)/shard_map/ppermute | solution.py:209
  139.6 12.2 %collective-permute-done.15.refs_1_ = bf16[1,64,768]{2,1,0:T(8,128)(2,1)S(1)} collective-permute-done((bf16[1,64,768]{2,1,0:T(8,128)(2,1)}, bf16[1,64,768]{2,1,0:T(8,128)(2,1)S(1)}, u32[]{:S(2)}, u32[]{:S(2)}) %collective-permute-start.15) | collective-permute-done | bytes 98336 | tf_op jit(solution)/shard_map/ppermute | solution.py:209
  152.8 1.9 collective-permute-start.16
  154.7 9.2 %collective-permute-done.16.refs_2_ = bf16[2,64,768]{2,1,0:T(8,128)(2,1)S(1)} collective-permute-done((bf16[2,64,768]{2,1,0:T(8,128)(2,1)S(1)}, bf16[2,64,768]{2,1,0:T(8,128)(2,1)S(1)}, u32[]{:S(2)}, u32[]{:S(2)}) %collective-permute-start.16) | collective-permute-done | bytes 196640 | tf_op jit(solution)/shard_map/ppermute | solution.py:209
  164.9 1.9 collective-permute-start.17
  166.8 5.3 %collective-permute-start.12 = (bf16[1,64,768]{2,1,0:T(8,128)(2,1)}, bf16[1,64,768]{2,1,0:T(8,128)(2,1)S(1)}, u32[]{:S(2)}, u32[]{:S(2)}) collective-permute-start(bf16[1,64,768]{2,1,0:T(8,128)(2,1)} %bitcast.41), channel_id=1, source_target_pairs={{0,256},{64,320},{128,384},{192,448},{256,0},{320,64},{384,128},{4... | collective-permute-start | bytes 294920 | tf_op jit(solution)/shard_map/ppermute | solution.py:209
  172.2 5.1 %collective-permute-done.12.refs_1_ = bf16[1,64,768]{2,1,0:T(8,128)(2,1)S(1)} collective-permute-done((bf16[1,64,768]{2,1,0:T(8,128)(2,1)}, bf16[1,64,768]{2,1,0:T(8,128)(2,1)S(1)}, u32[]{:S(2)}, u32[]{:S(2)}) %collective-permute-start.12) | collective-permute-done | bytes 98336 | tf_op jit(solution)/shard_map/ppermute | solution.py:209
  178.2 6.7 %collective-permute-start.13 = (bf16[2,64,768]{2,1,0:T(8,128)(2,1)S(1)}, bf16[2,64,768]{2,1,0:T(8,128)(2,1)S(1)}, u32[]{:S(2)}, u32[]{:S(2)}) collective-permute-start(bf16[2,64,768]{2,1,0:T(8,128)(2,1)S(1)} %pad_maximum_fusion.2), channel_id=1, source_target_pairs={{0,128},{64,192},{128,0},{192,64},{256,384},{320,448},{384,256},{4... | collective-permute-start | bytes 589832 | tf_op jit(solution)/shard_map/ppermute | solution.py:209
  185.7 4.2 %shard_map.110 = (bf16[2,512,512]{2,1,0:T(8,128)(2,1)}, bf16[512,768]{1,0:T(8,128)(2,1)}) custom-call(s32[1]{0:T(128)} %bitcast.1.core_ref, bf16[512,512]{1,0:T(8,128)(2,1)} %get-tuple-element.40.order_ref, bf16[1,64,768]{2,1,0:T(8,128)(2,1)} %bitcast.48, bf16[1,64,768]{2,1,0:T(8,128)(2,1)} %copy-done.5, bf16[2,64,768]{2,1,0:T(8,128)(2,1)} %copy-done.8, ...), custom_call_target="tpu_custom_call" | custom-call | flops 1000000000 | bytes 2883588 | tf_op jit(solution)/shard_map/pallas_call | solution.py:22
  190.0 8.5 %all-to-all-start.3 = ((bf16[32,32,512]{2,1,0:T(8,128)(2,1)}), bf16[32,32,512]{2,1,0:T(8,128)(2,1)S(1)}, u32[]{:S(2)}, u32[]{:S(2)}) async-start(bf16[32,32,512]{2,1,0:T(8,128)(2,1)} %bitcast.40), calls=%async_computation.3 | async-start | bytes 2097152 | tf_op jit(solution)/shard_map/all_to_all | solution.py:259
  198.6 4.9 %collective-permute-start.14 = (bf16[4,64,768]{2,1,0:T(8,128)(2,1)S(1)}, bf16[4,64,768]{2,1,0:T(8,128)(2,1)S(1)}, u32[]{:S(2)}, u32[]{:S(2)}) collective-permute-start(bf16[4,64,768]{2,1,0:T(8,128)(2,1)S(1)} %pad_maximum_fusion), channel_id=1, source_target_pairs={{0,64},{64,0},{128,192},{192,128},{256,320},{320,256},{384,448},{4... | collective-permute-start | bytes 1179656 | tf_op jit(solution)/shard_map/ppermute | solution.py:209
  203.6 9.1 %collective-permute-done.14.refs_3_ = bf16[4,64,768]{2,1,0:T(8,128)(2,1)S(1)} collective-permute-done((bf16[4,64,768]{2,1,0:T(8,128)(2,1)S(1)}, bf16[4,64,768]{2,1,0:T(8,128)(2,1)S(1)}, u32[]{:S(2)}, u32[]{:S(2)}) %collective-permute-start.14) | collective-permute-done | bytes 393248 | tf_op jit(solution)/shard_map/ppermute | solution.py:209
  213.4 4.3 %shard_map.109 = (bf16[2,512,512]{2,1,0:T(8,128)(2,1)}, bf16[512,768]{1,0:T(8,128)(2,1)}) custom-call(s32[1]{0:T(128)} %bitcast.1.core_ref, bf16[512,512]{1,0:T(8,128)(2,1)} %get-tuple-element.40.order_ref, bf16[1,64,768]{2,1,0:T(8,128)(2,1)} %bitcast.43, bf16[1,64,768]{2,1,0:T(8,128)(2,1)} %copy-done.4, bf16[2,64,768]{2,1,0:T(8,128)(2,1)} %copy-done.7, ...), custom_call_target="tpu_custom_call" | custom-call | flops 1000000000 | bytes 2883588 | tf_op jit(solution)/shard_map/pallas_call | solution.py:22
  217.7 4.8 %shard_map.111 = (f32[3,512,256]{2,1,0:T(8,128)}, bf16[3,512,256]{2,1,0:T(8,128)(2,1)}) custom-call(s32[1]{0:T(128)} %bitcast.1.core_ref, bf16[2,512,512]{2,1,0:T(8,128)(2,1)} %bitcast.37, bf16[2,512,512]{2,1,0:T(8,128)(2,1)} %bitcast.39, bf16[512,768]{1,0:T(8,128)(2,1)} %get-tuple-element.47.g0_ref, bf16[512,768]{1,0:T(8,128)(2,1)} %get-tuple-element.48.g1_ref), custom_call_target="tpu_custom_call" | custom-call | flops 1000000000 | bytes 3670020 | tf_op jit(solution)/shard_map/pallas_call | solution.py:22
  222.4 2.7 %collective-permute-start.19 = (bf16[3,512,256]{2,1,0:T(8,128)(2,1)}, bf16[3,512,256]{2,1,0:T(8,128)(2,1)S(1)}, u32[]{:S(2)}, u32[]{:S(2)}) collective-permute-start(bf16[3,512,256]{2,1,0:T(8,128)(2,1)} %get-tuple-element.50), channel_id=1, source_target_pairs={{0,32},{32,0},{1,33},{33,1},{2,34},{34,2},{3,35},{35,3},{4,36},{36... | collective-permute-start | bytes 2359304 | tf_op jit(solution)/shard_map/ppermute | solution.py:209
  225.1 7.2 %all-to-all-start.2 = ((bf16[32,32,512]{2,1,0:T(8,128)(2,1)}), bf16[32,32,512]{2,1,0:T(8,128)(2,1)S(1)}, u32[]{:S(2)}, u32[]{:S(2)}) async-start(bf16[32,32,512]{2,1,0:T(8,128)(2,1)} %bitcast.19), calls=%async_computation.2 | async-start | bytes 2097152 | tf_op jit(solution)/shard_map/all_to_all | solution.py:259
  232.3 2.5 fusion
  234.9 11.6 %collective-permute-start.18 = (bf16[2,32,512]{2,1,0:T(8,128)(2,1)S(1)}, bf16[2,32,512]{2,1,0:T(8,128)(2,1)S(1)}, u32[]{:S(2)}, u32[]{:S(2)}) collective-permute-start(bf16[2,32,512]{2,1,0:T(8,128)(2,1)S(1)} %bitcast_reduce_fusion), channel_id=1, source_target_pairs={{0,1},{1,0},{2,3},{3,2},{4,5},{5,4},{6,7},{7,6},{8,9},{9,8},{10,11... | collective-permute-start | bytes 196616 | tf_op jit(solution)/shard_map/ppermute | solution.py:209
  246.5 2.2 all-to-all-done.2
  (76 shorter events, 13.3 us)
Async XLA Ops:
  0.6 1.0 copy-start
  2.9 27.1 %all-to-all-start = ((bf16[32,32,512]{2,1,0:T(8,128)(2,1)}), bf16[32,32,512]{2,1,0:T(8,128)(2,1)S(1)}, u32[]{:S(2)}, u32[]{:S(2)}) async-start(bf16[32,32,512]{2,1,0:T(8,128)(2,1)} %bitcast.4), calls=%async_computation | async-start | bytes 2097152 | tf_op jit(solution)/shard_map/all_to_all | solution.py:259
  13.5 15.9 %collective-permute-start.4 = (bf16[2,1,32,512]{3,2,0,1:T(8,128)(2,1)S(1)}, bf16[2,1,32,512]{3,2,0,1:T(8,128)(2,1)S(1)}, u32[]{:S(2)}, u32[]{:S(2)}) collective-permute-start(bf16[2,1,32,512]{3,2,0,1:T(8,128)(2,1)S(1)} %bitcast.50), channel_id=1, source_target_pairs={{0,1},{1,0},{2,3},{3,2},{4,5},{5,4},{6,7},{7,6},{8,9},{9,8},{10,11... | collective-permute-start | bytes 196616 | tf_op jit(solution)/shard_map/ppermute | solution.py:209
  27.0 16.9 %collective-permute-start = (bf16[3,512,256]{2,1,0:T(8,128)(2,1)}, bf16[3,512,256]{2,1,0:T(8,128)(2,1)}, u32[]{:S(2)}, u32[]{:S(2)}) collective-permute-start(bf16[3,512,256]{2,1,0:T(8,128)(2,1)} %bitcast.6.own_ref.refs_4_), channel_id=1, source_target_pairs={{0,32},{32,0},{1,33},{33,1},{2,34},{34,2},{3,35},{35,3},{4,36},{36... | collective-permute-start | bytes 2359304 | tf_op jit(solution)/shard_map/ppermute | solution.py:209
  30.0 1.3 copy-start.1
  30.0 8.7 %copy-start.11 = (f32[16,128]{1,0:T(8,128)S(1)}, f32[16,128]{1,0:T(8,128)}, u32[]{:S(2)}) copy-start(f32[16,128]{1,0:T(8,128)} %taps_ref.1) | copy-start | bytes 24580
  30.0 8.8 %copy-start.12 = (f32[16]{0:T(128)S(1)}, f32[16]{0:T(128)}, u32[]{:S(2)}) copy-start(f32[16]{0:T(128)} %param.12) | copy-start | bytes 196
  31.3 23.7 %all-to-all-start.1 = ((bf16[32,32,512]{2,1,0:T(8,128)(2,1)}), bf16[32,32,512]{2,1,0:T(8,128)(2,1)S(1)}, u32[]{:S(2)}, u32[]{:S(2)}) async-start(bf16[32,32,512]{2,1,0:T(8,128)(2,1)} %bitcast.10), calls=%async_computation.1 | async-start | bytes 2097152 | tf_op jit(solution)/shard_map/all_to_all | solution.py:259
  48.5 16.0 %collective-permute-start.1 = (bf16[4,64,768]{2,1,0:T(8,128)(2,1)}, bf16[4,64,768]{2,1,0:T(8,128)(2,1)S(1)}, u32[]{:S(2)}, u32[]{:S(2)}) collective-permute-start(bf16[4,64,768]{2,1,0:T(8,128)(2,1)} %get-tuple-element.31), channel_id=1, source_target_pairs={{0,64},{64,0},{128,192},{192,128},{256,320},{320,256},{384,448},{4... | collective-permute-start | bytes 1179656 | tf_op jit(solution)/shard_map/ppermute | solution.py:209
  55.0 1.0 copy-start.2
  56.0 8.6 %copy-start.6 = (bf16[4,64,768]{2,1,0:T(8,128)(2,1)S(1)}, bf16[4,64,768]{2,1,0:T(8,128)(2,1)}, u32[]{:S(2)}) copy-start(bf16[4,64,768]{2,1,0:T(8,128)(2,1)} %get-tuple-element.30) | copy-start | bytes 1179652
  60.6 16.5 %collective-permute-start.5 = (bf16[4,64,768]{2,1,0:T(8,128)(2,1)}, bf16[4,64,768]{2,1,0:T(8,128)(2,1)S(1)}, u32[]{:S(2)}, u32[]{:S(2)}) collective-permute-start(bf16[4,64,768]{2,1,0:T(8,128)(2,1)} %get-tuple-element.33), channel_id=1, source_target_pairs={{0,64},{64,0},{128,192},{192,128},{256,320},{320,256},{384,448},{4... | collective-permute-start | bytes 1179656 | tf_op jit(solution)/shard_map/ppermute | solution.py:209
  64.6 15.5 %collective-permute-start.2 = (bf16[2,64,768]{2,1,0:T(8,128)(2,1)S(1)}, bf16[2,64,768]{2,1,0:T(8,128)(2,1)S(1)}, u32[]{:S(2)}, u32[]{:S(2)}) collective-permute-start(bf16[2,64,768]{2,1,0:T(8,128)(2,1)S(1)} %get-tuple-element.54), channel_id=1, source_target_pairs={{0,128},{64,192},{128,0},{192,64},{256,384},{320,448},{384,256},{4... | collective-permute-start | bytes 589832 | tf_op jit(solution)/shard_map/ppermute | solution.py:209
  78.2 16.2 %collective-permute-start.6 = (bf16[2,64,768]{2,1,0:T(8,128)(2,1)S(1)}, bf16[2,64,768]{2,1,0:T(8,128)(2,1)S(1)}, u32[]{:S(2)}, u32[]{:S(2)}) collective-permute-start(bf16[2,64,768]{2,1,0:T(8,128)(2,1)S(1)} %get-tuple-element.52), channel_id=1, source_target_pairs={{0,128},{64,192},{128,0},{192,64},{256,384},{320,448},{384,256},{4... | collective-permute-start | bytes 589832 | tf_op jit(solution)/shard_map/ppermute | solution.py:209
  80.1 21.1 %collective-permute-start.3 = (bf16[1,64,768]{2,1,0:T(8,128)(2,1)S(1)}, bf16[1,64,768]{2,1,0:T(8,128)(2,1)S(1)}, u32[]{:S(2)}, u32[]{:S(2)}) collective-permute-start(bf16[1,64,768]{2,1,0:T(8,128)(2,1)S(1)} %add_convert_fusion.9), channel_id=1, source_target_pairs={{0,256},{64,320},{128,384},{192,448},{256,0},{320,64},{384,128},{4... | collective-permute-start | bytes 294920 | tf_op jit(solution)/shard_map/ppermute | solution.py:209
  94.4 15.5 %collective-permute-start.7 = (bf16[1,64,768]{2,1,0:T(8,128)(2,1)S(1)}, bf16[1,64,768]{2,1,0:T(8,128)(2,1)S(1)}, u32[]{:S(2)}, u32[]{:S(2)}) collective-permute-start(bf16[1,64,768]{2,1,0:T(8,128)(2,1)S(1)} %add_convert_fusion.6), channel_id=1, source_target_pairs={{0,256},{64,320},{128,384},{192,448},{256,0},{320,64},{384,128},{4... | collective-permute-start | bytes 294920 | tf_op jit(solution)/shard_map/ppermute | solution.py:209
  101.3 11.7 %copy-start.9 = (bf16[1,64,768]{2,1,0:T(8,128)(2,1)}, bf16[1,64,768]{2,1,0:T(8,128)(2,1)S(1)}, u32[]{:S(2)}) copy-start(bf16[1,64,768]{2,1,0:T(8,128)(2,1)S(1)} %add_convert_fusion.8) | copy-start | bytes 294916
  109.9 3.1 %copy-start.10 = (bf16[1,64,768]{2,1,0:T(8,128)(2,1)}, bf16[1,64,768]{2,1,0:T(8,128)(2,1)S(1)}, u32[]{:S(2)}) copy-start(bf16[1,64,768]{2,1,0:T(8,128)(2,1)S(1)} %add_convert_fusion.5) | copy-start | bytes 294916
  109.9 3.1 %collective-permute-start.8 = (bf16[8,768]{1,0:T(8,128)(2,1)S(1)}, bf16[8,768]{1,0:T(8,128)(2,1)S(1)}, u32[]{:S(2)}, u32[]{:S(2)}) collective-permute-start(bf16[8,768]{1,0:T(8,128)(2,1)S(1)} %fusion.3), channel_id=1, source_target_pairs={{0,32},{32,64},{64,96},{96,128},{128,160},{160,192},{192,224},{224... | collective-permute-start | bytes 36872 | tf_op jit(solution)/shard_map/ppermute | solution.py:215
  113.0 0.6 copy-start.18
  115.6 5.8 %collective-permute-start.9 = (bf16[128,256]{1,0:T(8,128)(2,1)}, bf16[128,256]{1,0:T(8,128)(2,1)S(1)}, u32[]{:S(2)}, u32[]{:S(2)}) collective-permute-start(bf16[128,256]{1,0:T(8,128)(2,1)} %get-tuple-element.34.prod_ref), channel_id=1, source_target_pairs={{0,32},{32,64},{64,96},{96,128},{128,160},{160,192},{192,224},{224... | collective-permute-start | bytes 196616 | tf_op jit(solution)/shard_map/ppermute | solution.py:215
  119.5 5.8 %collective-permute-start.10 = (bf16[128,256]{1,0:T(8,128)(2,1)}, bf16[128,256]{1,0:T(8,128)(2,1)S(1)}, u32[]{:S(2)}, u32[]{:S(2)}) collective-permute-start(bf16[128,256]{1,0:T(8,128)(2,1)} %get-tuple-element.35.cg_ref), channel_id=1, source_target_pairs={{32,0},{64,32},{96,64},{128,96},{160,128},{192,160},{224,192},{256... | collective-permute-start | bytes 196616 | tf_op jit(solution)/shard_map/ppermute | solution.py:215
  121.4 3.9 %copy-start.15 = (bf16[128,256]{1,0:T(8,128)(2,1)}, bf16[128,256]{1,0:T(8,128)(2,1)S(1)}, u32[]{:S(2)}) copy-start(bf16[128,256]{1,0:T(8,128)(2,1)S(1)} %collective-permute-done.9.prev_ref) | copy-start | bytes 196612
  125.3 0.6 copy-start.16
  129.1 5.3 %collective-permute-start.11 = (f32[8,768]{1,0:T(8,128)}, f32[8,768]{1,0:T(8,128)S(1)}, u32[]{:S(2)}, u32[]{:S(2)}) collective-permute-start(f32[8,768]{1,0:T(8,128)} %get-tuple-element.42), channel_id=1, source_target_pairs={{32,0},{64,32},{96,64},{128,96},{160,128},{192,160},{224,192},{256... | collective-permute-start | bytes 73736 | tf_op jit(solution)/shard_map/ppermute | solution.py:215
  134.4 0.6 copy-start.17
  137.0 14.8 %collective-permute-start.15 = (bf16[1,64,768]{2,1,0:T(8,128)(2,1)}, bf16[1,64,768]{2,1,0:T(8,128)(2,1)S(1)}, u32[]{:S(2)}, u32[]{:S(2)}) collective-permute-start(bf16[1,64,768]{2,1,0:T(8,128)(2,1)} %bitcast.45), channel_id=1, source_target_pairs={{0,256},{64,320},{128,384},{192,448},{256,0},{320,64},{384,128},{4... | collective-permute-start | bytes 294920 | tf_op jit(solution)/shard_map/ppermute | solution.py:209
  151.8 33.1 %copy-start.5 = (bf16[1,64,768]{2,1,0:T(8,128)(2,1)}, bf16[1,64,768]{2,1,0:T(8,128)(2,1)S(1)}, u32[]{:S(2)}) copy-start(bf16[1,64,768]{2,1,0:T(8,128)(2,1)S(1)} %collective-permute-done.15.refs_1_) | copy-start | bytes 294916
  152.8 11.1 %collective-permute-start.16 = (bf16[2,64,768]{2,1,0:T(8,128)(2,1)S(1)}, bf16[2,64,768]{2,1,0:T(8,128)(2,1)S(1)}, u32[]{:S(2)}, u32[]{:S(2)}) collective-permute-start(bf16[2,64,768]{2,1,0:T(8,128)(2,1)S(1)} %pad_maximum_fusion.3), channel_id=1, source_target_pairs={{0,128},{64,192},{128,0},{192,64},{256,384},{320,448},{384,256},{4... | collective-permute-start | bytes 589832 | tf_op jit(solution)/shard_map/ppermute | solution.py:209
  163.9 21.1 %copy-start.8 = (bf16[2,64,768]{2,1,0:T(8,128)(2,1)}, bf16[2,64,768]{2,1,0:T(8,128)(2,1)S(1)}, u32[]{:S(2)}) copy-start(bf16[2,64,768]{2,1,0:T(8,128)(2,1)S(1)} %collective-permute-done.16.refs_2_) | copy-start | bytes 589828
  164.9 20.1 %collective-permute-start.17 = (bf16[4,64,768]{2,1,0:T(8,128)(2,1)S(1)}, bf16[4,64,768]{2,1,0:T(8,128)(2,1)S(1)}, u32[]{:S(2)}, u32[]{:S(2)}) collective-permute-start(bf16[4,64,768]{2,1,0:T(8,128)(2,1)S(1)} %pad_maximum_fusion.1), channel_id=1, source_target_pairs={{0,64},{64,0},{128,192},{192,128},{256,320},{320,256},{384,448},{4... | collective-permute-start | bytes 1179656 | tf_op jit(solution)/shard_map/ppermute | solution.py:209
  166.8 10.5 %collective-permute-start.12 = (bf16[1,64,768]{2,1,0:T(8,128)(2,1)}, bf16[1,64,768]{2,1,0:T(8,128)(2,1)S(1)}, u32[]{:S(2)}, u32[]{:S(2)}) collective-permute-start(bf16[1,64,768]{2,1,0:T(8,128)(2,1)} %bitcast.41), channel_id=1, source_target_pairs={{0,256},{64,320},{128,384},{192,448},{256,0},{320,64},{384,128},{4... | collective-permute-start | bytes 294920 | tf_op jit(solution)/shard_map/ppermute | solution.py:209
  177.3 21.2 %copy-start.4 = (bf16[1,64,768]{2,1,0:T(8,128)(2,1)}, bf16[1,64,768]{2,1,0:T(8,128)(2,1)S(1)}, u32[]{:S(2)}) copy-start(bf16[1,64,768]{2,1,0:T(8,128)(2,1)S(1)} %collective-permute-done.12.refs_1_) | copy-start | bytes 294916
  178.2 20.3 %collective-permute-start.13 = (bf16[2,64,768]{2,1,0:T(8,128)(2,1)S(1)}, bf16[2,64,768]{2,1,0:T(8,128)(2,1)S(1)}, u32[]{:S(2)}, u32[]{:S(2)}) collective-permute-start(bf16[2,64,768]{2,1,0:T(8,128)(2,1)S(1)} %pad_maximum_fusion.2), channel_id=1, source_target_pairs={{0,128},{64,192},{128,0},{192,64},{256,384},{320,448},{384,256},{4... | collective-permute-start | bytes 589832 | tf_op jit(solution)/shard_map/ppermute | solution.py:209
  185.0 0.7 copy-start.13
  190.0 8.6 %copy-start.3 = (bf16[64,768]{1,0:T(8,128)(2,1)S(1)}, bf16[64,768]{1,0:T(8,128)(2,1)}, u32[]{:S(2)}) copy-start(bf16[64,768]{1,0:T(8,128)(2,1)} %get-tuple-element.43) | copy-start | bytes 294916
  190.0 35.2 %all-to-all-start.3 = ((bf16[32,32,512]{2,1,0:T(8,128)(2,1)}), bf16[32,32,512]{2,1,0:T(8,128)(2,1)S(1)}, u32[]{:S(2)}, u32[]{:S(2)}) async-start(bf16[32,32,512]{2,1,0:T(8,128)(2,1)} %bitcast.40), calls=%async_computation.3 | async-start | bytes 2097152 | tf_op jit(solution)/shard_map/all_to_all | solution.py:259
  198.5 14.1 %copy-start.7 = (bf16[2,64,768]{2,1,0:T(8,128)(2,1)}, bf16[2,64,768]{2,1,0:T(8,128)(2,1)S(1)}, u32[]{:S(2)}) copy-start(bf16[2,64,768]{2,1,0:T(8,128)(2,1)S(1)} %collective-permute-done.13.refs_2_) | copy-start | bytes 589828
  198.6 14.0 %collective-permute-start.14 = (bf16[4,64,768]{2,1,0:T(8,128)(2,1)S(1)}, bf16[4,64,768]{2,1,0:T(8,128)(2,1)S(1)}, u32[]{:S(2)}, u32[]{:S(2)}) collective-permute-start(bf16[4,64,768]{2,1,0:T(8,128)(2,1)S(1)} %pad_maximum_fusion), channel_id=1, source_target_pairs={{0,64},{64,0},{128,192},{192,128},{256,320},{320,256},{384,448},{4... | collective-permute-start | bytes 1179656 | tf_op jit(solution)/shard_map/ppermute | solution.py:209
  212.6 0.8 copy-start.14
  222.4 9.9 %collective-permute-start.19 = (bf16[3,512,256]{2,1,0:T(8,128)(2,1)}, bf16[3,512,256]{2,1,0:T(8,128)(2,1)S(1)}, u32[]{:S(2)}, u32[]{:S(2)}) collective-permute-start(bf16[3,512,256]{2,1,0:T(8,128)(2,1)} %get-tuple-element.50), channel_id=1, source_target_pairs={{0,32},{32,0},{1,33},{33,1},{2,34},{34,2},{3,35},{35,3},{4,36},{36... | collective-permute-start | bytes 2359304 | tf_op jit(solution)/shard_map/ppermute | solution.py:209
  225.1 23.5 %all-to-all-start.2 = ((bf16[32,32,512]{2,1,0:T(8,128)(2,1)}), bf16[32,32,512]{2,1,0:T(8,128)(2,1)S(1)}, u32[]{:S(2)}, u32[]{:S(2)}) async-start(bf16[32,32,512]{2,1,0:T(8,128)(2,1)} %bitcast.19), calls=%async_computation.2 | async-start | bytes 2097152 | tf_op jit(solution)/shard_map/all_to_all | solution.py:259
  234.9 14.0 %collective-permute-start.18 = (bf16[2,32,512]{2,1,0:T(8,128)(2,1)S(1)}, bf16[2,32,512]{2,1,0:T(8,128)(2,1)S(1)}, u32[]{:S(2)}, u32[]{:S(2)}) collective-permute-start(bf16[2,32,512]{2,1,0:T(8,128)(2,1)S(1)} %bitcast_reduce_fusion), channel_id=1, source_target_pairs={{0,1},{1,0},{2,3},{3,2},{4,5},{5,4},{6,7},{7,6},{8,9},{9,8},{10,11... | collective-permute-start | bytes 196616 | tf_op jit(solution)/shard_map/ppermute | solution.py:209

commit v4 on v3

--- a/solution.py
+++ b/solution.py
@@ -148,61 +148,69 @@
     return moved
 
 
-def gate_body(tokens, f0_ref, f1_ref, halo_ref, short_ref, up_ref, half_ref, q_ref, k_ref, v_ref, prod_ref, cg_ref):
+def gate_body(tokens, f0_ref, f1_ref, tail_ref, head_ref, short_ref, up_ref, after_ref, half_ref, q_ref, k_ref, v_ref, n_ref, prod_ref, cg_ref):
     count = f0_ref.shape[0] * 2
     order = token_order(half_ref[0], tokens, count, False)
     features = dot(order, jnp.concatenate([f0_ref[...], f1_ref[...]], axis=0))
     channels = up_ref.shape[1]
     outs = (q_ref, k_ref, v_ref)
-    halo = halo_ref[...].astype(F32)
+    tail = tail_ref[...].astype(F32)
+    head = head_ref[...].astype(F32)
     for i in range(3):
         cols = slice(i * channels, (i + 1) * channels)
-        x, border = features[:, cols], halo[:, cols]
-        total = short_ref[0, i : i + 1] * x
+        own, border = features[:, cols], tail[:, cols]
+        following, own_tail = head[:, cols], features[count - 8 :, cols]
+        total = short_ref[0, i : i + 1] * own
+        ahead = short_ref[0, i : i + 1] * following
         for lag in range(1, short_ref.shape[0]):
-            total = total + short_ref[lag, i : i + 1] * later(x, border, lag)
+            total = total + short_ref[lag, i : i + 1] * later(own, border, lag)
+            ahead = ahead + short_ref[lag, i : i + 1] * later(following, own_tail, lag)
         outs[i][...] = total
+        n_ref[i] = ahead
     prod_ref[...] = (k_ref[...] * v_ref[...]).astype(BF16)
-    cg_ref[...] = (up_ref[...].astype(F32) * q_ref[...]).astype(BF16)
-
-
-def convolve(t_ref, own, far):
-    both = jnp.concatenate([own, far], axis=0)
-    count, channels = own.shape
+    cg_ref[:count] = (up_ref[...].astype(F32) * q_ref[...]).astype(BF16)
+    first = after_ref[...].astype(F32) * n_ref[0]
+    row = lax.broadcasted_iota(jnp.int32, first.shape, 0)
+    cg_ref[count:] = jnp.where(row == 0, first, 0.0).astype(BF16)
+
+
+def convolve(t_ref, both, rows):
+    count, channels = both.shape[0] // 2, both.shape[1]
     filters = t_ref.shape[0] // count
     group = lax.broadcasted_iota(jnp.int32, (1, channels), 1) // (channels // filters)
-    total = jnp.zeros((count, channels), F32)
+    total = jnp.zeros((rows, channels), F32)
     for n in range(filters):
-        part = dot(t_ref[n * count : (n + 1) * count, :], both)
+        part = dot(t_ref[n * count : n * count + rows, :], both)
         total = jnp.where(group == n, part, total)
     return total
 
 
-def hyena_body(fwd_ref, bwd_ref, prod_ref, prev_ref, cg_ref, next_ref, q_ref, k_ref, v_ref, up_ref, skip_ref, out_ref, fg_ref, head_ref):
-    channels = up_ref.shape[1]
+def hyena_body(
+    tokens, fwd_ref, bwd_ref, prod_ref, prev_ref, cg_ref, next_ref, q_ref, k_ref, v_ref, n_ref, up_ref, after_ref, skip_ref, short_ref, half_ref,
+    out_ref, g0_ref, g1_ref,
+):
+    count, channels = up_ref.shape
+    ahead = after_ref.shape[0]
     up, q, k, v, skip = up_ref[...].astype(F32), q_ref[...], k_ref[...], v_ref[...], skip_ref[...]
-    convolved = convolve(fwd_ref, prod_ref[...], prev_ref[...]) + skip * (k * v)
+    convolved = convolve(fwd_ref, jnp.concatenate([prod_ref[...], prev_ref[...]], axis=0), count) + skip * (k * v)
     out_ref[...] = (q * convolved).astype(BF16)
-    fg_ref[:, :channels] = up * convolved
-    back = convolve(bwd_ref, cg_ref[...], next_ref[...]) + skip * (up * q)
-    fg_ref[:, channels : 2 * channels] = back * v
-    fg_ref[:, 2 * channels :] = back * k
-    head_ref[...] = fg_ref[:8]
-
-
-def grad_body(tokens, fg_ref, head_ref, short_ref, half_ref, out0_ref, out1_ref):
-    count, wide = fg_ref.shape
-    channels = wide // 3
+    following = next_ref[...]
+    back = convolve(bwd_ref, jnp.concatenate([cg_ref[:count], following[:count]], axis=0), count) + skip * (up * q)
+    up_n, q_n, k_n, v_n = after_ref[...].astype(F32), n_ref[0], n_ref[1], n_ref[2]
+    pad = jnp.zeros((count - ahead, channels), BF16)
+    both = jnp.concatenate([(k_n * v_n).astype(BF16), pad, prod_ref[...]], axis=0)
+    convolved_n = convolve(fwd_ref, both, ahead) + skip * (k_n * v_n)
+    back_n = convolve(bwd_ref, jnp.concatenate([following, pad], axis=0), ahead) + skip * (up_n * q_n)
     order = token_order(half_ref[0], tokens, count, True)
-    for i in range(3):
+    grads = ((up * convolved, up_n * convolved_n), (back * v, back_n * v_n), (back * k, back_n * k_n))
+    for i, (x, border) in enumerate(grads):
         cols = slice(i * channels, (i + 1) * channels)
-        x, border = fg_ref[:, cols], head_ref[:, cols]
         total = short_ref[0, i : i + 1] * x
         for lag in range(1, short_ref.shape[0]):
             total = total + short_ref[lag, i : i + 1] * sooner(x, border, lag)
         turned = dot(order, total.astype(BF16)).astype(BF16)
-        out0_ref[:, cols] = turned[: count // 2]
-        out1_ref[:, cols] = turned[count // 2 :]
+        g0_ref[:, cols] = turned[: count // 2]
+        g1_ref[:, cols] = turned[count // 2 :]
 
 
 def swap(x, axis, by=1):
@@ -263,6 +271,8 @@
         return exchange(jnp.broadcast_to(x, (2, pieces, lines, rows))).reshape(2, pieces * lines, rows)
 
     x_near = spread(local)
+    upstream = output_grad.reshape(count, channels)
+    after = shifted(upstream[:16], -1)
     far = swap(local, "zh", 1)
     w_own = featurizer.transpose(1, 0, 2)
     w_peer = swap(w_own, "core")
@@ -283,23 +293,23 @@
     parts = call(project, part_shape, here, turn, x_far, w_own, w_peer)
     f_far = line_scatter(*parts)
 
-    last = jnp.where(zh == 1, f_near[-8:], f_far[-8:])
-    halo = shifted(last, 1)
-    upstream = output_grad.reshape(count, channels)
+    tail = shifted(jnp.where(zh == 1, f_near[-8:], f_far[-8:]), 1)
+    head = shifted(jnp.where(zh == 0, f_near[:16], f_far[:16]), -1)
     plane = shape((count, channels), F32)
     thin = shape((count, channels), BF16)
-    q, k, v, prod, cg = call(
-        functools.partial(gate_body, tokens), (plane, plane, plane, thin, thin), f_near, f_far, halo, short_filter, upstream, half
+    longer = shape((count + 16, channels), BF16)
+    q, k, v, ahead, prod, cg = call(
+        functools.partial(gate_body, tokens),
+        (plane, plane, plane, shape((3, 16, channels), F32), thin, longer),
+        f_near, f_far, tail, head, short_filter, upstream, after, half,
     )
     prev, nxt = shifted(prod, 1), shifted(cg, -1)
-    hyena, fg, head = call(
-        hyena_body,
-        (thin, shape((count, wide), F32), shape((8, wide), F32)),
-        t_fwd, t_bwd, prod, prev, cg, nxt, q, k, v, upstream, skip_gain[None, :],
+    piece_shape = shape((count // 2, wide), BF16)
+    hyena, g_near, g_far = call(
+        functools.partial(hyena_body, tokens),
+        (thin, piece_shape, piece_shape),
+        t_fwd, t_bwd, prod, prev, cg, nxt, q, k, v, ahead, upstream, after, skip_gain[None, :], short_filter, half,
     )
-    head = shifted(head, -1)
-    piece_shape = shape((count // 2, wide), BF16)
-    g_near, g_far = call(functools.partial(grad_body, tokens), (piece_shape, piece_shape), fg, head, short_filter, half)
     back_shapes = (shape((2, pieces * lines, rows), BF16), shape((pieces * lines, wide), BF16))
 
     def collect(x):

time: 254 us -> 252 us (level)
  waiting for transfers between devices: 74.4 us -> 70.1 us
  starting transfers between devices: 124 us -> 127 us
    ppermute x4 -> x5, waiting for transfers between devices: 8.42 us -> 4.68 us  [shifted(): lax.ppermute(x, axis, [(i, i + by) for i in range(count) if 0 <= i + by <...]
    ppermute x4 -> x5, starting transfers between devices: 9.6 us -> 11.8 us  [shifted(): lax.ppermute(x, axis, [(i, i + by) for i in range(count) if 0 <= i + by <...]
    pallas_call x9 -> x8, Pallas kernels: 33.4 us -> 32 us  [call(): pl.pallas_call(body, out_shape=outs, in_specs=[scalar if a.shape == (1,)...]
  transfers between devices with their start and end apart: 24 -> 25, of which waited for: 14 -> 13; matrix products, arithmetic and copies ran while one was open for 3% -> 3% of each run, Pallas kernels for 10% -> 11%
where the time goes in v4:
time: 252 us; the launch traced here: 248 us
  starting transfers between devices  127 us (50%)
  waiting for transfers between devices  70.1 us (28%)
  Pallas kernels  32 us (13%)
  other arithmetic  8.48 us (3%)
  local copies, waits for them, and re-layouts  7.86 us (3%)
    ppermute x16, starting transfers between devices, swap(): lax.ppermute(x, axis, [(i, i ^ by) for i in range(lax.axis_size(axis))])  81.3 us
    ppermute x16, waiting for transfers between devices, swap(): lax.ppermute(x, axis, [(i, i ^ by) for i in range(lax.axis_size(axis))])  60.4 us
    all_to_all x4, starting transfers between devices, exchange(): lax.all_to_all(x.reshape(2 * pieces, lines, rows), ('core', 'x', 'y'), 0,...  34.2 us
    pallas_call x8, Pallas kernels, call(): pl.pallas_call(body, out_shape=outs, in_specs=[scalar if a.shape == (1,)...  32 us
    ppermute x5, starting transfers between devices, shifted(): lax.ppermute(x, axis, [(i, i + by) for i in range(count) if 0 <= i + by <...  11.8 us
    all_to_all x4, waiting for transfers between devices, exchange(): lax.all_to_all(x.reshape(2 * pieces, lines, rows), ('core', 'x', 'y'), 0,...  5.09 us
  transfers between devices with their start and end apart: 25, of which 13 were waited for; matrix products, arithmetic and copies ran while one was open for 3% of the time, Pallas kernels for 11%

profile of v4, /device:TPU:1, one launch (start us, length us, event | category | flops | bytes accessed | tf_op | source)
XLA Modules:
  0.0 248.0 jit_solution(1533299602819000731)
XLA Ops:
  1.8 1.1 broadcast_in_dim.32
  2.9 10.5 %all-to-all-start = ((bf16[32,32,512]{2,1,0:T(8,128)(2,1)}), bf16[32,32,512]{2,1,0:T(8,128)(2,1)S(1)}, u32[]{:S(2)}, u32[]{:S(2)}) async-start(bf16[32,32,512]{2,1,0:T(8,128)(2,1)} %bitcast.4), calls=%async_computation | async-start | bytes 2097152 | tf_op jit(solution)/shard_map/all_to_all | solution.py:267
  13.5 13.5 %collective-permute-start.4 = (bf16[2,1,32,512]{3,2,0,1:T(8,128)(2,1)S(1)}, bf16[2,1,32,512]{3,2,0,1:T(8,128)(2,1)S(1)}, u32[]{:S(2)}, u32[]{:S(2)}) collective-permute-start(bf16[2,1,32,512]{3,2,0,1:T(8,128)(2,1)S(1)} %bitcast.54), channel_id=1, source_target_pairs={{0,1},{1,0},{2,3},{3,2},{4,5},{5,4},{6,7},{7,6},{8,9},{9,8},{10,11... | collective-permute-start | bytes 196616 | tf_op jit(solution)/shard_map/ppermute | solution.py:217
  27.0 2.4 collective-permute-start
  30.0 1.2 broadcast_in_dim.34
  31.3 7.4 %all-to-all-start.1 = ((bf16[32,32,512]{2,1,0:T(8,128)(2,1)}), bf16[32,32,512]{2,1,0:T(8,128)(2,1)S(1)}, u32[]{:S(2)}, u32[]{:S(2)}) async-start(bf16[32,32,512]{2,1,0:T(8,128)(2,1)} %bitcast.10), calls=%async_computation.1 | async-start | bytes 2097152 | tf_op jit(solution)/shard_map/all_to_all | solution.py:267
  40.2 3.7 %shard_map.103 = (bf16[2048,256]{1,0:T(8,128)(2,1)}, bf16[2048,256]{1,0:T(8,128)(2,1)}, bf16[512,512]{1,0:T(8,128)(2,1)}, bf16[512,512]{1,0:T(8,128)(2,1)}) custom-call(f32[16,128]{1,0:T(8,128)} %taps_ref.1, f32[16,128]{1,0:T(8,128)} %pad_maximum_fusion.4.rev_ref, f32[16,1]{1,0:T(8,128)} %copy.12.decay_ref), custom_call_target="tpu_custom_call" | custom-call | flops 1000000000 | bytes 16448 | tf_op jit(solution)/shard_map/pallas_call | solution.py:22
  43.9 4.6 %shard_map.104 = (bf16[4,64,768]{2,1,0:T(8,128)(2,1)}, bf16[4,64,768]{2,1,0:T(8,128)(2,1)}) custom-call(s32[1]{0:T(128)} %bitcast.1.core_ref, bf16[512,512]{1,0:T(8,128)(2,1)} %get-tuple-element.28.order_ref, bf16[2,512,512]{2,1,0:T(8,128)(2,1)} %bitcast.40, bf16[3,512,256]{2,1,0:T(8,128)(2,1)} %bitcast.6.own_ref.refs_4_, ...), custom_call_target="tpu_custom_call" | custom-call | flops 1000000000 | bytes 3145732 | tf_op jit(solution)/shard_map/pallas_call | solution.py:22
  48.5 3.9 %collective-permute-start.1 = (bf16[4,64,768]{2,1,0:T(8,128)(2,1)}, bf16[4,64,768]{2,1,0:T(8,128)(2,1)S(1)}, u32[]{:S(2)}, u32[]{:S(2)}) collective-permute-start(bf16[4,64,768]{2,1,0:T(8,128)(2,1)} %get-tuple-element.30), channel_id=1, source_target_pairs={{0,64},{64,0},{128,192},{192,128},{256,320},{320,256},{384,448},{4... | collective-permute-start | bytes 1179656 | tf_op jit(solution)/shard_map/ppermute | solution.py:217
  52.4 2.6 %all-to-all-done.1 = bf16[32,32,512]{2,1,0:T(8,128)(2,1)S(1)} async-done(((bf16[32,32,512]{2,1,0:T(8,128)(2,1)}), bf16[32,32,512]{2,1,0:T(8,128)(2,1)S(1)}, u32[]{:S(2)}, u32[]{:S(2)}) %all-to-all-start.1) | async-done | bytes 1048608 | tf_op jit(solution)/shard_map/all_to_all | solution.py:267
  55.9 4.6 %shard_map.105 = (bf16[4,64,768]{2,1,0:T(8,128)(2,1)}, bf16[4,64,768]{2,1,0:T(8,128)(2,1)}) custom-call(s32[1]{0:T(128)} %bitcast.1.core_ref, bf16[512,512]{1,0:T(8,128)(2,1)} %get-tuple-element.28.order_ref, bf16[2,512,512]{2,1,0:T(8,128)(2,1)} %bitcast.42, bf16[3,512,256]{2,1,0:T(8,128)(2,1)} %bitcast.6.own_ref.refs_4_, ...), custom_call_target="tpu_custom_call" | custom-call | flops 1000000000 | bytes 3145732 | tf_op jit(solution)/shard_map/pallas_call | solution.py:22
  60.5 3.9 %collective-permute-start.5 = (bf16[4,64,768]{2,1,0:T(8,128)(2,1)}, bf16[4,64,768]{2,1,0:T(8,128)(2,1)S(1)}, u32[]{:S(2)}, u32[]{:S(2)}) collective-permute-start(bf16[4,64,768]{2,1,0:T(8,128)(2,1)} %get-tuple-element.32), channel_id=1, source_target_pairs={{0,64},{64,0},{128,192},{192,128},{256,320},{320,256},{384,448},{4... | collective-permute-start | bytes 1179656 | tf_op jit(solution)/shard_map/ppermute | solution.py:217
  64.6 2.5 collective-permute-start.2
  67.1 9.9 %collective-permute-done.5 = bf16[4,64,768]{2,1,0:T(8,128)(2,1)S(1)} collective-permute-done((bf16[4,64,768]{2,1,0:T(8,128)(2,1)}, bf16[4,64,768]{2,1,0:T(8,128)(2,1)S(1)}, u32[]{:S(2)}, u32[]{:S(2)}) %collective-permute-start.5) | collective-permute-done | bytes 393248 | tf_op jit(solution)/shard_map/ppermute | solution.py:217
  77.0 1.1 add_convert_fusion.2
  78.1 1.9 collective-permute-start.6
  80.1 7.6 %collective-permute-start.3 = (bf16[1,64,768]{2,1,0:T(8,128)(2,1)S(1)}, bf16[1,64,768]{2,1,0:T(8,128)(2,1)S(1)}, u32[]{:S(2)}, u32[]{:S(2)}) collective-permute-start(bf16[1,64,768]{2,1,0:T(8,128)(2,1)S(1)} %add_convert_fusion.9), channel_id=1, source_target_pairs={{0,256},{64,320},{128,384},{192,448},{256,0},{320,64},{384,128},{4... | collective-permute-start | bytes 294920 | tf_op jit(solution)/shard_map/ppermute | solution.py:217
  87.7 6.6 %collective-permute-done.6 = bf16[2,64,768]{2,1,0:T(8,128)(2,1)S(1)} collective-permute-done((bf16[2,64,768]{2,1,0:T(8,128)(2,1)S(1)}, bf16[2,64,768]{2,1,0:T(8,128)(2,1)S(1)}, u32[]{:S(2)}, u32[]{:S(2)}) %collective-permute-start.6) | collective-permute-done | bytes 196640 | tf_op jit(solution)/shard_map/ppermute | solution.py:217
  94.3 6.9 %collective-permute-start.7 = (bf16[1,64,768]{2,1,0:T(8,128)(2,1)S(1)}, bf16[1,64,768]{2,1,0:T(8,128)(2,1)S(1)}, u32[]{:S(2)}, u32[]{:S(2)}) collective-permute-start(bf16[1,64,768]{2,1,0:T(8,128)(2,1)S(1)} %add_convert_fusion.6), channel_id=1, source_target_pairs={{0,256},{64,320},{128,384},{192,448},{256,0},{320,64},{384,128},{4... | collective-permute-start | bytes 294920 | tf_op jit(solution)/shard_map/ppermute | solution.py:217
  101.3 8.5 %collective-permute-done.7 = bf16[1,64,768]{2,1,0:T(8,128)(2,1)S(1)} collective-permute-done((bf16[1,64,768]{2,1,0:T(8,128)(2,1)S(1)}, bf16[1,64,768]{2,1,0:T(8,128)(2,1)S(1)}, u32[]{:S(2)}, u32[]{:S(2)}) %collective-permute-start.7) | collective-permute-done | bytes 98336 | tf_op jit(solution)/shard_map/ppermute | solution.py:217
  109.9 1.9 collective-permute-start.8
  111.8 2.4 collective-permute-start.9
  114.9 1.9 collective-permute-start.10
  116.9 3.0 %collective-permute-done.10.after_ref = bf16[16,256]{1,0:T(8,128)(2,1)S(1)} collective-permute-done((bf16[16,256]{1,0:T(8,128)(2,1)S(1)}, bf16[16,256]{1,0:T(8,128)(2,1)S(1)}, u32[]{:S(2)}, u32[]{:S(2)}) %collective-permute-start.10) | collective-permute-done | bytes 8224 | tf_op jit(solution)/shard_map/ppermute | solution.py:223
  120.5 2.0 shard_map.106
  122.6 1.9 collective-permute-start.12
  124.5 3.6 %collective-permute-start.11 = (bf16[128,256]{1,0:T(8,128)(2,1)}, bf16[128,256]{1,0:T(8,128)(2,1)S(1)}, u32[]{:S(2)}, u32[]{:S(2)}) collective-permute-start(bf16[128,256]{1,0:T(8,128)(2,1)} %get-tuple-element.33.prod_ref), channel_id=1, source_target_pairs={{0,32},{32,64},{64,96},{96,128},{128,160},{160,192},{192,224},{224... | collective-permute-start | bytes 196616 | tf_op jit(solution)/shard_map/ppermute | solution.py:223
  128.1 1.6 collective-permute-done.11.prev_ref
  130.4 3.7 %shard_map.107 = (bf16[128,256]{1,0:T(8,128)(2,1)}, bf16[64,768]{1,0:T(8,128)(2,1)}, bf16[64,768]{1,0:T(8,128)(2,1)}) custom-call(bf16[2048,256]{1,0:T(8,128)(2,1)} %get-tuple-element.26.fwd_ref, bf16[2048,256]{1,0:T(8,128)(2,1)} %get-tuple-element.27.bwd_ref, bf16[128,256]{1,0:T(8,128)(2,1)} %get-tuple-element.33.prod_ref, bf16[128,256]{1,0:T(8,128)(2,1)} %copy-done.16, ...), custom_call_target="tpu_custom_call" | custom-call | flops 1000000000 | bytes 2902020 | tf_op jit(solution)/shard_map/pallas_call | solution.py:22
  134.2 3.8 %collective-permute-start.16 = (bf16[1,64,768]{2,1,0:T(8,128)(2,1)}, bf16[1,64,768]{2,1,0:T(8,128)(2,1)S(1)}, u32[]{:S(2)}, u32[]{:S(2)}) collective-permute-start(bf16[1,64,768]{2,1,0:T(8,128)(2,1)} %bitcast.49), channel_id=1, source_target_pairs={{0,256},{64,320},{128,384},{192,448},{256,0},{320,64},{384,128},{4... | collective-permute-start | bytes 294920 | tf_op jit(solution)/shard_map/ppermute | solution.py:217
  138.0 12.4 %collective-permute-done.16.refs_1_ = bf16[1,64,768]{2,1,0:T(8,128)(2,1)S(1)} collective-permute-done((bf16[1,64,768]{2,1,0:T(8,128)(2,1)}, bf16[1,64,768]{2,1,0:T(8,128)(2,1)S(1)}, u32[]{:S(2)}, u32[]{:S(2)}) %collective-permute-start.16) | collective-permute-done | bytes 98336 | tf_op jit(solution)/shard_map/ppermute | solution.py:217
  151.3 1.9 collective-permute-start.17
  153.3 8.8 %collective-permute-done.17.refs_2_ = bf16[2,64,768]{2,1,0:T(8,128)(2,1)S(1)} collective-permute-done((bf16[2,64,768]{2,1,0:T(8,128)(2,1)S(1)}, bf16[2,64,768]{2,1,0:T(8,128)(2,1)S(1)}, u32[]{:S(2)}, u32[]{:S(2)}) %collective-permute-start.17) | collective-permute-done | bytes 196640 | tf_op jit(solution)/shard_map/ppermute | solution.py:217
  163.1 1.9 collective-permute-start.18
  165.0 5.5 %collective-permute-start.13 = (bf16[1,64,768]{2,1,0:T(8,128)(2,1)}, bf16[1,64,768]{2,1,0:T(8,128)(2,1)S(1)}, u32[]{:S(2)}, u32[]{:S(2)}) collective-permute-start(bf16[1,64,768]{2,1,0:T(8,128)(2,1)} %bitcast.45), channel_id=1, source_target_pairs={{0,256},{64,320},{128,384},{192,448},{256,0},{320,64},{384,128},{4... | collective-permute-start | bytes 294920 | tf_op jit(solution)/shard_map/ppermute | solution.py:217
  170.6 4.9 %collective-permute-done.13.refs_1_ = bf16[1,64,768]{2,1,0:T(8,128)(2,1)S(1)} collective-permute-done((bf16[1,64,768]{2,1,0:T(8,128)(2,1)}, bf16[1,64,768]{2,1,0:T(8,128)(2,1)S(1)}, u32[]{:S(2)}, u32[]{:S(2)}) %collective-permute-start.13) | collective-permute-done | bytes 98336 | tf_op jit(solution)/shard_map/ppermute | solution.py:217
  176.4 6.7 %collective-permute-start.14 = (bf16[2,64,768]{2,1,0:T(8,128)(2,1)S(1)}, bf16[2,64,768]{2,1,0:T(8,128)(2,1)S(1)}, u32[]{:S(2)}, u32[]{:S(2)}) collective-permute-start(bf16[2,64,768]{2,1,0:T(8,128)(2,1)S(1)} %pad_maximum_fusion.2), channel_id=1, source_target_pairs={{0,128},{64,192},{128,0},{192,64},{256,384},{320,448},{384,256},{4... | collective-permute-start | bytes 589832 | tf_op jit(solution)/shard_map/ppermute | solution.py:217
  183.9 4.2 %shard_map.109 = (bf16[2,512,512]{2,1,0:T(8,128)(2,1)}, bf16[512,768]{1,0:T(8,128)(2,1)}) custom-call(s32[1]{0:T(128)} %bitcast.1.core_ref, bf16[512,512]{1,0:T(8,128)(2,1)} %get-tuple-element.40.order_ref, bf16[1,64,768]{2,1,0:T(8,128)(2,1)} %bitcast.52, bf16[1,64,768]{2,1,0:T(8,128)(2,1)} %copy-done.5, bf16[2,64,768]{2,1,0:T(8,128)(2,1)} %copy-done.8, ...), custom_call_target="tpu_custom_call" | custom-call | flops 1000000000 | bytes 2883588 | tf_op jit(solution)/shard_map/pallas_call | solution.py:22
  188.1 9.2 %all-to-all-start.3 = ((bf16[32,32,512]{2,1,0:T(8,128)(2,1)}), bf16[32,32,512]{2,1,0:T(8,128)(2,1)S(1)}, u32[]{:S(2)}, u32[]{:S(2)}) async-start(bf16[32,32,512]{2,1,0:T(8,128)(2,1)} %bitcast.44), calls=%async_computation.3 | async-start | bytes 2097152 | tf_op jit(solution)/shard_map/all_to_all | solution.py:267
  197.4 4.3 %collective-permute-start.15 = (bf16[4,64,768]{2,1,0:T(8,128)(2,1)S(1)}, bf16[4,64,768]{2,1,0:T(8,128)(2,1)S(1)}, u32[]{:S(2)}, u32[]{:S(2)}) collective-permute-start(bf16[4,64,768]{2,1,0:T(8,128)(2,1)S(1)} %pad_maximum_fusion), channel_id=1, source_target_pairs={{0,64},{64,0},{128,192},{192,128},{256,320},{320,256},{384,448},{4... | collective-permute-start | bytes 1179656 | tf_op jit(solution)/shard_map/ppermute | solution.py:217
  201.7 9.1 %collective-permute-done.15.refs_3_ = bf16[4,64,768]{2,1,0:T(8,128)(2,1)S(1)} collective-permute-done((bf16[4,64,768]{2,1,0:T(8,128)(2,1)S(1)}, bf16[4,64,768]{2,1,0:T(8,128)(2,1)S(1)}, u32[]{:S(2)}, u32[]{:S(2)}) %collective-permute-start.15) | collective-permute-done | bytes 393248 | tf_op jit(solution)/shard_map/ppermute | solution.py:217
  211.5 4.3 %shard_map.108 = (bf16[2,512,512]{2,1,0:T(8,128)(2,1)}, bf16[512,768]{1,0:T(8,128)(2,1)}) custom-call(s32[1]{0:T(128)} %bitcast.1.core_ref, bf16[512,512]{1,0:T(8,128)(2,1)} %get-tuple-element.40.order_ref, bf16[1,64,768]{2,1,0:T(8,128)(2,1)} %bitcast.47, bf16[1,64,768]{2,1,0:T(8,128)(2,1)} %copy-done.4, bf16[2,64,768]{2,1,0:T(8,128)(2,1)} %copy-done.7, ...), custom_call_target="tpu_custom_call" | custom-call | flops 1000000000 | bytes 2883588 | tf_op jit(solution)/shard_map/pallas_call | solution.py:22
  215.8 4.8 %shard_map.110 = (f32[3,512,256]{2,1,0:T(8,128)}, bf16[3,512,256]{2,1,0:T(8,128)(2,1)}) custom-call(s32[1]{0:T(128)} %bitcast.1.core_ref, bf16[2,512,512]{2,1,0:T(8,128)(2,1)} %bitcast.41, bf16[2,512,512]{2,1,0:T(8,128)(2,1)} %bitcast.43, bf16[512,768]{1,0:T(8,128)(2,1)} %get-tuple-element.45.g0_ref, bf16[512,768]{1,0:T(8,128)(2,1)} %get-tuple-element.46.g1_ref), custom_call_target="tpu_custom_call" | custom-call | flops 1000000000 | bytes 3670020 | tf_op jit(solution)/shard_map/pallas_call | solution.py:22
  220.5 2.7 %collective-permute-start.20 = (bf16[3,512,256]{2,1,0:T(8,128)(2,1)}, bf16[3,512,256]{2,1,0:T(8,128)(2,1)S(1)}, u32[]{:S(2)}, u32[]{:S(2)}) collective-permute-start(bf16[3,512,256]{2,1,0:T(8,128)(2,1)} %get-tuple-element.48), channel_id=1, source_target_pairs={{0,32},{32,0},{1,33},{33,1},{2,34},{34,2},{3,35},{35,3},{4,36},{36... | collective-permute-start | bytes 2359304 | tf_op jit(solution)/shard_map/ppermute | solution.py:217
  223.3 7.2 %all-to-all-start.2 = ((bf16[32,32,512]{2,1,0:T(8,128)(2,1)}), bf16[32,32,512]{2,1,0:T(8,128)(2,1)S(1)}, u32[]{:S(2)}, u32[]{:S(2)}) async-start(bf16[32,32,512]{2,1,0:T(8,128)(2,1)} %bitcast.21), calls=%async_computation.2 | async-start | bytes 2097152 | tf_op jit(solution)/shard_map/all_to_all | solution.py:267
  230.4 2.5 fusion
  233.0 11.8 %collective-permute-start.19 = (bf16[2,32,512]{2,1,0:T(8,128)(2,1)S(1)}, bf16[2,32,512]{2,1,0:T(8,128)(2,1)S(1)}, u32[]{:S(2)}, u32[]{:S(2)}) collective-permute-start(bf16[2,32,512]{2,1,0:T(8,128)(2,1)S(1)} %bitcast_reduce_fusion), channel_id=1, source_target_pairs={{0,1},{1,0},{2,3},{3,2},{4,5},{5,4},{6,7},{7,6},{8,9},{9,8},{10,11... | collective-permute-start | bytes 196616 | tf_op jit(solution)/shard_map/ppermute | solution.py:217
  244.8 2.0 all-to-all-done.2
  (81 shorter events, 12.3 us)
Async XLA Ops:
  0.6 1.0 copy-start
  2.9 27.1 %all-to-all-start = ((bf16[32,32,512]{2,1,0:T(8,128)(2,1)}), bf16[32,32,512]{2,1,0:T(8,128)(2,1)S(1)}, u32[]{:S(2)}, u32[]{:S(2)}) async-start(bf16[32,32,512]{2,1,0:T(8,128)(2,1)} %bitcast.4), calls=%async_computation | async-start | bytes 2097152 | tf_op jit(solution)/shard_map/all_to_all | solution.py:267
  13.5 15.9 %collective-permute-start.4 = (bf16[2,1,32,512]{3,2,0,1:T(8,128)(2,1)S(1)}, bf16[2,1,32,512]{3,2,0,1:T(8,128)(2,1)S(1)}, u32[]{:S(2)}, u32[]{:S(2)}) collective-permute-start(bf16[2,1,32,512]{3,2,0,1:T(8,128)(2,1)S(1)} %bitcast.54), channel_id=1, source_target_pairs={{0,1},{1,0},{2,3},{3,2},{4,5},{5,4},{6,7},{7,6},{8,9},{9,8},{10,11... | collective-permute-start | bytes 196616 | tf_op jit(solution)/shard_map/ppermute | solution.py:217
  27.0 16.9 %collective-permute-start = (bf16[3,512,256]{2,1,0:T(8,128)(2,1)}, bf16[3,512,256]{2,1,0:T(8,128)(2,1)}, u32[]{:S(2)}, u32[]{:S(2)}) collective-permute-start(bf16[3,512,256]{2,1,0:T(8,128)(2,1)} %bitcast.6.own_ref.refs_4_), channel_id=1, source_target_pairs={{0,32},{32,0},{1,33},{33,1},{2,34},{34,2},{3,35},{35,3},{4,36},{36... | collective-permute-start | bytes 2359304 | tf_op jit(solution)/shard_map/ppermute | solution.py:217
  30.0 1.3 copy-start.1
  30.0 8.7 %copy-start.11 = (f32[16,128]{1,0:T(8,128)S(1)}, f32[16,128]{1,0:T(8,128)}, u32[]{:S(2)}) copy-start(f32[16,128]{1,0:T(8,128)} %taps_ref.1) | copy-start | bytes 24580
  30.0 8.8 %copy-start.12 = (f32[16]{0:T(128)S(1)}, f32[16]{0:T(128)}, u32[]{:S(2)}) copy-start(f32[16]{0:T(128)} %param.12) | copy-start | bytes 196
  31.3 23.7 %all-to-all-start.1 = ((bf16[32,32,512]{2,1,0:T(8,128)(2,1)}), bf16[32,32,512]{2,1,0:T(8,128)(2,1)S(1)}, u32[]{:S(2)}, u32[]{:S(2)}) async-start(bf16[32,32,512]{2,1,0:T(8,128)(2,1)} %bitcast.10), calls=%async_computation.1 | async-start | bytes 2097152 | tf_op jit(solution)/shard_map/all_to_all | solution.py:267
  48.5 16.0 %collective-permute-start.1 = (bf16[4,64,768]{2,1,0:T(8,128)(2,1)}, bf16[4,64,768]{2,1,0:T(8,128)(2,1)S(1)}, u32[]{:S(2)}, u32[]{:S(2)}) collective-permute-start(bf16[4,64,768]{2,1,0:T(8,128)(2,1)} %get-tuple-element.30), channel_id=1, source_target_pairs={{0,64},{64,0},{128,192},{192,128},{256,320},{320,256},{384,448},{4... | collective-permute-start | bytes 1179656 | tf_op jit(solution)/shard_map/ppermute | solution.py:217
  54.9 1.0 copy-start.2
  55.9 8.6 %copy-start.6 = (bf16[4,64,768]{2,1,0:T(8,128)(2,1)S(1)}, bf16[4,64,768]{2,1,0:T(8,128)(2,1)}, u32[]{:S(2)}) copy-start(bf16[4,64,768]{2,1,0:T(8,128)(2,1)} %get-tuple-element.29) | copy-start | bytes 1179652
  60.5 16.5 %collective-permute-start.5 = (bf16[4,64,768]{2,1,0:T(8,128)(2,1)}, bf16[4,64,768]{2,1,0:T(8,128)(2,1)S(1)}, u32[]{:S(2)}, u32[]{:S(2)}) collective-permute-start(bf16[4,64,768]{2,1,0:T(8,128)(2,1)} %get-tuple-element.32), channel_id=1, source_target_pairs={{0,64},{64,0},{128,192},{192,128},{256,320},{320,256},{384,448},{4... | collective-permute-start | bytes 1179656 | tf_op jit(solution)/shard_map/ppermute | solution.py:217
  64.6 15.5 %collective-permute-start.2 = (bf16[2,64,768]{2,1,0:T(8,128)(2,1)S(1)}, bf16[2,64,768]{2,1,0:T(8,128)(2,1)S(1)}, u32[]{:S(2)}, u32[]{:S(2)}) collective-permute-start(bf16[2,64,768]{2,1,0:T(8,128)(2,1)S(1)} %get-tuple-element.52), channel_id=1, source_target_pairs={{0,128},{64,192},{128,0},{192,64},{256,384},{320,448},{384,256},{4... | collective-permute-start | bytes 589832 | tf_op jit(solution)/shard_map/ppermute | solution.py:217
  78.1 16.2 %collective-permute-start.6 = (bf16[2,64,768]{2,1,0:T(8,128)(2,1)S(1)}, bf16[2,64,768]{2,1,0:T(8,128)(2,1)S(1)}, u32[]{:S(2)}, u32[]{:S(2)}) collective-permute-start(bf16[2,64,768]{2,1,0:T(8,128)(2,1)S(1)} %get-tuple-element.50), channel_id=1, source_target_pairs={{0,128},{64,192},{128,0},{192,64},{256,384},{320,448},{384,256},{4... | collective-permute-start | bytes 589832 | tf_op jit(solution)/shard_map/ppermute | solution.py:217
  80.1 21.1 %collective-permute-start.3 = (bf16[1,64,768]{2,1,0:T(8,128)(2,1)S(1)}, bf16[1,64,768]{2,1,0:T(8,128)(2,1)S(1)}, u32[]{:S(2)}, u32[]{:S(2)}) collective-permute-start(bf16[1,64,768]{2,1,0:T(8,128)(2,1)S(1)} %add_convert_fusion.9), channel_id=1, source_target_pairs={{0,256},{64,320},{128,384},{192,448},{256,0},{320,64},{384,128},{4... | collective-permute-start | bytes 294920 | tf_op jit(solution)/shard_map/ppermute | solution.py:217
  94.3 15.5 %collective-permute-start.7 = (bf16[1,64,768]{2,1,0:T(8,128)(2,1)S(1)}, bf16[1,64,768]{2,1,0:T(8,128)(2,1)S(1)}, u32[]{:S(2)}, u32[]{:S(2)}) collective-permute-start(bf16[1,64,768]{2,1,0:T(8,128)(2,1)S(1)} %add_convert_fusion.6), channel_id=1, source_target_pairs={{0,256},{64,320},{128,384},{192,448},{256,0},{320,64},{384,128},{4... | collective-permute-start | bytes 294920 | tf_op jit(solution)/shard_map/ppermute | solution.py:217
  101.3 18.6 %copy-start.9 = (bf16[1,64,768]{2,1,0:T(8,128)(2,1)}, bf16[1,64,768]{2,1,0:T(8,128)(2,1)S(1)}, u32[]{:S(2)}) copy-start(bf16[1,64,768]{2,1,0:T(8,128)(2,1)S(1)} %add_convert_fusion.8) | copy-start | bytes 294916
  109.9 10.1 %copy-start.10 = (bf16[1,64,768]{2,1,0:T(8,128)(2,1)}, bf16[1,64,768]{2,1,0:T(8,128)(2,1)S(1)}, u32[]{:S(2)}) copy-start(bf16[1,64,768]{2,1,0:T(8,128)(2,1)S(1)} %add_convert_fusion.5) | copy-start | bytes 294916
  109.9 10.0 %collective-permute-start.8 = (bf16[8,768]{1,0:T(8,128)(2,1)S(1)}, bf16[8,768]{1,0:T(8,128)(2,1)S(1)}, u32[]{:S(2)}, u32[]{:S(2)}) collective-permute-start(bf16[8,768]{1,0:T(8,128)(2,1)S(1)} %fusion.4), channel_id=1, source_target_pairs={{0,32},{32,64},{64,96},{96,128},{128,160},{160,192},{192,224},{224... | collective-permute-start | bytes 36872 | tf_op jit(solution)/shard_map/ppermute | solution.py:223
  111.8 8.1 %collective-permute-start.9 = (bf16[16,768]{1,0:T(8,128)(2,1)S(1)}, bf16[16,768]{1,0:T(8,128)(2,1)S(1)}, u32[]{:S(2)}, u32[]{:S(2)}) collective-permute-start(bf16[16,768]{1,0:T(8,128)(2,1)S(1)} %fusion.1), channel_id=1, source_target_pairs={{32,0},{64,32},{96,64},{128,96},{160,128},{192,160},{224,192},{256... | collective-permute-start | bytes 73736 | tf_op jit(solution)/shard_map/ppermute | solution.py:223
  114.9 5.0 %collective-permute-start.10 = (bf16[16,256]{1,0:T(8,128)(2,1)S(1)}, bf16[16,256]{1,0:T(8,128)(2,1)S(1)}, u32[]{:S(2)}, u32[]{:S(2)}) collective-permute-start(bf16[16,256]{1,0:T(8,128)(2,1)S(1)} %slice_bitcast_fusion), channel_id=1, source_target_pairs={{32,0},{64,32},{96,64},{128,96},{160,128},{192,160},{224,192},{256... | collective-permute-start | bytes 24584 | tf_op jit(solution)/shard_map/ppermute | solution.py:223
  119.9 0.6 copy-start.19
  119.9 0.6 copy-start.18
  119.9 0.6 copy-start.17
  122.6 7.2 %collective-permute-start.12 = (bf16[144,256]{1,0:T(8,128)(2,1)}, bf16[144,256]{1,0:T(8,128)(2,1)S(1)}, u32[]{:S(2)}, u32[]{:S(2)}) collective-permute-start(bf16[144,256]{1,0:T(8,128)(2,1)} %get-tuple-element.34.cg_ref), channel_id=1, source_target_pairs={{32,0},{64,32},{96,64},{128,96},{160,128},{192,160},{224,192},{256... | collective-permute-start | bytes 221192 | tf_op jit(solution)/shard_map/ppermute | solution.py:223
  124.5 5.3 %collective-permute-start.11 = (bf16[128,256]{1,0:T(8,128)(2,1)}, bf16[128,256]{1,0:T(8,128)(2,1)S(1)}, u32[]{:S(2)}, u32[]{:S(2)}) collective-permute-start(bf16[128,256]{1,0:T(8,128)(2,1)} %get-tuple-element.33.prod_ref), channel_id=1, source_target_pairs={{0,32},{32,64},{64,96},{96,128},{128,160},{160,192},{192,224},{224... | collective-permute-start | bytes 196616 | tf_op jit(solution)/shard_map/ppermute | solution.py:223
  129.8 0.6 copy-start.16
  129.8 0.6 copy-start.15
  134.2 16.2 %collective-permute-start.16 = (bf16[1,64,768]{2,1,0:T(8,128)(2,1)}, bf16[1,64,768]{2,1,0:T(8,128)(2,1)S(1)}, u32[]{:S(2)}, u32[]{:S(2)}) collective-permute-start(bf16[1,64,768]{2,1,0:T(8,128)(2,1)} %bitcast.49), channel_id=1, source_target_pairs={{0,256},{64,320},{128,384},{192,448},{256,0},{320,64},{384,128},{4... | collective-permute-start | bytes 294920 | tf_op jit(solution)/shard_map/ppermute | solution.py:217
  150.4 32.8 %copy-start.5 = (bf16[1,64,768]{2,1,0:T(8,128)(2,1)}, bf16[1,64,768]{2,1,0:T(8,128)(2,1)S(1)}, u32[]{:S(2)}) copy-start(bf16[1,64,768]{2,1,0:T(8,128)(2,1)S(1)} %collective-permute-done.16.refs_1_) | copy-start | bytes 294916
  151.3 10.8 %collective-permute-start.17 = (bf16[2,64,768]{2,1,0:T(8,128)(2,1)S(1)}, bf16[2,64,768]{2,1,0:T(8,128)(2,1)S(1)}, u32[]{:S(2)}, u32[]{:S(2)}) collective-permute-start(bf16[2,64,768]{2,1,0:T(8,128)(2,1)S(1)} %pad_maximum_fusion.3), channel_id=1, source_target_pairs={{0,128},{64,192},{128,0},{192,64},{256,384},{320,448},{384,256},{4... | collective-permute-start | bytes 589832 | tf_op jit(solution)/shard_map/ppermute | solution.py:217
  162.1 21.1 %copy-start.8 = (bf16[2,64,768]{2,1,0:T(8,128)(2,1)}, bf16[2,64,768]{2,1,0:T(8,128)(2,1)S(1)}, u32[]{:S(2)}) copy-start(bf16[2,64,768]{2,1,0:T(8,128)(2,1)S(1)} %collective-permute-done.17.refs_2_) | copy-start | bytes 589828
  163.1 20.0 %collective-permute-start.18 = (bf16[4,64,768]{2,1,0:T(8,128)(2,1)S(1)}, bf16[4,64,768]{2,1,0:T(8,128)(2,1)S(1)}, u32[]{:S(2)}, u32[]{:S(2)}) collective-permute-start(bf16[4,64,768]{2,1,0:T(8,128)(2,1)S(1)} %pad_maximum_fusion.1), channel_id=1, source_target_pairs={{0,64},{64,0},{128,192},{192,128},{256,320},{320,256},{384,448},{4... | collective-permute-start | bytes 1179656 | tf_op jit(solution)/shard_map/ppermute | solution.py:217
  165.0 10.5 %collective-permute-start.13 = (bf16[1,64,768]{2,1,0:T(8,128)(2,1)}, bf16[1,64,768]{2,1,0:T(8,128)(2,1)S(1)}, u32[]{:S(2)}, u32[]{:S(2)}) collective-permute-start(bf16[1,64,768]{2,1,0:T(8,128)(2,1)} %bitcast.45), channel_id=1, source_target_pairs={{0,256},{64,320},{128,384},{192,448},{256,0},{320,64},{384,128},{4... | collective-permute-start | bytes 294920 | tf_op jit(solution)/shard_map/ppermute | solution.py:217
  175.5 21.9 %copy-start.4 = (bf16[1,64,768]{2,1,0:T(8,128)(2,1)}, bf16[1,64,768]{2,1,0:T(8,128)(2,1)S(1)}, u32[]{:S(2)}) copy-start(bf16[1,64,768]{2,1,0:T(8,128)(2,1)S(1)} %collective-permute-done.13.refs_1_) | copy-start | bytes 294916
  176.4 20.9 %collective-permute-start.14 = (bf16[2,64,768]{2,1,0:T(8,128)(2,1)S(1)}, bf16[2,64,768]{2,1,0:T(8,128)(2,1)S(1)}, u32[]{:S(2)}, u32[]{:S(2)}) collective-permute-start(bf16[2,64,768]{2,1,0:T(8,128)(2,1)S(1)} %pad_maximum_fusion.2), channel_id=1, source_target_pairs={{0,128},{64,192},{128,0},{192,64},{256,384},{320,448},{384,256},{4... | collective-permute-start | bytes 589832 | tf_op jit(solution)/shard_map/ppermute | solution.py:217
  183.1 0.7 copy-start.13
  188.1 9.2 %copy-start.3 = (bf16[64,768]{1,0:T(8,128)(2,1)S(1)}, bf16[64,768]{1,0:T(8,128)(2,1)}, u32[]{:S(2)}) copy-start(bf16[64,768]{1,0:T(8,128)(2,1)} %get-tuple-element.41) | copy-start | bytes 294916
  188.1 35.1 %all-to-all-start.3 = ((bf16[32,32,512]{2,1,0:T(8,128)(2,1)}), bf16[32,32,512]{2,1,0:T(8,128)(2,1)S(1)}, u32[]{:S(2)}, u32[]{:S(2)}) async-start(bf16[32,32,512]{2,1,0:T(8,128)(2,1)} %bitcast.44), calls=%async_computation.3 | async-start | bytes 2097152 | tf_op jit(solution)/shard_map/all_to_all | solution.py:267
  197.4 13.4 %copy-start.7 = (bf16[2,64,768]{2,1,0:T(8,128)(2,1)}, bf16[2,64,768]{2,1,0:T(8,128)(2,1)S(1)}, u32[]{:S(2)}) copy-start(bf16[2,64,768]{2,1,0:T(8,128)(2,1)S(1)} %collective-permute-done.14.refs_2_) | copy-start | bytes 589828
  197.4 13.3 %collective-permute-start.15 = (bf16[4,64,768]{2,1,0:T(8,128)(2,1)S(1)}, bf16[4,64,768]{2,1,0:T(8,128)(2,1)S(1)}, u32[]{:S(2)}, u32[]{:S(2)}) collective-permute-start(bf16[4,64,768]{2,1,0:T(8,128)(2,1)S(1)} %pad_maximum_fusion), channel_id=1, source_target_pairs={{0,64},{64,0},{128,192},{192,128},{256,320},{320,256},{384,448},{4... | collective-permute-start | bytes 1179656 | tf_op jit(solution)/shard_map/ppermute | solution.py:217
  210.8 0.8 copy-start.14
  220.5 9.9 %collective-permute-start.20 = (bf16[3,512,256]{2,1,0:T(8,128)(2,1)}, bf16[3,512,256]{2,1,0:T(8,128)(2,1)S(1)}, u32[]{:S(2)}, u32[]{:S(2)}) collective-permute-start(bf16[3,512,256]{2,1,0:T(8,128)(2,1)} %get-tuple-element.48), channel_id=1, source_target_pairs={{0,32},{32,0},{1,33},{33,1},{2,34},{34,2},{3,35},{35,3},{4,36},{36... | collective-permute-start | bytes 2359304 | tf_op jit(solution)/shard_map/ppermute | solution.py:217
  223.3 23.5 %all-to-all-start.2 = ((bf16[32,32,512]{2,1,0:T(8,128)(2,1)}), bf16[32,32,512]{2,1,0:T(8,128)(2,1)S(1)}, u32[]{:S(2)}, u32[]{:S(2)}) async-start(bf16[32,32,512]{2,1,0:T(8,128)(2,1)} %bitcast.21), calls=%async_computation.2 | async-start | bytes 2097152 | tf_op jit(solution)/shard_map/all_to_all | solution.py:267
  233.0 14.0 %collective-permute-start.19 = (bf16[2,32,512]{2,1,0:T(8,128)(2,1)S(1)}, bf16[2,32,512]{2,1,0:T(8,128)(2,1)S(1)}, u32[]{:S(2)}, u32[]{:S(2)}) collective-permute-start(bf16[2,32,512]{2,1,0:T(8,128)(2,1)S(1)} %bitcast_reduce_fusion), channel_id=1, source_target_pairs={{0,1},{1,0},{2,3},{3,2},{4,5},{5,4},{6,7},{7,6},{8,9},{9,8},{10,11... | collective-permute-start | bytes 196616 | tf_op jit(solution)/shard_map/ppermute | solution.py:217

commit v5 on v4

--- a/solution.py
+++ b/solution.py
@@ -73,9 +73,12 @@
     return jnp.where(c == relative * (count // 2) + piece * tokens + token, 1.0, 0.0).astype(BF16)
 
 
-def prepare_body(pieces, members, taps_ref, rev_ref, decay_ref, fwd_ref, bwd_ref, turn_ref, unturn_ref):
-    tokens = turn_ref.shape[0] // (pieces * members)
-    turn_ref[...] = row_order(pieces, members, tokens, False)
+def prepare_body(pieces, members, taps_ref, rev_ref, decay_ref, fwd_ref, bwd_ref, keep_ref, send_ref, unturn_ref):
+    rows = unturn_ref.shape[0]
+    tokens = rows // (pieces * members)
+    turn = row_order(pieces, members, tokens, False)
+    keep_ref[...] = turn[: rows // 2]
+    send_ref[...] = turn[rows // 2 :]
     unturn_ref[...] = row_order(pieces, members, tokens, True)
     filters, taps = taps_ref.shape
     lag = lax.broadcasted_iota(jnp.int32, (1, taps), 1)
@@ -93,19 +96,16 @@
             ref[rows, taps:] = jnp.where(near, 0.0, ring).astype(BF16)
 
 
-def project_body(members, core_ref, order_ref, x_ref, own_ref, peer_ref, keep_ref, send_ref):
+def project_body(core_ref, order_ref, x_ref, own_ref, peer_ref, out_ref):
     core = core_ref[0]
-    rows = x_ref.shape[1]
+    members, rows, _ = out_ref.shape
     order = order_ref[...]
     mine = dot(order, x_ref[core]).astype(BF16)
     theirs = dot(order, x_ref[1 - core]).astype(BF16)
     streams, _, channels = own_ref.shape
-    half = rows // 2
     for i in range(streams):
-        cols = slice(i * channels, (i + 1) * channels)
         part = (dot(mine, own_ref[i]) + dot(theirs, peer_ref[i])).astype(BF16)
-        keep_ref[:, :, cols] = part[:half].reshape(members // 2, rows // members, channels)
-        send_ref[:, :, cols] = part[half:].reshape(members // 2, rows // members, channels)
+        out_ref[:, :, i * channels : (i + 1) * channels] = part.reshape(members, rows, channels)
 
 
 def back_body(core_ref, order_ref, *refs):
@@ -275,24 +275,27 @@
     after = shifted(upstream[:16], -1)
     far = swap(local, "zh", 1)
     w_own = featurizer.transpose(1, 0, 2)
-    w_peer = swap(w_own, "core")
+    w_peer = swap(w_own, "core", 1)
     rolled = jnp.roll(long_filter[:, ::-1], 1, axis=1)
     matrix = shape((long_filter.shape[0] * count, 2 * count), BF16)
+    oblong = shape((pieces * lines // 2, pieces * lines), BF16)
     square = shape((pieces * lines, pieces * lines), BF16)
-    t_fwd, t_bwd, turn, unturn = call(
+    t_fwd, t_bwd, turn_keep, turn_send, unturn = call(
         functools.partial(prepare_body, pieces, members),
-        (matrix, matrix, square, square),
+        (matrix, matrix, oblong, oblong, square),
         long_filter, rolled, decay_rate[:, None],
     )
 
-    project = functools.partial(project_body, members)
-    part_shape = (shape((members // 2, pieces * tokens, wide), BF16),) * 2
-    parts = call(project, part_shape, here, turn, x_near, w_own, w_peer)
-    f_near = line_scatter(*parts)
+    part_shape = shape((members // 2, pieces * tokens, wide), BF16)
+
+    def project(x):
+        send = call(project_body, part_shape, here, turn_send, x, w_own, w_peer)
+        keep = call(project_body, part_shape, here, turn_keep, x, w_own, w_peer)
+        return line_scatter(keep, send)
+
+    f_near = project(x_near)
     x_far = spread(far)
-    parts = call(project, part_shape, here, turn, x_far, w_own, w_peer)
-    f_far = line_scatter(*parts)
-
+    f_far = project(x_far)
     tail = shifted(jnp.where(zh == 1, f_near[-8:], f_far[-8:]), 1)
     head = shifted(jnp.where(zh == 0, f_near[:16], f_far[:16]), -1)
     plane = shape((count, channels), F32)

time: 252 us -> 255 us (1.012)
  Pallas kernels: 32 us -> 37.2 us
  starting transfers between devices: 127 us -> 123 us
    pallas_call x8 -> x10, Pallas kernels: 32 us -> 37.2 us  [call(): pl.pallas_call(body, out_shape=outs, in_specs=[scalar if a.shape == (1,)...]
    all_to_all x4, starting transfers between devices: 34.2 us -> 31.3 us  [exchange(): lax.all_to_all(x.reshape(2 * pieces, lines, rows), ('core', 'x', 'y'), 0,...]
  transfers between devices with their start and end apart: 25 -> 25, of which waited for: 13 -> 13; matrix products, arithmetic and copies ran while one was open for 3% -> 3% of each run, Pallas kernels for 11% -> 13%
where the time goes in v5:
time: 255 us; the launch traced here: 251 us
  starting transfers between devices  123 us (48%)
  waiting for transfers between devices  71.8 us (28%)
  Pallas kernels  37.2 us (15%)
  local copies, waits for them, and re-layouts  8.75 us (3%)
  other arithmetic  8.56 us (3%)
    ppermute x16, starting transfers between devices, swap(): lax.ppermute(x, axis, [(i, i ^ by) for i in range(lax.axis_size(axis))])  79.4 us
    ppermute x16, waiting for transfers between devices, swap(): lax.ppermute(x, axis, [(i, i ^ by) for i in range(lax.axis_size(axis))])  62.3 us
    pallas_call x10, Pallas kernels, call(): pl.pallas_call(body, out_shape=outs, in_specs=[scalar if a.shape == (1,)...  37.2 us
    all_to_all x4, starting transfers between devices, exchange(): lax.all_to_all(x.reshape(2 * pieces, lines, rows), ('core', 'x', 'y'), 0,...  31.3 us
    ppermute x5, starting transfers between devices, shifted(): lax.ppermute(x, axis, [(i, i + by) for i in range(count) if 0 <= i + by <...  12 us
  transfers between devices with their start and end apart: 25, of which 13 were waited for; matrix products, arithmetic and copies ran while one was open for 3% of the time, Pallas kernels for 13%

profile of v5, /device:TPU:1, one launch (start us, length us, event | category | flops | bytes accessed | tf_op | source)
XLA Modules:
  0.0 251.3 jit_solution(5839848213280849443)
XLA Ops:
  1.8 1.1 broadcast_in_dim.32
  2.9 10.5 %all-to-all-start = ((bf16[32,32,512]{2,1,0:T(8,128)(2,1)}), bf16[32,32,512]{2,1,0:T(8,128)(2,1)S(1)}, u32[]{:S(2)}, u32[]{:S(2)}) async-start(bf16[32,32,512]{2,1,0:T(8,128)(2,1)} %bitcast.4), calls=%async_computation | async-start | bytes 2097152 | tf_op jit(solution)/shard_map/all_to_all | solution.py:267
  13.5 13.5 %collective-permute-start.4 = (bf16[2,1,32,512]{3,2,0,1:T(8,128)(2,1)S(1)}, bf16[2,1,32,512]{3,2,0,1:T(8,128)(2,1)S(1)}, u32[]{:S(2)}, u32[]{:S(2)}) collective-permute-start(bf16[2,1,32,512]{3,2,0,1:T(8,128)(2,1)S(1)} %bitcast.56), channel_id=1, source_target_pairs={{0,1},{1,0},{2,3},{3,2},{4,5},{5,4},{6,7},{7,6},{8,9},{9,8},{10,11... | collective-permute-start | bytes 196616 | tf_op jit(solution)/shard_map/ppermute | solution.py:217
  27.0 2.2 collective-permute-done.4
  31.3 7.4 %all-to-all-start.1 = ((bf16[32,32,512]{2,1,0:T(8,128)(2,1)}), bf16[32,32,512]{2,1,0:T(8,128)(2,1)S(1)}, u32[]{:S(2)}, u32[]{:S(2)}) async-start(bf16[32,32,512]{2,1,0:T(8,128)(2,1)} %bitcast.10), calls=%async_computation.1 | async-start | bytes 2097152 | tf_op jit(solution)/shard_map/all_to_all | solution.py:267
  38.7 2.1 collective-permute-start
  42.3 3.7 %shard_map.103 = (bf16[2048,256]{1,0:T(8,128)(2,1)}, bf16[2048,256]{1,0:T(8,128)(2,1)}, bf16[256,512]{1,0:T(8,128)(2,1)}, bf16[256,512]{1,0:T(8,128)(2,1)}, bf16[512,512]{1,0:T(8,128)(2,1)}) custom-call(f32[16,128]{1,0:T(8,128)} %taps_ref.1, f32[16,128]{1,0:T(8,128)} %pad_maximum_fusion.4.rev_ref, f32[16,1]{1,0:T(8,128)} %copy.12.decay_ref), custom_call_target="tpu_custom_call" | custom-call | flops 1000000000 | bytes 16448 | tf_op jit(solution)/shard_map/pallas_call | solution.py:22
  46.9 3.6 %shard_map.105 = bf16[4,64,768]{2,1,0:T(8,128)(2,1)} custom-call(s32[1]{0:T(128)} %bitcast.1.core_ref, bf16[256,512]{1,0:T(8,128)(2,1)} %get-tuple-element.26.order_ref, bf16[2,512,512]{2,1,0:T(8,128)(2,1)} %bitcast.40, bf16[3,512,256]{2,1,0:T(8,128)(2,1)} %bitcast.66, bf16[3,512,256]{2,1,0:T(8,128)(2,1)} %copy-done.14), custom_call_target="tpu_custom_call" | custom-call | flops 1000000000 | bytes 2883588 | tf_op jit(solution)/shard_map/pallas_call | solution.py:22
  50.6 3.9 %collective-permute-start.1 = (bf16[4,64,768]{2,1,0:T(8,128)(2,1)}, bf16[4,64,768]{2,1,0:T(8,128)(2,1)S(1)}, u32[]{:S(2)}, u32[]{:S(2)}) collective-permute-start(bf16[4,64,768]{2,1,0:T(8,128)(2,1)} %shard_map.105), channel_id=1, source_target_pairs={{0,64},{64,0},{128,192},{192,128},{256,320},{320,256},{384,448},{4... | collective-permute-start | bytes 1179656 | tf_op jit(solution)/shard_map/ppermute | solution.py:217
  55.9 3.6 %shard_map.107 = bf16[4,64,768]{2,1,0:T(8,128)(2,1)} custom-call(s32[1]{0:T(128)} %bitcast.1.core_ref, bf16[256,512]{1,0:T(8,128)(2,1)} %get-tuple-element.26.order_ref, bf16[2,512,512]{2,1,0:T(8,128)(2,1)} %bitcast.43, bf16[3,512,256]{2,1,0:T(8,128)(2,1)} %bitcast.67, bf16[3,512,256]{2,1,0:T(8,128)(2,1)} %copy-done.14), custom_call_target="tpu_custom_call" | custom-call | flops 1000000000 | bytes 2883588 | tf_op jit(solution)/shard_map/pallas_call | solution.py:22
  59.5 3.9 %collective-permute-start.5 = (bf16[4,64,768]{2,1,0:T(8,128)(2,1)}, bf16[4,64,768]{2,1,0:T(8,128)(2,1)S(1)}, u32[]{:S(2)}, u32[]{:S(2)}) collective-permute-start(bf16[4,64,768]{2,1,0:T(8,128)(2,1)} %shard_map.107), channel_id=1, source_target_pairs={{0,64},{64,0},{128,192},{192,128},{256,320},{320,256},{384,448},{4... | collective-permute-start | bytes 1179656 | tf_op jit(solution)/shard_map/ppermute | solution.py:217
  63.5 3.6 %shard_map.104 = bf16[4,64,768]{2,1,0:T(8,128)(2,1)} custom-call(s32[1]{0:T(128)} %bitcast.1.core_ref, bf16[256,512]{1,0:T(8,128)(2,1)} %get-tuple-element.25.order_ref, bf16[2,512,512]{2,1,0:T(8,128)(2,1)} %bitcast.41, bf16[3,512,256]{2,1,0:T(8,128)(2,1)} %bitcast.68, bf16[3,512,256]{2,1,0:T(8,128)(2,1)} %copy-done.14), custom_call_target="tpu_custom_call" | custom-call | flops 1000000000 | bytes 2883588 | tf_op jit(solution)/shard_map/pallas_call | solution.py:22
  67.1 3.7 %shard_map.106 = bf16[4,64,768]{2,1,0:T(8,128)(2,1)} custom-call(s32[1]{0:T(128)} %bitcast.1.core_ref, bf16[256,512]{1,0:T(8,128)(2,1)} %get-tuple-element.25.order_ref, bf16[2,512,512]{2,1,0:T(8,128)(2,1)} %bitcast.44, bf16[3,512,256]{2,1,0:T(8,128)(2,1)} %bitcast.69, bf16[3,512,256]{2,1,0:T(8,128)(2,1)} %copy-done.14), custom_call_target="tpu_custom_call" | custom-call | flops 1000000000 | bytes 2883588 | tf_op jit(solution)/shard_map/pallas_call | solution.py:22
  70.8 2.5 collective-permute-start.2
  73.3 1.1 add_convert_fusion.2
  74.5 3.7 %collective-permute-start.6 = (bf16[2,64,768]{2,1,0:T(8,128)(2,1)S(1)}, bf16[2,64,768]{2,1,0:T(8,128)(2,1)S(1)}, u32[]{:S(2)}, u32[]{:S(2)}) collective-permute-start(bf16[2,64,768]{2,1,0:T(8,128)(2,1)S(1)} %get-tuple-element.44), channel_id=1, source_target_pairs={{0,128},{64,192},{128,0},{192,64},{256,384},{320,448},{384,256},{4... | collective-permute-start | bytes 589832 | tf_op jit(solution)/shard_map/ppermute | solution.py:217
  78.2 10.4 %collective-permute-done.2 = bf16[2,64,768]{2,1,0:T(8,128)(2,1)S(1)} collective-permute-done((bf16[2,64,768]{2,1,0:T(8,128)(2,1)S(1)}, bf16[2,64,768]{2,1,0:T(8,128)(2,1)S(1)}, u32[]{:S(2)}, u32[]{:S(2)}) %collective-permute-start.2) | collective-permute-done | bytes 196640 | tf_op jit(solution)/shard_map/ppermute | solution.py:217
  88.6 6.3 %collective-permute-start.3 = (bf16[1,64,768]{2,1,0:T(8,128)(2,1)S(1)}, bf16[1,64,768]{2,1,0:T(8,128)(2,1)S(1)}, u32[]{:S(2)}, u32[]{:S(2)}) collective-permute-start(bf16[1,64,768]{2,1,0:T(8,128)(2,1)S(1)} %add_convert_fusion.9), channel_id=1, source_target_pairs={{0,256},{64,320},{128,384},{192,448},{256,0},{320,64},{384,128},{4... | collective-permute-start | bytes 294920 | tf_op jit(solution)/shard_map/ppermute | solution.py:217
  95.0 4.2 %collective-permute-start.7 = (bf16[1,64,768]{2,1,0:T(8,128)(2,1)S(1)}, bf16[1,64,768]{2,1,0:T(8,128)(2,1)S(1)}, u32[]{:S(2)}, u32[]{:S(2)}) collective-permute-start(bf16[1,64,768]{2,1,0:T(8,128)(2,1)S(1)} %add_convert_fusion.6), channel_id=1, source_target_pairs={{0,256},{64,320},{128,384},{192,448},{256,0},{320,64},{384,128},{4... | collective-permute-start | bytes 294920 | tf_op jit(solution)/shard_map/ppermute | solution.py:217
  99.2 13.7 %collective-permute-done.7 = bf16[1,64,768]{2,1,0:T(8,128)(2,1)S(1)} collective-permute-done((bf16[1,64,768]{2,1,0:T(8,128)(2,1)S(1)}, bf16[1,64,768]{2,1,0:T(8,128)(2,1)S(1)}, u32[]{:S(2)}, u32[]{:S(2)}) %collective-permute-start.7) | collective-permute-done | bytes 98336 | tf_op jit(solution)/shard_map/ppermute | solution.py:217
  113.0 1.9 collective-permute-start.8
  114.9 2.7 %collective-permute-start.9 = (bf16[16,768]{1,0:T(8,128)(2,1)S(1)}, bf16[16,768]{1,0:T(8,128)(2,1)S(1)}, u32[]{:S(2)}, u32[]{:S(2)}) collective-permute-start(bf16[16,768]{1,0:T(8,128)(2,1)S(1)} %fusion.1), channel_id=1, source_target_pairs={{32,0},{64,32},{96,64},{128,96},{160,128},{192,160},{224,192},{256... | collective-permute-start | bytes 73736 | tf_op jit(solution)/shard_map/ppermute | solution.py:223
  118.3 1.9 collective-permute-start.10
  120.2 3.0 %collective-permute-done.10.after_ref = bf16[16,256]{1,0:T(8,128)(2,1)S(1)} collective-permute-done((bf16[16,256]{1,0:T(8,128)(2,1)S(1)}, bf16[16,256]{1,0:T(8,128)(2,1)S(1)}, u32[]{:S(2)}, u32[]{:S(2)}) %collective-permute-start.10) | collective-permute-done | bytes 8224 | tf_op jit(solution)/shard_map/ppermute | solution.py:223
  123.9 2.1 shard_map.108
  125.9 1.9 collective-permute-start.12
  127.8 3.6 %collective-permute-start.11 = (bf16[128,256]{1,0:T(8,128)(2,1)}, bf16[128,256]{1,0:T(8,128)(2,1)S(1)}, u32[]{:S(2)}, u32[]{:S(2)}) collective-permute-start(bf16[128,256]{1,0:T(8,128)(2,1)} %get-tuple-element.27.prod_ref), channel_id=1, source_target_pairs={{0,32},{32,64},{64,96},{96,128},{128,160},{160,192},{192,224},{224... | collective-permute-start | bytes 196616 | tf_op jit(solution)/shard_map/ppermute | solution.py:223
  131.5 1.6 collective-permute-done.11.prev_ref
  133.8 3.7 %shard_map.109 = (bf16[128,256]{1,0:T(8,128)(2,1)}, bf16[64,768]{1,0:T(8,128)(2,1)}, bf16[64,768]{1,0:T(8,128)(2,1)}) custom-call(bf16[2048,256]{1,0:T(8,128)(2,1)} %get-tuple-element.23.fwd_ref, bf16[2048,256]{1,0:T(8,128)(2,1)} %get-tuple-element.24.bwd_ref, bf16[128,256]{1,0:T(8,128)(2,1)} %get-tuple-element.27.prod_ref, bf16[128,256]{1,0:T(8,128)(2,1)} %copy-done.18, ...), custom_call_target="tpu_custom_call" | custom-call | flops 1000000000 | bytes 2902020 | tf_op jit(solution)/shard_map/pallas_call | solution.py:22
  137.5 4.4 %collective-permute-start.16 = (bf16[1,64,768]{2,1,0:T(8,128)(2,1)}, bf16[1,64,768]{2,1,0:T(8,128)(2,1)S(1)}, u32[]{:S(2)}, u32[]{:S(2)}) collective-permute-start(bf16[1,64,768]{2,1,0:T(8,128)(2,1)} %bitcast.51), channel_id=1, source_target_pairs={{0,256},{64,320},{128,384},{192,448},{256,0},{320,64},{384,128},{4... | collective-permute-start | bytes 294920 | tf_op jit(solution)/shard_map/ppermute | solution.py:217
  141.9 11.0 %collective-permute-done.16.refs_1_ = bf16[1,64,768]{2,1,0:T(8,128)(2,1)S(1)} collective-permute-done((bf16[1,64,768]{2,1,0:T(8,128)(2,1)}, bf16[1,64,768]{2,1,0:T(8,128)(2,1)S(1)}, u32[]{:S(2)}, u32[]{:S(2)}) %collective-permute-start.16) | collective-permute-done | bytes 98336 | tf_op jit(solution)/shard_map/ppermute | solution.py:217
  153.8 1.9 collective-permute-start.17
  155.8 10.7 %collective-permute-done.17.refs_2_ = bf16[2,64,768]{2,1,0:T(8,128)(2,1)S(1)} collective-permute-done((bf16[2,64,768]{2,1,0:T(8,128)(2,1)S(1)}, bf16[2,64,768]{2,1,0:T(8,128)(2,1)S(1)}, u32[]{:S(2)}, u32[]{:S(2)}) %collective-permute-start.17) | collective-permute-done | bytes 196640 | tf_op jit(solution)/shard_map/ppermute | solution.py:217
  167.5 1.9 collective-permute-start.18
  169.4 5.4 %collective-permute-start.13 = (bf16[1,64,768]{2,1,0:T(8,128)(2,1)}, bf16[1,64,768]{2,1,0:T(8,128)(2,1)S(1)}, u32[]{:S(2)}, u32[]{:S(2)}) collective-permute-start(bf16[1,64,768]{2,1,0:T(8,128)(2,1)} %bitcast.47), channel_id=1, source_target_pairs={{0,256},{64,320},{128,384},{192,448},{256,0},{320,64},{384,128},{4... | collective-permute-start | bytes 294920 | tf_op jit(solution)/shard_map/ppermute | solution.py:217
  174.8 5.1 %collective-permute-done.13.refs_1_ = bf16[1,64,768]{2,1,0:T(8,128)(2,1)S(1)} collective-permute-done((bf16[1,64,768]{2,1,0:T(8,128)(2,1)}, bf16[1,64,768]{2,1,0:T(8,128)(2,1)S(1)}, u32[]{:S(2)}, u32[]{:S(2)}) %collective-permute-start.13) | collective-permute-done | bytes 98336 | tf_op jit(solution)/shard_map/ppermute | solution.py:217
  180.8 8.2 %collective-permute-start.14 = (bf16[2,64,768]{2,1,0:T(8,128)(2,1)S(1)}, bf16[2,64,768]{2,1,0:T(8,128)(2,1)S(1)}, u32[]{:S(2)}, u32[]{:S(2)}) collective-permute-start(bf16[2,64,768]{2,1,0:T(8,128)(2,1)S(1)} %pad_maximum_fusion.2), channel_id=1, source_target_pairs={{0,128},{64,192},{128,0},{192,64},{256,384},{320,448},{384,256},{4... | collective-permute-start | bytes 589832 | tf_op jit(solution)/shard_map/ppermute | solution.py:217
  189.8 4.2 %shard_map.111 = (bf16[2,512,512]{2,1,0:T(8,128)(2,1)}, bf16[512,768]{1,0:T(8,128)(2,1)}) custom-call(s32[1]{0:T(128)} %bitcast.1.core_ref, bf16[512,512]{1,0:T(8,128)(2,1)} %get-tuple-element.34.order_ref, bf16[1,64,768]{2,1,0:T(8,128)(2,1)} %bitcast.54, bf16[1,64,768]{2,1,0:T(8,128)(2,1)} %copy-done.5, bf16[2,64,768]{2,1,0:T(8,128)(2,1)} %copy-done.8, ...), custom_call_target="tpu_custom_call" | custom-call | flops 1000000000 | bytes 2883588 | tf_op jit(solution)/shard_map/pallas_call | solution.py:22
  194.1 6.2 %all-to-all-start.3 = ((bf16[32,32,512]{2,1,0:T(8,128)(2,1)}), bf16[32,32,512]{2,1,0:T(8,128)(2,1)S(1)}, u32[]{:S(2)}, u32[]{:S(2)}) async-start(bf16[32,32,512]{2,1,0:T(8,128)(2,1)} %bitcast.46), calls=%async_computation.3 | async-start | bytes 2097152 | tf_op jit(solution)/shard_map/all_to_all | solution.py:267
  200.4 4.6 %collective-permute-start.15 = (bf16[4,64,768]{2,1,0:T(8,128)(2,1)S(1)}, bf16[4,64,768]{2,1,0:T(8,128)(2,1)S(1)}, u32[]{:S(2)}, u32[]{:S(2)}) collective-permute-start(bf16[4,64,768]{2,1,0:T(8,128)(2,1)S(1)} %pad_maximum_fusion), channel_id=1, source_target_pairs={{0,64},{64,0},{128,192},{192,128},{256,320},{320,256},{384,448},{4... | collective-permute-start | bytes 1179656 | tf_op jit(solution)/shard_map/ppermute | solution.py:217
  205.0 9.1 %collective-permute-done.15.refs_3_ = bf16[4,64,768]{2,1,0:T(8,128)(2,1)S(1)} collective-permute-done((bf16[4,64,768]{2,1,0:T(8,128)(2,1)S(1)}, bf16[4,64,768]{2,1,0:T(8,128)(2,1)S(1)}, u32[]{:S(2)}, u32[]{:S(2)}) %collective-permute-start.15) | collective-permute-done | bytes 393248 | tf_op jit(solution)/shard_map/ppermute | solution.py:217
  214.8 4.3 %shard_map.110 = (bf16[2,512,512]{2,1,0:T(8,128)(2,1)}, bf16[512,768]{1,0:T(8,128)(2,1)}) custom-call(s32[1]{0:T(128)} %bitcast.1.core_ref, bf16[512,512]{1,0:T(8,128)(2,1)} %get-tuple-element.34.order_ref, bf16[1,64,768]{2,1,0:T(8,128)(2,1)} %bitcast.49, bf16[1,64,768]{2,1,0:T(8,128)(2,1)} %copy-done.4, bf16[2,64,768]{2,1,0:T(8,128)(2,1)} %copy-done.7, ...), custom_call_target="tpu_custom_call" | custom-call | flops 1000000000 | bytes 2883588 | tf_op jit(solution)/shard_map/pallas_call | solution.py:22
  219.1 4.7 %shard_map.112 = (f32[3,512,256]{2,1,0:T(8,128)}, bf16[3,512,256]{2,1,0:T(8,128)(2,1)}) custom-call(s32[1]{0:T(128)} %bitcast.1.core_ref, bf16[2,512,512]{2,1,0:T(8,128)(2,1)} %bitcast.42, bf16[2,512,512]{2,1,0:T(8,128)(2,1)} %bitcast.45, bf16[512,768]{1,0:T(8,128)(2,1)} %get-tuple-element.39.g0_ref, bf16[512,768]{1,0:T(8,128)(2,1)} %get-tuple-element.40.g1_ref), custom_call_target="tpu_custom_call" | custom-call | flops 1000000000 | bytes 3670020 | tf_op jit(solution)/shard_map/pallas_call | solution.py:22
  223.8 2.7 %collective-permute-start.20 = (bf16[3,512,256]{2,1,0:T(8,128)(2,1)}, bf16[3,512,256]{2,1,0:T(8,128)(2,1)S(1)}, u32[]{:S(2)}, u32[]{:S(2)}) collective-permute-start(bf16[3,512,256]{2,1,0:T(8,128)(2,1)} %get-tuple-element.42), channel_id=1, source_target_pairs={{0,32},{32,0},{1,33},{33,1},{2,34},{34,2},{3,35},{35,3},{4,36},{36... | collective-permute-start | bytes 2359304 | tf_op jit(solution)/shard_map/ppermute | solution.py:217
  226.5 7.2 %all-to-all-start.2 = ((bf16[32,32,512]{2,1,0:T(8,128)(2,1)}), bf16[32,32,512]{2,1,0:T(8,128)(2,1)S(1)}, u32[]{:S(2)}, u32[]{:S(2)}) async-start(bf16[32,32,512]{2,1,0:T(8,128)(2,1)} %bitcast.21), calls=%async_computation.2 | async-start | bytes 2097152 | tf_op jit(solution)/shard_map/all_to_all | solution.py:267
  233.7 2.5 fusion
  236.4 10.1 %collective-permute-start.19 = (bf16[2,32,512]{2,1,0:T(8,128)(2,1)S(1)}, bf16[2,32,512]{2,1,0:T(8,128)(2,1)S(1)}, u32[]{:S(2)}, u32[]{:S(2)}) collective-permute-start(bf16[2,32,512]{2,1,0:T(8,128)(2,1)S(1)} %bitcast_reduce_fusion), channel_id=1, source_target_pairs={{0,1},{1,0},{2,3},{3,2},{4,5},{5,4},{6,7},{7,6},{8,9},{9,8},{10,11... | collective-permute-start | bytes 196616 | tf_op jit(solution)/shard_map/ppermute | solution.py:217
  246.5 3.6 %all-to-all-done.2 = bf16[32,32,512]{2,1,0:T(8,128)(2,1)S(1)} async-done(((bf16[32,32,512]{2,1,0:T(8,128)(2,1)}), bf16[32,32,512]{2,1,0:T(8,128)(2,1)S(1)}, u32[]{:S(2)}, u32[]{:S(2)}) %all-to-all-start.2) | async-done | bytes 1048608 | tf_op jit(solution)/shard_map/all_to_all | solution.py:267
  (87 shorter events, 15.1 us)
Async XLA Ops:
  0.6 1.0 copy-start
  2.9 27.1 %all-to-all-start = ((bf16[32,32,512]{2,1,0:T(8,128)(2,1)}), bf16[32,32,512]{2,1,0:T(8,128)(2,1)S(1)}, u32[]{:S(2)}, u32[]{:S(2)}) async-start(bf16[32,32,512]{2,1,0:T(8,128)(2,1)} %bitcast.4), calls=%async_computation | async-start | bytes 2097152 | tf_op jit(solution)/shard_map/all_to_all | solution.py:267
  13.5 15.7 %collective-permute-start.4 = (bf16[2,1,32,512]{3,2,0,1:T(8,128)(2,1)S(1)}, bf16[2,1,32,512]{3,2,0,1:T(8,128)(2,1)S(1)}, u32[]{:S(2)}, u32[]{:S(2)}) collective-permute-start(bf16[2,1,32,512]{3,2,0,1:T(8,128)(2,1)S(1)} %bitcast.56), channel_id=1, source_target_pairs={{0,1},{1,0},{2,3},{3,2},{4,5},{5,4},{6,7},{7,6},{8,9},{9,8},{10,11... | collective-permute-start | bytes 196616 | tf_op jit(solution)/shard_map/ppermute | solution.py:217
  30.0 1.3 copy-start.1
  30.0 8.7 %copy-start.13 = (bf16[512,3,256]{2,0,1:T(8,128)(2,1)S(1)}, bf16[512,3,256]{2,0,1:T(8,128)(2,1)}, u32[]{:S(2)}) copy-start(bf16[512,3,256]{2,0,1:T(8,128)(2,1)} %param.9) | copy-start | bytes 2359300
  30.0 10.8 %copy-start.11 = (f32[16,128]{1,0:T(8,128)S(1)}, f32[16,128]{1,0:T(8,128)}, u32[]{:S(2)}) copy-start(f32[16,128]{1,0:T(8,128)} %taps_ref.1) | copy-start | bytes 24580
  30.0 11.0 %copy-start.12 = (f32[16]{0:T(128)S(1)}, f32[16]{0:T(128)}, u32[]{:S(2)}) copy-start(f32[16]{0:T(128)} %param.12) | copy-start | bytes 196
  31.3 23.7 %all-to-all-start.1 = ((bf16[32,32,512]{2,1,0:T(8,128)(2,1)}), bf16[32,32,512]{2,1,0:T(8,128)(2,1)S(1)}, u32[]{:S(2)}, u32[]{:S(2)}) async-start(bf16[32,32,512]{2,1,0:T(8,128)(2,1)} %bitcast.10), calls=%async_computation.1 | async-start | bytes 2097152 | tf_op jit(solution)/shard_map/all_to_all | solution.py:267
  38.7 7.4 %collective-permute-start = (bf16[3,512,256]{2,1,0:T(8,128)(2,1)S(1)}, bf16[3,512,256]{2,1,0:T(8,128)(2,1)S(1)}, u32[]{:S(2)}, u32[]{:S(2)}) collective-permute-start(bf16[3,512,256]{2,1,0:T(8,128)(2,1)S(1)} %bitcast.72), channel_id=1, source_target_pairs={{0,32},{32,0},{1,33},{33,1},{2,34},{34,2},{3,35},{35,3},{4,36},{36... | collective-permute-start | bytes 2359304 | tf_op jit(solution)/shard_map/ppermute | solution.py:217
  46.1 0.9 copy-start.14
  50.6 20.2 %collective-permute-start.1 = (bf16[4,64,768]{2,1,0:T(8,128)(2,1)}, bf16[4,64,768]{2,1,0:T(8,128)(2,1)S(1)}, u32[]{:S(2)}, u32[]{:S(2)}) collective-permute-start(bf16[4,64,768]{2,1,0:T(8,128)(2,1)} %shard_map.105), channel_id=1, source_target_pairs={{0,64},{64,0},{128,192},{192,128},{256,320},{320,256},{384,448},{4... | collective-permute-start | bytes 1179656 | tf_op jit(solution)/shard_map/ppermute | solution.py:217
  55.0 1.0 copy-start.2
  59.5 13.8 %collective-permute-start.5 = (bf16[4,64,768]{2,1,0:T(8,128)(2,1)}, bf16[4,64,768]{2,1,0:T(8,128)(2,1)S(1)}, u32[]{:S(2)}, u32[]{:S(2)}) collective-permute-start(bf16[4,64,768]{2,1,0:T(8,128)(2,1)} %shard_map.107), channel_id=1, source_target_pairs={{0,64},{64,0},{128,192},{192,128},{256,320},{320,256},{384,448},{4... | collective-permute-start | bytes 1179656 | tf_op jit(solution)/shard_map/ppermute | solution.py:217
  67.1 3.7 %copy-start.6 = (bf16[4,64,768]{2,1,0:T(8,128)(2,1)S(1)}, bf16[4,64,768]{2,1,0:T(8,128)(2,1)}, u32[]{:S(2)}) copy-start(bf16[4,64,768]{2,1,0:T(8,128)(2,1)} %shard_map.104) | copy-start | bytes 1179652
  70.8 17.8 %collective-permute-start.2 = (bf16[2,64,768]{2,1,0:T(8,128)(2,1)S(1)}, bf16[2,64,768]{2,1,0:T(8,128)(2,1)S(1)}, u32[]{:S(2)}, u32[]{:S(2)}) collective-permute-start(bf16[2,64,768]{2,1,0:T(8,128)(2,1)S(1)} %get-tuple-element.46), channel_id=1, source_target_pairs={{0,128},{64,192},{128,0},{192,64},{256,384},{320,448},{384,256},{4... | collective-permute-start | bytes 589832 | tf_op jit(solution)/shard_map/ppermute | solution.py:217
  74.5 20.4 %collective-permute-start.6 = (bf16[2,64,768]{2,1,0:T(8,128)(2,1)S(1)}, bf16[2,64,768]{2,1,0:T(8,128)(2,1)S(1)}, u32[]{:S(2)}, u32[]{:S(2)}) collective-permute-start(bf16[2,64,768]{2,1,0:T(8,128)(2,1)S(1)} %get-tuple-element.44), channel_id=1, source_target_pairs={{0,128},{64,192},{128,0},{192,64},{256,384},{320,448},{384,256},{4... | collective-permute-start | bytes 589832 | tf_op jit(solution)/shard_map/ppermute | solution.py:217
  88.6 10.5 %collective-permute-start.3 = (bf16[1,64,768]{2,1,0:T(8,128)(2,1)S(1)}, bf16[1,64,768]{2,1,0:T(8,128)(2,1)S(1)}, u32[]{:S(2)}, u32[]{:S(2)}) collective-permute-start(bf16[1,64,768]{2,1,0:T(8,128)(2,1)S(1)} %add_convert_fusion.9), channel_id=1, source_target_pairs={{0,256},{64,320},{128,384},{192,448},{256,0},{320,64},{384,128},{4... | collective-permute-start | bytes 294920 | tf_op jit(solution)/shard_map/ppermute | solution.py:217
  95.0 18.0 %collective-permute-start.7 = (bf16[1,64,768]{2,1,0:T(8,128)(2,1)S(1)}, bf16[1,64,768]{2,1,0:T(8,128)(2,1)S(1)}, u32[]{:S(2)}, u32[]{:S(2)}) collective-permute-start(bf16[1,64,768]{2,1,0:T(8,128)(2,1)S(1)} %add_convert_fusion.6), channel_id=1, source_target_pairs={{0,256},{64,320},{128,384},{192,448},{256,0},{320,64},{384,128},{4... | collective-permute-start | bytes 294920 | tf_op jit(solution)/shard_map/ppermute | solution.py:217
  99.2 24.1 %copy-start.9 = (bf16[1,64,768]{2,1,0:T(8,128)(2,1)}, bf16[1,64,768]{2,1,0:T(8,128)(2,1)S(1)}, u32[]{:S(2)}) copy-start(bf16[1,64,768]{2,1,0:T(8,128)(2,1)S(1)} %add_convert_fusion.8) | copy-start | bytes 294916
  112.9 10.3 %copy-start.10 = (bf16[1,64,768]{2,1,0:T(8,128)(2,1)}, bf16[1,64,768]{2,1,0:T(8,128)(2,1)S(1)}, u32[]{:S(2)}) copy-start(bf16[1,64,768]{2,1,0:T(8,128)(2,1)S(1)} %add_convert_fusion.5) | copy-start | bytes 294916
  113.0 10.3 %collective-permute-start.8 = (bf16[8,768]{1,0:T(8,128)(2,1)S(1)}, bf16[8,768]{1,0:T(8,128)(2,1)S(1)}, u32[]{:S(2)}, u32[]{:S(2)}) collective-permute-start(bf16[8,768]{1,0:T(8,128)(2,1)S(1)} %fusion.4), channel_id=1, source_target_pairs={{0,32},{32,64},{64,96},{96,128},{128,160},{160,192},{192,224},{224... | collective-permute-start | bytes 36872 | tf_op jit(solution)/shard_map/ppermute | solution.py:223
  114.9 8.3 %collective-permute-start.9 = (bf16[16,768]{1,0:T(8,128)(2,1)S(1)}, bf16[16,768]{1,0:T(8,128)(2,1)S(1)}, u32[]{:S(2)}, u32[]{:S(2)}) collective-permute-start(bf16[16,768]{1,0:T(8,128)(2,1)S(1)} %fusion.1), channel_id=1, source_target_pairs={{32,0},{64,32},{96,64},{128,96},{160,128},{192,160},{224,192},{256... | collective-permute-start | bytes 73736 | tf_op jit(solution)/shard_map/ppermute | solution.py:223
  118.3 5.0 %collective-permute-start.10 = (bf16[16,256]{1,0:T(8,128)(2,1)S(1)}, bf16[16,256]{1,0:T(8,128)(2,1)S(1)}, u32[]{:S(2)}, u32[]{:S(2)}) collective-permute-start(bf16[16,256]{1,0:T(8,128)(2,1)S(1)} %slice_bitcast_fusion), channel_id=1, source_target_pairs={{32,0},{64,32},{96,64},{128,96},{160,128},{192,160},{224,192},{256... | collective-permute-start | bytes 24584 | tf_op jit(solution)/shard_map/ppermute | solution.py:223
  123.2 0.6 copy-start.21
  123.2 0.6 copy-start.20
  123.3 0.6 copy-start.19
  125.9 7.2 %collective-permute-start.12 = (bf16[144,256]{1,0:T(8,128)(2,1)}, bf16[144,256]{1,0:T(8,128)(2,1)S(1)}, u32[]{:S(2)}, u32[]{:S(2)}) collective-permute-start(bf16[144,256]{1,0:T(8,128)(2,1)} %get-tuple-element.28.cg_ref), channel_id=1, source_target_pairs={{32,0},{64,32},{96,64},{128,96},{160,128},{192,160},{224,192},{256... | collective-permute-start | bytes 221192 | tf_op jit(solution)/shard_map/ppermute | solution.py:223
  127.8 5.3 %collective-permute-start.11 = (bf16[128,256]{1,0:T(8,128)(2,1)}, bf16[128,256]{1,0:T(8,128)(2,1)S(1)}, u32[]{:S(2)}, u32[]{:S(2)}) collective-permute-start(bf16[128,256]{1,0:T(8,128)(2,1)} %get-tuple-element.27.prod_ref), channel_id=1, source_target_pairs={{0,32},{32,64},{64,96},{96,128},{128,160},{160,192},{192,224},{224... | collective-permute-start | bytes 196616 | tf_op jit(solution)/shard_map/ppermute | solution.py:223
  133.1 0.6 copy-start.18
  133.1 0.7 copy-start.17
  137.5 15.4 %collective-permute-start.16 = (bf16[1,64,768]{2,1,0:T(8,128)(2,1)}, bf16[1,64,768]{2,1,0:T(8,128)(2,1)S(1)}, u32[]{:S(2)}, u32[]{:S(2)}) collective-permute-start(bf16[1,64,768]{2,1,0:T(8,128)(2,1)} %bitcast.51), channel_id=1, source_target_pairs={{0,256},{64,320},{128,384},{192,448},{256,0},{320,64},{384,128},{4... | collective-permute-start | bytes 294920 | tf_op jit(solution)/shard_map/ppermute | solution.py:217
  152.9 36.2 %copy-start.5 = (bf16[1,64,768]{2,1,0:T(8,128)(2,1)}, bf16[1,64,768]{2,1,0:T(8,128)(2,1)S(1)}, u32[]{:S(2)}) copy-start(bf16[1,64,768]{2,1,0:T(8,128)(2,1)S(1)} %collective-permute-done.16.refs_1_) | copy-start | bytes 294916
  153.8 12.6 %collective-permute-start.17 = (bf16[2,64,768]{2,1,0:T(8,128)(2,1)S(1)}, bf16[2,64,768]{2,1,0:T(8,128)(2,1)S(1)}, u32[]{:S(2)}, u32[]{:S(2)}) collective-permute-start(bf16[2,64,768]{2,1,0:T(8,128)(2,1)S(1)} %pad_maximum_fusion.3), channel_id=1, source_target_pairs={{0,128},{64,192},{128,0},{192,64},{256,384},{320,448},{384,256},{4... | collective-permute-start | bytes 589832 | tf_op jit(solution)/shard_map/ppermute | solution.py:217
  166.5 22.6 %copy-start.8 = (bf16[2,64,768]{2,1,0:T(8,128)(2,1)}, bf16[2,64,768]{2,1,0:T(8,128)(2,1)S(1)}, u32[]{:S(2)}) copy-start(bf16[2,64,768]{2,1,0:T(8,128)(2,1)S(1)} %collective-permute-done.17.refs_2_) | copy-start | bytes 589828
  167.5 21.6 %collective-permute-start.18 = (bf16[4,64,768]{2,1,0:T(8,128)(2,1)S(1)}, bf16[4,64,768]{2,1,0:T(8,128)(2,1)S(1)}, u32[]{:S(2)}, u32[]{:S(2)}) collective-permute-start(bf16[4,64,768]{2,1,0:T(8,128)(2,1)S(1)} %pad_maximum_fusion.1), channel_id=1, source_target_pairs={{0,64},{64,0},{128,192},{192,128},{256,320},{320,256},{384,448},{4... | collective-permute-start | bytes 1179656 | tf_op jit(solution)/shard_map/ppermute | solution.py:217
  169.4 10.4 %collective-permute-start.13 = (bf16[1,64,768]{2,1,0:T(8,128)(2,1)}, bf16[1,64,768]{2,1,0:T(8,128)(2,1)S(1)}, u32[]{:S(2)}, u32[]{:S(2)}) collective-permute-start(bf16[1,64,768]{2,1,0:T(8,128)(2,1)} %bitcast.47), channel_id=1, source_target_pairs={{0,256},{64,320},{128,384},{192,448},{256,0},{320,64},{384,128},{4... | collective-permute-start | bytes 294920 | tf_op jit(solution)/shard_map/ppermute | solution.py:217
  179.8 20.5 %copy-start.4 = (bf16[1,64,768]{2,1,0:T(8,128)(2,1)}, bf16[1,64,768]{2,1,0:T(8,128)(2,1)S(1)}, u32[]{:S(2)}) copy-start(bf16[1,64,768]{2,1,0:T(8,128)(2,1)S(1)} %collective-permute-done.13.refs_1_) | copy-start | bytes 294916
  180.8 19.5 %collective-permute-start.14 = (bf16[2,64,768]{2,1,0:T(8,128)(2,1)S(1)}, bf16[2,64,768]{2,1,0:T(8,128)(2,1)S(1)}, u32[]{:S(2)}, u32[]{:S(2)}) collective-permute-start(bf16[2,64,768]{2,1,0:T(8,128)(2,1)S(1)} %pad_maximum_fusion.2), channel_id=1, source_target_pairs={{0,128},{64,192},{128,0},{192,64},{256,384},{320,448},{384,256},{4... | collective-permute-start | bytes 589832 | tf_op jit(solution)/shard_map/ppermute | solution.py:217
  189.1 0.8 copy-start.15
  194.0 6.3 %copy-start.3 = (bf16[64,768]{1,0:T(8,128)(2,1)S(1)}, bf16[64,768]{1,0:T(8,128)(2,1)}, u32[]{:S(2)}) copy-start(bf16[64,768]{1,0:T(8,128)(2,1)} %get-tuple-element.35) | copy-start | bytes 294916
  194.1 32.5 %all-to-all-start.3 = ((bf16[32,32,512]{2,1,0:T(8,128)(2,1)}), bf16[32,32,512]{2,1,0:T(8,128)(2,1)S(1)}, u32[]{:S(2)}, u32[]{:S(2)}) async-start(bf16[32,32,512]{2,1,0:T(8,128)(2,1)} %bitcast.46), calls=%async_computation.3 | async-start | bytes 2097152 | tf_op jit(solution)/shard_map/all_to_all | solution.py:267
  200.3 13.8 %copy-start.7 = (bf16[2,64,768]{2,1,0:T(8,128)(2,1)}, bf16[2,64,768]{2,1,0:T(8,128)(2,1)S(1)}, u32[]{:S(2)}) copy-start(bf16[2,64,768]{2,1,0:T(8,128)(2,1)S(1)} %collective-permute-done.14.refs_2_) | copy-start | bytes 589828
  200.4 13.7 %collective-permute-start.15 = (bf16[4,64,768]{2,1,0:T(8,128)(2,1)S(1)}, bf16[4,64,768]{2,1,0:T(8,128)(2,1)S(1)}, u32[]{:S(2)}, u32[]{:S(2)}) collective-permute-start(bf16[4,64,768]{2,1,0:T(8,128)(2,1)S(1)} %pad_maximum_fusion), channel_id=1, source_target_pairs={{0,64},{64,0},{128,192},{192,128},{256,320},{320,256},{384,448},{4... | collective-permute-start | bytes 1179656 | tf_op jit(solution)/shard_map/ppermute | solution.py:217
  214.1 0.8 copy-start.16
  223.8 9.9 %collective-permute-start.20 = (bf16[3,512,256]{2,1,0:T(8,128)(2,1)}, bf16[3,512,256]{2,1,0:T(8,128)(2,1)S(1)}, u32[]{:S(2)}, u32[]{:S(2)}) collective-permute-start(bf16[3,512,256]{2,1,0:T(8,128)(2,1)} %get-tuple-element.42), channel_id=1, source_target_pairs={{0,32},{32,0},{1,33},{33,1},{2,34},{34,2},{3,35},{35,3},{4,36},{36... | collective-permute-start | bytes 2359304 | tf_op jit(solution)/shard_map/ppermute | solution.py:217
  226.5 23.5 %all-to-all-start.2 = ((bf16[32,32,512]{2,1,0:T(8,128)(2,1)}), bf16[32,32,512]{2,1,0:T(8,128)(2,1)S(1)}, u32[]{:S(2)}, u32[]{:S(2)}) async-start(bf16[32,32,512]{2,1,0:T(8,128)(2,1)} %bitcast.21), calls=%async_computation.2 | async-start | bytes 2097152 | tf_op jit(solution)/shard_map/all_to_all | solution.py:267
  236.4 14.0 %collective-permute-start.19 = (bf16[2,32,512]{2,1,0:T(8,128)(2,1)S(1)}, bf16[2,32,512]{2,1,0:T(8,128)(2,1)S(1)}, u32[]{:S(2)}, u32[]{:S(2)}) collective-permute-start(bf16[2,32,512]{2,1,0:T(8,128)(2,1)S(1)} %bitcast_reduce_fusion), channel_id=1, source_target_pairs={{0,1},{1,0},{2,3},{3,2},{4,5},{5,4},{6,7},{7,6},{8,9},{9,8},{10,11... | collective-permute-start | bytes 196616 | tf_op jit(solution)/shard_map/ppermute | solution.py:217

commit v6 on v5

--- a/solution.py
+++ b/solution.py
@@ -14,17 +14,36 @@
 INTERPRET = False
 
 
-def call(body, outs, *args, scratch=()):
+def call(body, outs, *args):
     whole = pl.BlockSpec(memory_space=pltpu.VMEM)
-    scalar = pl.BlockSpec(memory_space=pltpu.SMEM)
     many = isinstance(outs, (tuple, list))
     size = sum(math.prod(a.shape) * a.dtype.itemsize for a in args)
+    loose = [i for i, a in enumerate(args) if a.ndim > 1 and a.shape[-1] % 128 == 0 and a.shape[-2] % 16 == 0 and a.size >= 1 << 14]
+
+    def spec(i):
+        if args[i].shape == (1,):
+            return pl.BlockSpec(memory_space=pltpu.SMEM)
+        return pl.BlockSpec(memory_space=pl.ANY) if i in loose else whole
+
+    def run(*refs):
+        held, sems = refs[-1 - len(loose) : -1], refs[-1]
+        rest = list(refs[: -1 - len(loose)])
+        copies = [pltpu.make_async_copy(rest[i], held[j], sems.at[j]) for j, i in enumerate(loose)]
+        for copy in copies:
+            copy.start()
+        for copy in copies:
+            copy.wait()
+        for j, i in enumerate(loose):
+            rest[i] = held[j]
+        body(*rest)
+
     return pl.pallas_call(
-        body,
+        run if loose else body,
         out_shape=outs,
-        in_specs=[scalar if a.shape == (1,) else whole for a in args],
+        in_specs=[spec(i) for i in range(len(args))],
         out_specs=[whole] * len(outs) if many else whole,
-        scratch_shapes=list(scratch),
+        scratch_shapes=[pltpu.VMEM(args[i].shape, args[i].dtype) for i in loose] + [pltpu.SemaphoreType.DMA((len(loose),))] * bool(loose),
+        compiler_params=pltpu.CompilerParams(vmem_limit_bytes=20 << 20),
         cost_estimate=pl.CostEstimate(flops=10**9, bytes_accessed=size, transcendentals=0),
         interpret=INTERPRET,
     )(*args)

time: 255 us -> 242 us (0.949)
  Pallas kernels: 37.2 us -> 25 us
    pallas_call x10, Pallas kernels: 37.2 us -> 25 us  [call(): pl.pallas_call(run if loose else body, out_shape=outs, in_specs=[spec(i)...]
    concatenate x4, other arithmetic: 2.94 us -> 0.12 us  [line_gather(): so_far = jnp.concatenate(parts, axis=0) if len(parts) > 1 else parts[0]]
  transfers between devices with their start and end apart: 25 -> 25, of which waited for: 13 -> 13; matrix products, arithmetic and copies ran while one was open for 3% -> 2% of each run, Pallas kernels for 13% -> 9%
where the time goes in v6:
time: 242 us; the launch traced here: 239 us
  starting transfers between devices  124 us (51%)
  waiting for transfers between devices  73.2 us (30%)
  Pallas kernels  25 us (10%)
  local copies, waits for them, and re-layouts  8.41 us (3%)
  other arithmetic  6.03 us (2%)
    ppermute x16, starting transfers between devices, swap(): lax.ppermute(x, axis, [(i, i ^ by) for i in range(lax.axis_size(axis))])  80.6 us
    ppermute x16, waiting for transfers between devices, swap(): lax.ppermute(x, axis, [(i, i ^ by) for i in range(lax.axis_size(axis))])  63.8 us
    all_to_all x4, starting transfers between devices, exchange(): lax.all_to_all(x.reshape(2 * pieces, lines, rows), ('core', 'x', 'y'), 0,...  31.2 us
    pallas_call x10, Pallas kernels, call(): pl.pallas_call(run if loose else body, out_shape=outs, in_specs=[spec(i)...  25 us
    ppermute x5, starting transfers between devices, shifted(): lax.ppermute(x, axis, [(i, i + by) for i in range(count) if 0 <= i + by <...  12.1 us
    unnamed x44, local copies, waits for them, and re-layouts  5.8 us
    all_to_all x4, waiting for transfers between devices, exchange(): lax.all_to_all(x.reshape(2 * pieces, lines, rows), ('core', 'x', 'y'), 0,...  4.96 us
  transfers between devices with their start and end apart: 25, of which 13 were waited for; matrix products, arithmetic and copies ran while one was open for 2% of the time, Pallas kernels for 9%

profile of v6, /device:TPU:1, one launch (start us, length us, event | category | flops | bytes accessed | tf_op | source)
XLA Modules:
  0.0 238.8 jit_solution(9986356707875155165)
XLA Ops:
  2.9 10.5 %all-to-all-start = ((bf16[32,32,512]{2,1,0:T(8,128)(2,1)}), bf16[32,32,512]{2,1,0:T(8,128)(2,1)S(1)}, u32[]{:S(2)}, u32[]{:S(2)}) async-start(bf16[32,32,512]{2,1,0:T(8,128)(2,1)} %bitcast.4), calls=%async_computation | async-start | bytes 2097152 | tf_op jit(solution)/shard_map/all_to_all | solution.py:286
  13.5 13.5 %collective-permute-start.4 = (bf16[2,1,32,512]{3,2,0,1:T(8,128)(2,1)S(1)}, bf16[2,1,32,512]{3,2,0,1:T(8,128)(2,1)S(1)}, u32[]{:S(2)}, u32[]{:S(2)}) collective-permute-start(bf16[2,1,32,512]{3,2,0,1:T(8,128)(2,1)S(1)} %bitcast.70), channel_id=1, source_target_pairs={{0,1},{1,0},{2,3},{3,2},{4,5},{5,4},{6,7},{7,6},{8,9},{9,8},{10,11... | collective-permute-start | bytes 196616 | tf_op jit(solution)/shard_map/ppermute | solution.py:236
  27.0 2.2 collective-permute-done.4
  31.1 7.4 %all-to-all-start.1 = ((bf16[32,32,512]{2,1,0:T(8,128)(2,1)}), bf16[32,32,512]{2,1,0:T(8,128)(2,1)S(1)}, u32[]{:S(2)}, u32[]{:S(2)}) async-start(bf16[32,32,512]{2,1,0:T(8,128)(2,1)} %bitcast.68), calls=%async_computation.1 | async-start | bytes 2097152 | tf_op jit(solution)/shard_map/all_to_all | solution.py:286
  38.5 2.1 collective-permute-start
  40.9 1.8 shard_map.103
  45.5 2.5 %shard_map.105 = bf16[4,64,768]{2,1,0:T(8,128)(2,1)S(1)} custom-call(s32[1]{0:T(128)} %bitcast.1.refs_0_, bf16[256,512]{1,0:T(8,128)(2,1)S(1)} %get-tuple-element.26.refs_1_, bf16[2,512,512]{2,1,0:T(8,128)(2,1)S(1)} %bitcast.40, bf16[3,512,256]{2,1,0:T(8,128)(2,1)S(1)} %bitcast.61, bf16[3,512,256]{2,1,0:T(8,128)(2,1)} %collective-permute-done.refs_4_.refs_7_), custom_call_target="tpu_custom_call" | custom-call | flops 1000000000 | bytes 2883588 | tf_op jit(solution)/shard_map/pallas_call | solution.py:40
  48.0 3.9 %collective-permute-start.1 = (bf16[4,64,768]{2,1,0:T(8,128)(2,1)S(1)}, bf16[4,64,768]{2,1,0:T(8,128)(2,1)}, u32[]{:S(2)}, u32[]{:S(2)}) collective-permute-start(bf16[4,64,768]{2,1,0:T(8,128)(2,1)S(1)} %shard_map.105), channel_id=1, source_target_pairs={{0,64},{64,0},{128,192},{192,128},{256,320},{320,256},{384,448},{4... | collective-permute-start | bytes 1179656 | tf_op jit(solution)/shard_map/ppermute | solution.py:236
  51.9 2.8 %all-to-all-done.1 = bf16[32,32,512]{2,1,0:T(8,128)(2,1)S(1)} async-done(((bf16[32,32,512]{2,1,0:T(8,128)(2,1)}), bf16[32,32,512]{2,1,0:T(8,128)(2,1)S(1)}, u32[]{:S(2)}, u32[]{:S(2)}) %all-to-all-start.1) | async-done | bytes 1048608 | tf_op jit(solution)/shard_map/all_to_all | solution.py:286
  55.9 2.4 %shard_map.107 = bf16[4,64,768]{2,1,0:T(8,128)(2,1)S(1)} custom-call(s32[1]{0:T(128)} %bitcast.1.refs_0_, bf16[256,512]{1,0:T(8,128)(2,1)S(1)} %copy-done.18, bf16[2,512,512]{2,1,0:T(8,128)(2,1)S(1)} %bitcast.43, bf16[3,512,256]{2,1,0:T(8,128)(2,1)S(1)} %bitcast.62, bf16[3,512,256]{2,1,0:T(8,128)(2,1)} %collective-permute-done.refs_4_.refs_7_), custom_call_target="tpu_custom_call" | custom-call | flops 1000000000 | bytes 2883588 | tf_op jit(solution)/shard_map/pallas_call | solution.py:40
  58.3 3.9 %collective-permute-start.5 = (bf16[4,64,768]{2,1,0:T(8,128)(2,1)S(1)}, bf16[4,64,768]{2,1,0:T(8,128)(2,1)S(1)}, u32[]{:S(2)}, u32[]{:S(2)}) collective-permute-start(bf16[4,64,768]{2,1,0:T(8,128)(2,1)S(1)} %shard_map.107), channel_id=1, source_target_pairs={{0,64},{64,0},{128,192},{192,128},{256,320},{320,256},{384,448},{4... | collective-permute-start | bytes 1179656 | tf_op jit(solution)/shard_map/ppermute | solution.py:236
  62.2 2.4 %shard_map.104 = bf16[4,64,768]{2,1,0:T(8,128)(2,1)S(1)} custom-call(s32[1]{0:T(128)} %bitcast.1.refs_0_, bf16[256,512]{1,0:T(8,128)(2,1)S(1)} %copy-done.16, bf16[2,512,512]{2,1,0:T(8,128)(2,1)S(1)} %bitcast.41, bf16[3,512,256]{2,1,0:T(8,128)(2,1)S(1)} %bitcast.63, bf16[3,512,256]{2,1,0:T(8,128)(2,1)} %collective-permute-done.refs_4_.refs_7_), custom_call_target="tpu_custom_call" | custom-call | flops 1000000000 | bytes 2883588 | tf_op jit(solution)/shard_map/pallas_call | solution.py:40
  64.6 2.4 %shard_map.106 = bf16[4,64,768]{2,1,0:T(8,128)(2,1)S(1)} custom-call(s32[1]{0:T(128)} %bitcast.1.refs_0_, bf16[256,512]{1,0:T(8,128)(2,1)S(1)} %copy-done.16, bf16[2,512,512]{2,1,0:T(8,128)(2,1)S(1)} %bitcast.44, bf16[3,512,256]{2,1,0:T(8,128)(2,1)S(1)} %bitcast.64, bf16[3,512,256]{2,1,0:T(8,128)(2,1)} %collective-permute-done.refs_4_.refs_7_), custom_call_target="tpu_custom_call" | custom-call | flops 1000000000 | bytes 2883588 | tf_op jit(solution)/shard_map/pallas_call | solution.py:40
  67.1 1.1 add_convert_fusion.4
  68.2 2.6 %collective-permute-start.2 = (bf16[2,64,768]{2,1,0:T(8,128)(2,1)S(1)}, bf16[2,64,768]{2,1,0:T(8,128)(2,1)S(1)}, u32[]{:S(2)}, u32[]{:S(2)}) collective-permute-start(bf16[2,64,768]{2,1,0:T(8,128)(2,1)S(1)} %get-tuple-element.46), channel_id=1, source_target_pairs={{0,128},{64,192},{128,0},{192,64},{256,384},{320,448},{384,256},{4... | collective-permute-start | bytes 589832 | tf_op jit(solution)/shard_map/ppermute | solution.py:236
  70.9 3.7 %collective-permute-start.6 = (bf16[2,64,768]{2,1,0:T(8,128)(2,1)S(1)}, bf16[2,64,768]{2,1,0:T(8,128)(2,1)S(1)}, u32[]{:S(2)}, u32[]{:S(2)}) collective-permute-start(bf16[2,64,768]{2,1,0:T(8,128)(2,1)S(1)} %get-tuple-element.44), channel_id=1, source_target_pairs={{0,128},{64,192},{128,0},{192,64},{256,384},{320,448},{384,256},{4... | collective-permute-start | bytes 589832 | tf_op jit(solution)/shard_map/ppermute | solution.py:236
  74.7 11.5 %collective-permute-done.2 = bf16[2,64,768]{2,1,0:T(8,128)(2,1)S(1)} collective-permute-done((bf16[2,64,768]{2,1,0:T(8,128)(2,1)S(1)}, bf16[2,64,768]{2,1,0:T(8,128)(2,1)S(1)}, u32[]{:S(2)}, u32[]{:S(2)}) %collective-permute-start.2) | collective-permute-done | bytes 196640 | tf_op jit(solution)/shard_map/ppermute | solution.py:236
  86.2 6.2 %collective-permute-start.3 = (bf16[1,64,768]{2,1,0:T(8,128)(2,1)S(1)}, bf16[1,64,768]{2,1,0:T(8,128)(2,1)S(1)}, u32[]{:S(2)}, u32[]{:S(2)}) collective-permute-start(bf16[1,64,768]{2,1,0:T(8,128)(2,1)S(1)} %add_convert_fusion.9), channel_id=1, source_target_pairs={{0,256},{64,320},{128,384},{192,448},{256,0},{320,64},{384,128},{4... | collective-permute-start | bytes 294920 | tf_op jit(solution)/shard_map/ppermute | solution.py:236
  92.4 4.2 %collective-permute-start.7 = (bf16[1,64,768]{2,1,0:T(8,128)(2,1)S(1)}, bf16[1,64,768]{2,1,0:T(8,128)(2,1)S(1)}, u32[]{:S(2)}, u32[]{:S(2)}) collective-permute-start(bf16[1,64,768]{2,1,0:T(8,128)(2,1)S(1)} %add_convert_fusion.6), channel_id=1, source_target_pairs={{0,256},{64,320},{128,384},{192,448},{256,0},{320,64},{384,128},{4... | collective-permute-start | bytes 294920 | tf_op jit(solution)/shard_map/ppermute | solution.py:236
  96.6 13.8 %collective-permute-done.7 = bf16[1,64,768]{2,1,0:T(8,128)(2,1)S(1)} collective-permute-done((bf16[1,64,768]{2,1,0:T(8,128)(2,1)S(1)}, bf16[1,64,768]{2,1,0:T(8,128)(2,1)S(1)}, u32[]{:S(2)}, u32[]{:S(2)}) %collective-permute-start.7) | collective-permute-done | bytes 98336 | tf_op jit(solution)/shard_map/ppermute | solution.py:236
  110.5 1.9 collective-permute-start.8
  112.4 2.7 %collective-permute-start.9 = (bf16[16,768]{1,0:T(8,128)(2,1)S(1)}, bf16[16,768]{1,0:T(8,128)(2,1)S(1)}, u32[]{:S(2)}, u32[]{:S(2)}) collective-permute-start(bf16[16,768]{1,0:T(8,128)(2,1)S(1)} %fusion.1), channel_id=1, source_target_pairs={{32,0},{64,32},{96,64},{128,96},{160,128},{192,160},{224,192},{256... | collective-permute-start | bytes 73736 | tf_op jit(solution)/shard_map/ppermute | solution.py:242
  115.2 1.9 collective-permute-start.10
  117.1 3.0 %collective-permute-done.10.refs_6_.refs_11_ = bf16[16,256]{1,0:T(8,128)(2,1)S(1)} collective-permute-done((bf16[16,256]{1,0:T(8,128)(2,1)S(1)}, bf16[16,256]{1,0:T(8,128)(2,1)S(1)}, u32[]{:S(2)}, u32[]{:S(2)}) %collective-permute-start.10) | collective-permute-done | bytes 8224 | tf_op jit(solution)/shard_map/ppermute | solution.py:242
  120.9 1.9 collective-permute-start.12
  122.8 3.6 %collective-permute-start.11 = (bf16[128,256]{1,0:T(8,128)(2,1)S(1)}, bf16[128,256]{1,0:T(8,128)(2,1)S(1)}, u32[]{:S(2)}, u32[]{:S(2)}) collective-permute-start(bf16[128,256]{1,0:T(8,128)(2,1)S(1)} %get-tuple-element.27.refs_2_), channel_id=1, source_target_pairs={{0,32},{32,64},{64,96},{96,128},{128,160},{160,192},{192,224},{224... | collective-permute-start | bytes 196616 | tf_op jit(solution)/shard_map/ppermute | solution.py:242
  126.4 1.3 collective-permute-done.11.refs_3_
  127.8 2.8 %shard_map.109 = (bf16[128,256]{1,0:T(8,128)(2,1)}, bf16[64,768]{1,0:T(8,128)(2,1)S(1)}, bf16[64,768]{1,0:T(8,128)(2,1)S(1)}) custom-call(bf16[2048,256]{1,0:T(8,128)(2,1)S(1)} %copy-done.12, bf16[2048,256]{1,0:T(8,128)(2,1)S(1)} %copy-done.14, bf16[128,256]{1,0:T(8,128)(2,1)S(1)} %get-tuple-element.27.refs_2_, ...), custom_call_target="tpu_custom_call" | custom-call | flops 1000000000 | bytes 2902020 | tf_op jit(solution)/shard_map/pallas_call | solution.py:40
  130.6 4.5 %collective-permute-start.16 = (bf16[1,64,768]{2,1,0:T(8,128)(2,1)S(1)}, bf16[1,64,768]{2,1,0:T(8,128)(2,1)S(1)}, u32[]{:S(2)}, u32[]{:S(2)}) collective-permute-start(bf16[1,64,768]{2,1,0:T(8,128)(2,1)S(1)} %bitcast.51), channel_id=1, source_target_pairs={{0,256},{64,320},{128,384},{192,448},{256,0},{320,64},{384,128},{4... | collective-permute-start | bytes 294920 | tf_op jit(solution)/shard_map/ppermute | solution.py:236
  135.1 11.0 %collective-permute-done.16.refs_3_ = bf16[1,64,768]{2,1,0:T(8,128)(2,1)S(1)} collective-permute-done((bf16[1,64,768]{2,1,0:T(8,128)(2,1)S(1)}, bf16[1,64,768]{2,1,0:T(8,128)(2,1)S(1)}, u32[]{:S(2)}, u32[]{:S(2)}) %collective-permute-start.16) | collective-permute-done | bytes 98336 | tf_op jit(solution)/shard_map/ppermute | solution.py:236
  146.1 1.9 collective-permute-start.17
  148.1 10.3 %collective-permute-done.17.refs_4_ = bf16[2,64,768]{2,1,0:T(8,128)(2,1)S(1)} collective-permute-done((bf16[2,64,768]{2,1,0:T(8,128)(2,1)S(1)}, bf16[2,64,768]{2,1,0:T(8,128)(2,1)S(1)}, u32[]{:S(2)}, u32[]{:S(2)}) %collective-permute-start.17) | collective-permute-done | bytes 196640 | tf_op jit(solution)/shard_map/ppermute | solution.py:236
  158.5 1.9 collective-permute-start.18
  160.4 5.5 %collective-permute-start.13 = (bf16[1,64,768]{2,1,0:T(8,128)(2,1)S(1)}, bf16[1,64,768]{2,1,0:T(8,128)(2,1)S(1)}, u32[]{:S(2)}, u32[]{:S(2)}) collective-permute-start(bf16[1,64,768]{2,1,0:T(8,128)(2,1)S(1)} %bitcast.47), channel_id=1, source_target_pairs={{0,256},{64,320},{128,384},{192,448},{256,0},{320,64},{384,128},{4... | collective-permute-start | bytes 294920 | tf_op jit(solution)/shard_map/ppermute | solution.py:236
  165.9 4.8 %collective-permute-done.13.refs_3_ = bf16[1,64,768]{2,1,0:T(8,128)(2,1)S(1)} collective-permute-done((bf16[1,64,768]{2,1,0:T(8,128)(2,1)S(1)}, bf16[1,64,768]{2,1,0:T(8,128)(2,1)S(1)}, u32[]{:S(2)}, u32[]{:S(2)}) %collective-permute-start.13) | collective-permute-done | bytes 98336 | tf_op jit(solution)/shard_map/ppermute | solution.py:236
  170.7 8.2 %collective-permute-start.14 = (bf16[2,64,768]{2,1,0:T(8,128)(2,1)S(1)}, bf16[2,64,768]{2,1,0:T(8,128)(2,1)S(1)}, u32[]{:S(2)}, u32[]{:S(2)}) collective-permute-start(bf16[2,64,768]{2,1,0:T(8,128)(2,1)S(1)} %pad_maximum_fusion.2), channel_id=1, source_target_pairs={{0,128},{64,192},{128,0},{192,64},{256,384},{320,448},{384,256},{4... | collective-permute-start | bytes 589832 | tf_op jit(solution)/shard_map/ppermute | solution.py:236
  179.0 4.4 %shard_map.111 = (bf16[2,512,512]{2,1,0:T(8,128)(2,1)}, bf16[512,768]{1,0:T(8,128)(2,1)S(1)}) custom-call(s32[1]{0:T(128)} %bitcast.1.refs_0_, bf16[512,512]{1,0:T(8,128)(2,1)S(1)} %copy-done.20, bf16[1,64,768]{2,1,0:T(8,128)(2,1)S(1)} %bitcast.54, bf16[1,64,768]{2,1,0:T(8,128)(2,1)S(1)} %collective-permute-done.16.refs_3_, ...), custom_call_target="tpu_custom_call" | custom-call | flops 1000000000 | bytes 2883588 | tf_op jit(solution)/shard_map/pallas_call | solution.py:40
  184.3 6.1 %all-to-all-start.3 = ((bf16[32,32,512]{2,1,0:T(8,128)(2,1)}), bf16[32,32,512]{2,1,0:T(8,128)(2,1)}, u32[]{:S(2)}, u32[]{:S(2)}) async-start(bf16[32,32,512]{2,1,0:T(8,128)(2,1)} %bitcast.24), calls=%async_computation.3 | async-start | bytes 2097152 | tf_op jit(solution)/shard_map/all_to_all | solution.py:286
  190.5 4.2 %collective-permute-start.15 = (bf16[4,64,768]{2,1,0:T(8,128)(2,1)S(1)}, bf16[4,64,768]{2,1,0:T(8,128)(2,1)S(1)}, u32[]{:S(2)}, u32[]{:S(2)}) collective-permute-start(bf16[4,64,768]{2,1,0:T(8,128)(2,1)S(1)} %pad_maximum_fusion), channel_id=1, source_target_pairs={{0,64},{64,0},{128,192},{192,128},{256,320},{320,256},{384,448},{4... | collective-permute-start | bytes 1179656 | tf_op jit(solution)/shard_map/ppermute | solution.py:236
  194.7 9.1 %collective-permute-done.15.refs_5_ = bf16[4,64,768]{2,1,0:T(8,128)(2,1)S(1)} collective-permute-done((bf16[4,64,768]{2,1,0:T(8,128)(2,1)S(1)}, bf16[4,64,768]{2,1,0:T(8,128)(2,1)S(1)}, u32[]{:S(2)}, u32[]{:S(2)}) %collective-permute-start.15) | collective-permute-done | bytes 393248 | tf_op jit(solution)/shard_map/ppermute | solution.py:236
  203.8 3.4 %shard_map.110 = (bf16[2,512,512]{2,1,0:T(8,128)(2,1)S(1)}, bf16[512,768]{1,0:T(8,128)(2,1)S(1)}) custom-call(s32[1]{0:T(128)} %bitcast.1.refs_0_, bf16[512,512]{1,0:T(8,128)(2,1)S(1)} %copy-done.20, bf16[1,64,768]{2,1,0:T(8,128)(2,1)S(1)} %bitcast.50, bf16[1,64,768]{2,1,0:T(8,128)(2,1)S(1)} %collective-permute-done.13.refs_3_, ...), custom_call_target="tpu_custom_call" | custom-call | flops 1000000000 | bytes 2883588 | tf_op jit(solution)/shard_map/pallas_call | solution.py:40
  208.2 2.1 shard_map.112
  210.3 2.7 %collective-permute-start.20 = (bf16[3,512,256]{2,1,0:T(8,128)(2,1)S(1)}, bf16[3,512,256]{2,1,0:T(8,128)(2,1)}, u32[]{:S(2)}, u32[]{:S(2)}) collective-permute-start(bf16[3,512,256]{2,1,0:T(8,128)(2,1)S(1)} %get-tuple-element.42), channel_id=1, source_target_pairs={{0,32},{32,0},{1,33},{33,1},{2,34},{34,2},{3,35},{35,3},{4,36},{36... | collective-permute-start | bytes 2359304 | tf_op jit(solution)/shard_map/ppermute | solution.py:236
  213.1 7.2 %all-to-all-start.2 = ((bf16[32,32,512]{2,1,0:T(8,128)(2,1)}), bf16[32,32,512]{2,1,0:T(8,128)(2,1)S(1)}, u32[]{:S(2)}, u32[]{:S(2)}) async-start(bf16[32,32,512]{2,1,0:T(8,128)(2,1)} %bitcast.46), calls=%async_computation.2 | async-start | bytes 2097152 | tf_op jit(solution)/shard_map/all_to_all | solution.py:286
  220.3 2.2 fusion
  222.4 1.4 bitcast_reduce_fusion
  223.8 11.4 %collective-permute-start.19 = (bf16[2,32,512]{2,1,0:T(8,128)(2,1)S(1)}, bf16[2,32,512]{2,1,0:T(8,128)(2,1)S(1)}, u32[]{:S(2)}, u32[]{:S(2)}) collective-permute-start(bf16[2,32,512]{2,1,0:T(8,128)(2,1)S(1)} %bitcast_reduce_fusion), channel_id=1, source_target_pairs={{0,1},{1,0},{2,3},{3,2},{4,5},{5,4},{6,7},{7,6},{8,9},{9,8},{10,11... | collective-permute-start | bytes 196616 | tf_op jit(solution)/shard_map/ppermute | solution.py:236
  235.2 1.4 all-to-all-done.2
  (87 shorter events, 13.4 us)
Async XLA Ops:
  0.6 1.0 copy-start
  2.9 27.1 %all-to-all-start = ((bf16[32,32,512]{2,1,0:T(8,128)(2,1)}), bf16[32,32,512]{2,1,0:T(8,128)(2,1)S(1)}, u32[]{:S(2)}, u32[]{:S(2)}) async-start(bf16[32,32,512]{2,1,0:T(8,128)(2,1)} %bitcast.4), calls=%async_computation | async-start | bytes 2097152 | tf_op jit(solution)/shard_map/all_to_all | solution.py:286
  13.5 15.7 %collective-permute-start.4 = (bf16[2,1,32,512]{3,2,0,1:T(8,128)(2,1)S(1)}, bf16[2,1,32,512]{3,2,0,1:T(8,128)(2,1)S(1)}, u32[]{:S(2)}, u32[]{:S(2)}) collective-permute-start(bf16[2,1,32,512]{3,2,0,1:T(8,128)(2,1)S(1)} %bitcast.70), channel_id=1, source_target_pairs={{0,1},{1,0},{2,3},{3,2},{4,5},{5,4},{6,7},{7,6},{8,9},{9,8},{10,11... | collective-permute-start | bytes 196616 | tf_op jit(solution)/shard_map/ppermute | solution.py:236
  30.0 8.5 %copy-start.6 = (bf16[512,3,256]{2,0,1:T(8,128)(2,1)S(1)}, bf16[512,3,256]{2,0,1:T(8,128)(2,1)}, u32[]{:S(2)}) copy-start(bf16[512,3,256]{2,0,1:T(8,128)(2,1)} %param.9) | copy-start | bytes 2359300
  30.0 10.6 %copy-start.4 = (f32[16,128]{1,0:T(8,128)S(1)}, f32[16,128]{1,0:T(8,128)}, u32[]{:S(2)}) copy-start(f32[16,128]{1,0:T(8,128)} %taps_ref.1) | copy-start | bytes 24580
  30.0 10.8 %copy-start.21 = (f32[16]{0:T(128)S(1)}, f32[16]{0:T(128)}, u32[]{:S(2)}) copy-start(f32[16]{0:T(128)} %param.12) | copy-start | bytes 196
  31.1 23.7 %all-to-all-start.1 = ((bf16[32,32,512]{2,1,0:T(8,128)(2,1)}), bf16[32,32,512]{2,1,0:T(8,128)(2,1)S(1)}, u32[]{:S(2)}, u32[]{:S(2)}) async-start(bf16[32,32,512]{2,1,0:T(8,128)(2,1)} %bitcast.68), calls=%async_computation.1 | async-start | bytes 2097152 | tf_op jit(solution)/shard_map/all_to_all | solution.py:286
  38.5 7.1 %collective-permute-start = (bf16[3,512,256]{2,1,0:T(8,128)(2,1)S(1)}, bf16[3,512,256]{2,1,0:T(8,128)(2,1)}, u32[]{:S(2)}, u32[]{:S(2)}) collective-permute-start(bf16[3,512,256]{2,1,0:T(8,128)(2,1)S(1)} %bitcast.60), channel_id=1, source_target_pairs={{0,32},{32,0},{1,33},{33,1},{2,34},{34,2},{3,35},{35,3},{4,36},{36... | collective-permute-start | bytes 2359304 | tf_op jit(solution)/shard_map/ppermute | solution.py:236
  42.8 1.0 copy-start.11
  43.8 1.0 copy-start.13
  44.7 0.8 copy-start.19
  45.5 2.5 %copy-start.15 = (bf16[256,512]{1,0:T(8,128)(2,1)}, bf16[256,512]{1,0:T(8,128)(2,1)S(1)}, u32[]{:S(2)}) copy-start(bf16[256,512]{1,0:T(8,128)(2,1)S(1)} %get-tuple-element.25.refs_1_) | copy-start | bytes 786436
  45.5 2.5 %copy-start.17 = (bf16[256,512]{1,0:T(8,128)(2,1)}, bf16[256,512]{1,0:T(8,128)(2,1)S(1)}, u32[]{:S(2)}) copy-start(bf16[256,512]{1,0:T(8,128)(2,1)S(1)} %get-tuple-element.26.refs_1_) | copy-start | bytes 786436
  48.0 19.0 %collective-permute-start.1 = (bf16[4,64,768]{2,1,0:T(8,128)(2,1)S(1)}, bf16[4,64,768]{2,1,0:T(8,128)(2,1)}, u32[]{:S(2)}, u32[]{:S(2)}) collective-permute-start(bf16[4,64,768]{2,1,0:T(8,128)(2,1)S(1)} %shard_map.105), channel_id=1, source_target_pairs={{0,64},{64,0},{128,192},{192,128},{256,320},{320,256},{384,448},{4... | collective-permute-start | bytes 1179656 | tf_op jit(solution)/shard_map/ppermute | solution.py:236
  54.7 9.9 %copy-start.1 = (bf16[32,32,512]{2,1,0:T(8,128)(2,1)}, bf16[32,32,512]{2,1,0:T(8,128)(2,1)S(1)}, u32[]{:S(2)}) copy-start(bf16[32,32,512]{2,1,0:T(8,128)(2,1)S(1)} %all-to-all-done.1) | copy-start | bytes 3145732
  54.7 1.1 copy-start.18
  55.9 6.3 %copy-start.16 = (bf16[256,512]{1,0:T(8,128)(2,1)S(1)}, bf16[256,512]{1,0:T(8,128)(2,1)}, u32[]{:S(2)}) copy-start(bf16[256,512]{1,0:T(8,128)(2,1)} %copy-done.15) | copy-start | bytes 786436
  58.3 12.6 %collective-permute-start.5 = (bf16[4,64,768]{2,1,0:T(8,128)(2,1)S(1)}, bf16[4,64,768]{2,1,0:T(8,128)(2,1)S(1)}, u32[]{:S(2)}, u32[]{:S(2)}) collective-permute-start(bf16[4,64,768]{2,1,0:T(8,128)(2,1)S(1)} %shard_map.107), channel_id=1, source_target_pairs={{0,64},{64,0},{128,192},{192,128},{256,320},{320,256},{384,448},{4... | collective-permute-start | bytes 1179656 | tf_op jit(solution)/shard_map/ppermute | solution.py:236
  68.2 47.0 %copy-start.5 = (bf16[128,1,256]{2,0,1:T(8,128)(2,1)S(1)}, bf16[128,1,256]{2,0,1:T(8,128)(2,1)}, u32[]{:S(2)}) copy-start(bf16[128,1,256]{2,0,1:T(8,128)(2,1)} %param.14) | copy-start | bytes 196612
  68.2 51.9 %copy-start.7 = (f32[3,3,256]{2,1,0:T(4,128)S(1)}, f32[3,3,256]{2,1,0:T(4,128)}, u32[]{:S(2)}) copy-start(f32[3,3,256]{2,1,0:T(4,128)} %refs_13_.1) | copy-start | bytes 27652
  68.2 17.9 %collective-permute-start.2 = (bf16[2,64,768]{2,1,0:T(8,128)(2,1)S(1)}, bf16[2,64,768]{2,1,0:T(8,128)(2,1)S(1)}, u32[]{:S(2)}, u32[]{:S(2)}) collective-permute-start(bf16[2,64,768]{2,1,0:T(8,128)(2,1)S(1)} %get-tuple-element.46), channel_id=1, source_target_pairs={{0,128},{64,192},{128,0},{192,64},{256,384},{320,448},{384,256},{4... | collective-permute-start | bytes 589832 | tf_op jit(solution)/shard_map/ppermute | solution.py:236
  70.9 21.4 %collective-permute-start.6 = (bf16[2,64,768]{2,1,0:T(8,128)(2,1)S(1)}, bf16[2,64,768]{2,1,0:T(8,128)(2,1)S(1)}, u32[]{:S(2)}, u32[]{:S(2)}) collective-permute-start(bf16[2,64,768]{2,1,0:T(8,128)(2,1)S(1)} %get-tuple-element.44), channel_id=1, source_target_pairs={{0,128},{64,192},{128,0},{192,64},{256,384},{320,448},{384,256},{4... | collective-permute-start | bytes 589832 | tf_op jit(solution)/shard_map/ppermute | solution.py:236
  86.2 10.4 %collective-permute-start.3 = (bf16[1,64,768]{2,1,0:T(8,128)(2,1)S(1)}, bf16[1,64,768]{2,1,0:T(8,128)(2,1)S(1)}, u32[]{:S(2)}, u32[]{:S(2)}) collective-permute-start(bf16[1,64,768]{2,1,0:T(8,128)(2,1)S(1)} %add_convert_fusion.9), channel_id=1, source_target_pairs={{0,256},{64,320},{128,384},{192,448},{256,0},{320,64},{384,128},{4... | collective-permute-start | bytes 294920 | tf_op jit(solution)/shard_map/ppermute | solution.py:236
  92.4 18.0 %collective-permute-start.7 = (bf16[1,64,768]{2,1,0:T(8,128)(2,1)S(1)}, bf16[1,64,768]{2,1,0:T(8,128)(2,1)S(1)}, u32[]{:S(2)}, u32[]{:S(2)}) collective-permute-start(bf16[1,64,768]{2,1,0:T(8,128)(2,1)S(1)} %add_convert_fusion.6), channel_id=1, source_target_pairs={{0,256},{64,320},{128,384},{192,448},{256,0},{320,64},{384,128},{4... | collective-permute-start | bytes 294920 | tf_op jit(solution)/shard_map/ppermute | solution.py:236
  110.5 9.7 %collective-permute-start.8 = (bf16[8,768]{1,0:T(8,128)(2,1)S(1)}, bf16[8,768]{1,0:T(8,128)(2,1)S(1)}, u32[]{:S(2)}, u32[]{:S(2)}) collective-permute-start(bf16[8,768]{1,0:T(8,128)(2,1)S(1)} %fusion.4), channel_id=1, source_target_pairs={{0,32},{32,64},{64,96},{96,128},{128,160},{160,192},{192,224},{224... | collective-permute-start | bytes 36872 | tf_op jit(solution)/shard_map/ppermute | solution.py:242
  112.4 7.7 %collective-permute-start.9 = (bf16[16,768]{1,0:T(8,128)(2,1)S(1)}, bf16[16,768]{1,0:T(8,128)(2,1)S(1)}, u32[]{:S(2)}, u32[]{:S(2)}) collective-permute-start(bf16[16,768]{1,0:T(8,128)(2,1)S(1)} %fusion.1), channel_id=1, source_target_pairs={{32,0},{64,32},{96,64},{128,96},{160,128},{192,160},{224,192},{256... | collective-permute-start | bytes 73736 | tf_op jit(solution)/shard_map/ppermute | solution.py:242
  115.2 5.0 %collective-permute-start.10 = (bf16[16,256]{1,0:T(8,128)(2,1)S(1)}, bf16[16,256]{1,0:T(8,128)(2,1)S(1)}, u32[]{:S(2)}, u32[]{:S(2)}) collective-permute-start(bf16[16,256]{1,0:T(8,128)(2,1)S(1)} %slice_bitcast_fusion), channel_id=1, source_target_pairs={{32,0},{64,32},{96,64},{128,96},{160,128},{192,160},{224,192},{256... | collective-permute-start | bytes 24584 | tf_op jit(solution)/shard_map/ppermute | solution.py:242
  120.2 7.6 %copy-start.8 = (f32[256]{0:T(256)S(1)}, f32[256]{0:T(256)}, u32[]{:S(2)}) copy-start(f32[256]{0:T(256)} %param.13) | copy-start | bytes 3076
  120.2 7.6 %copy-start.12 = (bf16[2048,256]{1,0:T(8,128)(2,1)S(1)}, bf16[2048,256]{1,0:T(8,128)(2,1)}, u32[]{:S(2)}) copy-start(bf16[2048,256]{1,0:T(8,128)(2,1)} %copy-done.11) | copy-start | bytes 3145732
  120.2 7.6 %copy-start.14 = (bf16[2048,256]{1,0:T(8,128)(2,1)S(1)}, bf16[2048,256]{1,0:T(8,128)(2,1)}, u32[]{:S(2)}) copy-start(bf16[2048,256]{1,0:T(8,128)(2,1)} %copy-done.13) | copy-start | bytes 3145732
  120.9 6.9 %collective-permute-start.12 = (bf16[144,256]{1,0:T(8,128)(2,1)S(1)}, bf16[144,256]{1,0:T(8,128)(2,1)S(1)}, u32[]{:S(2)}, u32[]{:S(2)}) collective-permute-start(bf16[144,256]{1,0:T(8,128)(2,1)S(1)} %get-tuple-element.28.refs_4_), channel_id=1, source_target_pairs={{32,0},{64,32},{96,64},{128,96},{160,128},{192,160},{224,192},{256... | collective-permute-start | bytes 221192 | tf_op jit(solution)/shard_map/ppermute | solution.py:242
  122.8 5.0 %collective-permute-start.11 = (bf16[128,256]{1,0:T(8,128)(2,1)S(1)}, bf16[128,256]{1,0:T(8,128)(2,1)S(1)}, u32[]{:S(2)}, u32[]{:S(2)}) collective-permute-start(bf16[128,256]{1,0:T(8,128)(2,1)S(1)} %get-tuple-element.27.refs_2_), channel_id=1, source_target_pairs={{0,32},{32,64},{64,96},{96,128},{128,160},{160,192},{192,224},{224... | collective-permute-start | bytes 196616 | tf_op jit(solution)/shard_map/ppermute | solution.py:242
  130.6 48.4 %copy-start.20 = (bf16[512,512]{1,0:T(8,128)(2,1)S(1)}, bf16[512,512]{1,0:T(8,128)(2,1)}, u32[]{:S(2)}) copy-start(bf16[512,512]{1,0:T(8,128)(2,1)} %copy-done.19) | copy-start | bytes 1572868
  130.6 15.5 %collective-permute-start.16 = (bf16[1,64,768]{2,1,0:T(8,128)(2,1)S(1)}, bf16[1,64,768]{2,1,0:T(8,128)(2,1)S(1)}, u32[]{:S(2)}, u32[]{:S(2)}) collective-permute-start(bf16[1,64,768]{2,1,0:T(8,128)(2,1)S(1)} %bitcast.51), channel_id=1, source_target_pairs={{0,256},{64,320},{128,384},{192,448},{256,0},{320,64},{384,128},{4... | collective-permute-start | bytes 294920 | tf_op jit(solution)/shard_map/ppermute | solution.py:236
  146.1 12.3 %collective-permute-start.17 = (bf16[2,64,768]{2,1,0:T(8,128)(2,1)S(1)}, bf16[2,64,768]{2,1,0:T(8,128)(2,1)S(1)}, u32[]{:S(2)}, u32[]{:S(2)}) collective-permute-start(bf16[2,64,768]{2,1,0:T(8,128)(2,1)S(1)} %pad_maximum_fusion.3), channel_id=1, source_target_pairs={{0,128},{64,192},{128,0},{192,64},{256,384},{320,448},{384,256},{4... | collective-permute-start | bytes 589832 | tf_op jit(solution)/shard_map/ppermute | solution.py:236
  158.5 20.5 %collective-permute-start.18 = (bf16[4,64,768]{2,1,0:T(8,128)(2,1)S(1)}, bf16[4,64,768]{2,1,0:T(8,128)(2,1)S(1)}, u32[]{:S(2)}, u32[]{:S(2)}) collective-permute-start(bf16[4,64,768]{2,1,0:T(8,128)(2,1)S(1)} %pad_maximum_fusion.1), channel_id=1, source_target_pairs={{0,64},{64,0},{128,192},{192,128},{256,320},{320,256},{384,448},{4... | collective-permute-start | bytes 1179656 | tf_op jit(solution)/shard_map/ppermute | solution.py:236
  160.4 10.3 %collective-permute-start.13 = (bf16[1,64,768]{2,1,0:T(8,128)(2,1)S(1)}, bf16[1,64,768]{2,1,0:T(8,128)(2,1)S(1)}, u32[]{:S(2)}, u32[]{:S(2)}) collective-permute-start(bf16[1,64,768]{2,1,0:T(8,128)(2,1)S(1)} %bitcast.47), channel_id=1, source_target_pairs={{0,256},{64,320},{128,384},{192,448},{256,0},{320,64},{384,128},{4... | collective-permute-start | bytes 294920 | tf_op jit(solution)/shard_map/ppermute | solution.py:236
  170.7 19.6 %collective-permute-start.14 = (bf16[2,64,768]{2,1,0:T(8,128)(2,1)S(1)}, bf16[2,64,768]{2,1,0:T(8,128)(2,1)S(1)}, u32[]{:S(2)}, u32[]{:S(2)}) collective-permute-start(bf16[2,64,768]{2,1,0:T(8,128)(2,1)S(1)} %pad_maximum_fusion.2), channel_id=1, source_target_pairs={{0,128},{64,192},{128,0},{192,64},{256,384},{320,448},{384,256},{4... | collective-permute-start | bytes 589832 | tf_op jit(solution)/shard_map/ppermute | solution.py:236
  183.4 0.9 copy-start.9
  184.3 28.8 %all-to-all-start.3 = ((bf16[32,32,512]{2,1,0:T(8,128)(2,1)}), bf16[32,32,512]{2,1,0:T(8,128)(2,1)}, u32[]{:S(2)}, u32[]{:S(2)}) async-start(bf16[32,32,512]{2,1,0:T(8,128)(2,1)} %bitcast.24), calls=%async_computation.3 | async-start | bytes 2097152 | tf_op jit(solution)/shard_map/all_to_all | solution.py:286
  190.5 17.7 %copy-start.2 = (bf16[32,32,512]{2,1,0:T(8,128)(2,1)S(1)}, bf16[32,32,512]{2,1,0:T(8,128)(2,1)}, u32[]{:S(2)}) copy-start(bf16[32,32,512]{2,1,0:T(8,128)(2,1)} %copy-done.1) | copy-start | bytes 3145732
  190.5 17.7 %copy-start.10 = (bf16[512,768]{1,0:T(8,128)(2,1)S(1)}, bf16[512,768]{1,0:T(8,128)(2,1)}, u32[]{:S(2)}) copy-start(bf16[512,768]{1,0:T(8,128)(2,1)} %copy-done.9) | copy-start | bytes 2359300
  190.5 13.3 %collective-permute-start.15 = (bf16[4,64,768]{2,1,0:T(8,128)(2,1)S(1)}, bf16[4,64,768]{2,1,0:T(8,128)(2,1)S(1)}, u32[]{:S(2)}, u32[]{:S(2)}) collective-permute-start(bf16[4,64,768]{2,1,0:T(8,128)(2,1)S(1)} %pad_maximum_fusion), channel_id=1, source_target_pairs={{0,64},{64,0},{128,192},{192,128},{256,320},{320,256},{384,448},{4... | collective-permute-start | bytes 1179656 | tf_op jit(solution)/shard_map/ppermute | solution.py:236
  207.2 1.0 copy-start.3
  210.3 9.9 %collective-permute-start.20 = (bf16[3,512,256]{2,1,0:T(8,128)(2,1)S(1)}, bf16[3,512,256]{2,1,0:T(8,128)(2,1)}, u32[]{:S(2)}, u32[]{:S(2)}) collective-permute-start(bf16[3,512,256]{2,1,0:T(8,128)(2,1)S(1)} %get-tuple-element.42), channel_id=1, source_target_pairs={{0,32},{32,0},{1,33},{33,1},{2,34},{34,2},{3,35},{35,3},{4,36},{36... | collective-permute-start | bytes 2359304 | tf_op jit(solution)/shard_map/ppermute | solution.py:236
  213.1 23.6 %all-to-all-start.2 = ((bf16[32,32,512]{2,1,0:T(8,128)(2,1)}), bf16[32,32,512]{2,1,0:T(8,128)(2,1)S(1)}, u32[]{:S(2)}, u32[]{:S(2)}) async-start(bf16[32,32,512]{2,1,0:T(8,128)(2,1)} %bitcast.46), calls=%async_computation.2 | async-start | bytes 2097152 | tf_op jit(solution)/shard_map/all_to_all | solution.py:286
  223.8 14.0 %collective-permute-start.19 = (bf16[2,32,512]{2,1,0:T(8,128)(2,1)S(1)}, bf16[2,32,512]{2,1,0:T(8,128)(2,1)S(1)}, u32[]{:S(2)}, u32[]{:S(2)}) collective-permute-start(bf16[2,32,512]{2,1,0:T(8,128)(2,1)S(1)} %bitcast_reduce_fusion), channel_id=1, source_target_pairs={{0,1},{1,0},{2,3},{3,2},{4,5},{5,4},{6,7},{7,6},{8,9},{9,8},{10,11... | collective-permute-start | bytes 196616 | tf_op jit(solution)/shard_map/ppermute | solution.py:236

commit v7 on v6

--- a/solution.py
+++ b/solution.py
@@ -119,11 +119,10 @@
     core = core_ref[0]
     members, rows, _ = out_ref.shape
     order = order_ref[...]
-    mine = dot(order, x_ref[core]).astype(BF16)
-    theirs = dot(order, x_ref[1 - core]).astype(BF16)
+    x = jnp.concatenate([dot(order, x_ref[place]).astype(BF16) for place in (core, 1 - core)], axis=1)
     streams, _, channels = own_ref.shape
     for i in range(streams):
-        part = (dot(mine, own_ref[i]) + dot(theirs, peer_ref[i])).astype(BF16)
+        part = dot(x, jnp.concatenate([own_ref[i], peer_ref[i]], axis=0)).astype(BF16)
         out_ref[:, :, i * channels : (i + 1) * channels] = part.reshape(members, rows, channels)
 
 
@@ -135,10 +134,8 @@
     g = dot(order_ref[...], gathered).astype(BF16)
     turned_ref[...] = g
     for place, ref in ((core, own_ref), (1 - core, peer_ref)):
-        total = dot_nt(g[:, :channels], ref[0])
-        for i in range(1, streams):
-            total = total + dot_nt(g[:, i * channels : (i + 1) * channels], ref[i])
-        out_ref[place] = total.astype(BF16)
+        weights = jnp.concatenate([ref[i] for i in range(streams)], axis=1)
+        out_ref[place] = dot_nt(g, weights).astype(BF16)
 
 
 def weight_body(core_ref, x0_ref, x1_ref, g0_ref, g1_ref, own_ref, peer_ref):

time: 242 us -> 242 us (level)
  no operation moved by 1% of the time
where the time goes in v7:
time: 242 us; the launch traced here: 238 us
  starting transfers between devices  124 us (51%)
  waiting for transfers between devices  73.4 us (30%)
  Pallas kernels  24.4 us (10%)
  local copies, waits for them, and re-layouts  8.41 us (3%)
  other arithmetic  6.03 us (2%)
    ppermute x16, starting transfers between devices, swap(): lax.ppermute(x, axis, [(i, i ^ by) for i in range(lax.axis_size(axis))])  80.5 us
    ppermute x16, waiting for transfers between devices, swap(): lax.ppermute(x, axis, [(i, i ^ by) for i in range(lax.axis_size(axis))])  63.9 us
    all_to_all x4, starting transfers between devices, exchange(): lax.all_to_all(x.reshape(2 * pieces, lines, rows), ('core', 'x', 'y'), 0,...  31.1 us
    pallas_call x10, Pallas kernels, call(): pl.pallas_call(run if loose else body, out_shape=outs, in_specs=[spec(i)...  24.4 us
    ppermute x5, starting transfers between devices, shifted(): lax.ppermute(x, axis, [(i, i + by) for i in range(count) if 0 <= i + by <...  12.1 us
    unnamed x44, local copies, waits for them, and re-layouts  5.8 us
    all_to_all x4, waiting for transfers between devices, exchange(): lax.all_to_all(x.reshape(2 * pieces, lines, rows), ('core', 'x', 'y'), 0,...  5.15 us
  transfers between devices with their start and end apart: 25, of which 13 were waited for; matrix products, arithmetic and copies ran while one was open for 2% of the time, Pallas kernels for 9%

profile of v7, /device:TPU:1, one launch (start us, length us, event | category | flops | bytes accessed | tf_op | source)
XLA Modules:
  0.0 238.3 jit_solution(6460053445364614637)
XLA Ops:
  2.9 10.5 %all-to-all-start = ((bf16[32,32,512]{2,1,0:T(8,128)(2,1)}), bf16[32,32,512]{2,1,0:T(8,128)(2,1)S(1)}, u32[]{:S(2)}, u32[]{:S(2)}) async-start(bf16[32,32,512]{2,1,0:T(8,128)(2,1)} %bitcast.4), calls=%async_computation | async-start | bytes 2097152 | tf_op jit(solution)/shard_map/all_to_all | solution.py:283
  13.5 13.5 %collective-permute-start.4 = (bf16[2,1,32,512]{3,2,0,1:T(8,128)(2,1)S(1)}, bf16[2,1,32,512]{3,2,0,1:T(8,128)(2,1)S(1)}, u32[]{:S(2)}, u32[]{:S(2)}) collective-permute-start(bf16[2,1,32,512]{3,2,0,1:T(8,128)(2,1)S(1)} %bitcast.70), channel_id=1, source_target_pairs={{0,1},{1,0},{2,3},{3,2},{4,5},{5,4},{6,7},{7,6},{8,9},{9,8},{10,11... | collective-permute-start | bytes 196616 | tf_op jit(solution)/shard_map/ppermute | solution.py:233
  27.0 2.2 collective-permute-done.4
  31.1 7.4 %all-to-all-start.1 = ((bf16[32,32,512]{2,1,0:T(8,128)(2,1)}), bf16[32,32,512]{2,1,0:T(8,128)(2,1)S(1)}, u32[]{:S(2)}, u32[]{:S(2)}) async-start(bf16[32,32,512]{2,1,0:T(8,128)(2,1)} %bitcast.68), calls=%async_computation.1 | async-start | bytes 2097152 | tf_op jit(solution)/shard_map/all_to_all | solution.py:283
  38.5 2.1 collective-permute-start
  40.9 1.8 shard_map.103
  45.5 2.3 shard_map.105
  47.9 3.9 %collective-permute-start.1 = (bf16[4,64,768]{2,1,0:T(8,128)(2,1)S(1)}, bf16[4,64,768]{2,1,0:T(8,128)(2,1)}, u32[]{:S(2)}, u32[]{:S(2)}) collective-permute-start(bf16[4,64,768]{2,1,0:T(8,128)(2,1)S(1)} %shard_map.105), channel_id=1, source_target_pairs={{0,64},{64,0},{128,192},{192,128},{256,320},{320,256},{384,448},{4... | collective-permute-start | bytes 1179656 | tf_op jit(solution)/shard_map/ppermute | solution.py:233
  51.8 2.9 %all-to-all-done.1 = bf16[32,32,512]{2,1,0:T(8,128)(2,1)S(1)} async-done(((bf16[32,32,512]{2,1,0:T(8,128)(2,1)}), bf16[32,32,512]{2,1,0:T(8,128)(2,1)S(1)}, u32[]{:S(2)}, u32[]{:S(2)}) %all-to-all-start.1) | async-done | bytes 1048608 | tf_op jit(solution)/shard_map/all_to_all | solution.py:283
  55.9 2.3 shard_map.107
  58.1 3.9 %collective-permute-start.5 = (bf16[4,64,768]{2,1,0:T(8,128)(2,1)S(1)}, bf16[4,64,768]{2,1,0:T(8,128)(2,1)S(1)}, u32[]{:S(2)}, u32[]{:S(2)}) collective-permute-start(bf16[4,64,768]{2,1,0:T(8,128)(2,1)S(1)} %shard_map.107), channel_id=1, source_target_pairs={{0,64},{64,0},{128,192},{192,128},{256,320},{320,256},{384,448},{4... | collective-permute-start | bytes 1179656 | tf_op jit(solution)/shard_map/ppermute | solution.py:233
  62.1 2.3 shard_map.104
  64.4 2.3 shard_map.106
  66.7 1.1 add_convert_fusion.4
  67.9 2.6 %collective-permute-start.2 = (bf16[2,64,768]{2,1,0:T(8,128)(2,1)S(1)}, bf16[2,64,768]{2,1,0:T(8,128)(2,1)S(1)}, u32[]{:S(2)}, u32[]{:S(2)}) collective-permute-start(bf16[2,64,768]{2,1,0:T(8,128)(2,1)S(1)} %get-tuple-element.46), channel_id=1, source_target_pairs={{0,128},{64,192},{128,0},{192,64},{256,384},{320,448},{384,256},{4... | collective-permute-start | bytes 589832 | tf_op jit(solution)/shard_map/ppermute | solution.py:233
  70.6 3.7 %collective-permute-start.6 = (bf16[2,64,768]{2,1,0:T(8,128)(2,1)S(1)}, bf16[2,64,768]{2,1,0:T(8,128)(2,1)S(1)}, u32[]{:S(2)}, u32[]{:S(2)}) collective-permute-start(bf16[2,64,768]{2,1,0:T(8,128)(2,1)S(1)} %get-tuple-element.44), channel_id=1, source_target_pairs={{0,128},{64,192},{128,0},{192,64},{256,384},{320,448},{384,256},{4... | collective-permute-start | bytes 589832 | tf_op jit(solution)/shard_map/ppermute | solution.py:233
  74.3 11.5 %collective-permute-done.2 = bf16[2,64,768]{2,1,0:T(8,128)(2,1)S(1)} collective-permute-done((bf16[2,64,768]{2,1,0:T(8,128)(2,1)S(1)}, bf16[2,64,768]{2,1,0:T(8,128)(2,1)S(1)}, u32[]{:S(2)}, u32[]{:S(2)}) %collective-permute-start.2) | collective-permute-done | bytes 196640 | tf_op jit(solution)/shard_map/ppermute | solution.py:233
  85.8 6.1 %collective-permute-start.3 = (bf16[1,64,768]{2,1,0:T(8,128)(2,1)S(1)}, bf16[1,64,768]{2,1,0:T(8,128)(2,1)S(1)}, u32[]{:S(2)}, u32[]{:S(2)}) collective-permute-start(bf16[1,64,768]{2,1,0:T(8,128)(2,1)S(1)} %add_convert_fusion.9), channel_id=1, source_target_pairs={{0,256},{64,320},{128,384},{192,448},{256,0},{320,64},{384,128},{4... | collective-permute-start | bytes 294920 | tf_op jit(solution)/shard_map/ppermute | solution.py:233
  92.0 4.2 %collective-permute-start.7 = (bf16[1,64,768]{2,1,0:T(8,128)(2,1)S(1)}, bf16[1,64,768]{2,1,0:T(8,128)(2,1)S(1)}, u32[]{:S(2)}, u32[]{:S(2)}) collective-permute-start(bf16[1,64,768]{2,1,0:T(8,128)(2,1)S(1)} %add_convert_fusion.6), channel_id=1, source_target_pairs={{0,256},{64,320},{128,384},{192,448},{256,0},{320,64},{384,128},{4... | collective-permute-start | bytes 294920 | tf_op jit(solution)/shard_map/ppermute | solution.py:233
  96.2 13.8 %collective-permute-done.7 = bf16[1,64,768]{2,1,0:T(8,128)(2,1)S(1)} collective-permute-done((bf16[1,64,768]{2,1,0:T(8,128)(2,1)S(1)}, bf16[1,64,768]{2,1,0:T(8,128)(2,1)S(1)}, u32[]{:S(2)}, u32[]{:S(2)}) %collective-permute-start.7) | collective-permute-done | bytes 98336 | tf_op jit(solution)/shard_map/ppermute | solution.py:233
  110.1 1.9 collective-permute-start.8
  112.0 2.7 %collective-permute-start.9 = (bf16[16,768]{1,0:T(8,128)(2,1)S(1)}, bf16[16,768]{1,0:T(8,128)(2,1)S(1)}, u32[]{:S(2)}, u32[]{:S(2)}) collective-permute-start(bf16[16,768]{1,0:T(8,128)(2,1)S(1)} %fusion.1), channel_id=1, source_target_pairs={{32,0},{64,32},{96,64},{128,96},{160,128},{192,160},{224,192},{256... | collective-permute-start | bytes 73736 | tf_op jit(solution)/shard_map/ppermute | solution.py:239
  114.8 1.9 collective-permute-start.10
  116.7 3.0 %collective-permute-done.10.refs_6_.refs_11_ = bf16[16,256]{1,0:T(8,128)(2,1)S(1)} collective-permute-done((bf16[16,256]{1,0:T(8,128)(2,1)S(1)}, bf16[16,256]{1,0:T(8,128)(2,1)S(1)}, u32[]{:S(2)}, u32[]{:S(2)}) %collective-permute-start.10) | collective-permute-done | bytes 8224 | tf_op jit(solution)/shard_map/ppermute | solution.py:239
  120.5 1.9 collective-permute-start.12
  122.4 3.6 %collective-permute-start.11 = (bf16[128,256]{1,0:T(8,128)(2,1)S(1)}, bf16[128,256]{1,0:T(8,128)(2,1)S(1)}, u32[]{:S(2)}, u32[]{:S(2)}) collective-permute-start(bf16[128,256]{1,0:T(8,128)(2,1)S(1)} %get-tuple-element.27.refs_2_), channel_id=1, source_target_pairs={{0,32},{32,64},{64,96},{96,128},{128,160},{160,192},{192,224},{224... | collective-permute-start | bytes 196616 | tf_op jit(solution)/shard_map/ppermute | solution.py:239
  126.1 1.3 collective-permute-done.11.refs_3_
  127.4 2.8 %shard_map.109 = (bf16[128,256]{1,0:T(8,128)(2,1)}, bf16[64,768]{1,0:T(8,128)(2,1)S(1)}, bf16[64,768]{1,0:T(8,128)(2,1)S(1)}) custom-call(bf16[2048,256]{1,0:T(8,128)(2,1)S(1)} %copy-done.12, bf16[2048,256]{1,0:T(8,128)(2,1)S(1)} %copy-done.14, bf16[128,256]{1,0:T(8,128)(2,1)S(1)} %get-tuple-element.27.refs_2_, ...), custom_call_target="tpu_custom_call" | custom-call | flops 1000000000 | bytes 2902020 | tf_op jit(solution)/shard_map/pallas_call | solution.py:40
  130.2 4.5 %collective-permute-start.16 = (bf16[1,64,768]{2,1,0:T(8,128)(2,1)S(1)}, bf16[1,64,768]{2,1,0:T(8,128)(2,1)S(1)}, u32[]{:S(2)}, u32[]{:S(2)}) collective-permute-start(bf16[1,64,768]{2,1,0:T(8,128)(2,1)S(1)} %bitcast.51), channel_id=1, source_target_pairs={{0,256},{64,320},{128,384},{192,448},{256,0},{320,64},{384,128},{4... | collective-permute-start | bytes 294920 | tf_op jit(solution)/shard_map/ppermute | solution.py:233
  134.7 11.0 %collective-permute-done.16.refs_3_ = bf16[1,64,768]{2,1,0:T(8,128)(2,1)S(1)} collective-permute-done((bf16[1,64,768]{2,1,0:T(8,128)(2,1)S(1)}, bf16[1,64,768]{2,1,0:T(8,128)(2,1)S(1)}, u32[]{:S(2)}, u32[]{:S(2)}) %collective-permute-start.16) | collective-permute-done | bytes 98336 | tf_op jit(solution)/shard_map/ppermute | solution.py:233
  145.8 1.9 collective-permute-start.17
  147.7 10.4 %collective-permute-done.17.refs_4_ = bf16[2,64,768]{2,1,0:T(8,128)(2,1)S(1)} collective-permute-done((bf16[2,64,768]{2,1,0:T(8,128)(2,1)S(1)}, bf16[2,64,768]{2,1,0:T(8,128)(2,1)S(1)}, u32[]{:S(2)}, u32[]{:S(2)}) %collective-permute-start.17) | collective-permute-done | bytes 196640 | tf_op jit(solution)/shard_map/ppermute | solution.py:233
  158.1 1.9 collective-permute-start.18
  160.0 5.5 %collective-permute-start.13 = (bf16[1,64,768]{2,1,0:T(8,128)(2,1)S(1)}, bf16[1,64,768]{2,1,0:T(8,128)(2,1)S(1)}, u32[]{:S(2)}, u32[]{:S(2)}) collective-permute-start(bf16[1,64,768]{2,1,0:T(8,128)(2,1)S(1)} %bitcast.47), channel_id=1, source_target_pairs={{0,256},{64,320},{128,384},{192,448},{256,0},{320,64},{384,128},{4... | collective-permute-start | bytes 294920 | tf_op jit(solution)/shard_map/ppermute | solution.py:233
  165.5 4.8 %collective-permute-done.13.refs_3_ = bf16[1,64,768]{2,1,0:T(8,128)(2,1)S(1)} collective-permute-done((bf16[1,64,768]{2,1,0:T(8,128)(2,1)S(1)}, bf16[1,64,768]{2,1,0:T(8,128)(2,1)S(1)}, u32[]{:S(2)}, u32[]{:S(2)}) %collective-permute-start.13) | collective-permute-done | bytes 98336 | tf_op jit(solution)/shard_map/ppermute | solution.py:233
  170.4 8.3 %collective-permute-start.14 = (bf16[2,64,768]{2,1,0:T(8,128)(2,1)S(1)}, bf16[2,64,768]{2,1,0:T(8,128)(2,1)S(1)}, u32[]{:S(2)}, u32[]{:S(2)}) collective-permute-start(bf16[2,64,768]{2,1,0:T(8,128)(2,1)S(1)} %pad_maximum_fusion.2), channel_id=1, source_target_pairs={{0,128},{64,192},{128,0},{192,64},{256,384},{320,448},{384,256},{4... | collective-permute-start | bytes 589832 | tf_op jit(solution)/shard_map/ppermute | solution.py:233
  178.7 4.4 %shard_map.111 = (bf16[2,512,512]{2,1,0:T(8,128)(2,1)}, bf16[512,768]{1,0:T(8,128)(2,1)S(1)}) custom-call(s32[1]{0:T(128)} %bitcast.1.refs_0_, bf16[512,512]{1,0:T(8,128)(2,1)S(1)} %copy-done.20, bf16[1,64,768]{2,1,0:T(8,128)(2,1)S(1)} %bitcast.54, bf16[1,64,768]{2,1,0:T(8,128)(2,1)S(1)} %collective-permute-done.16.refs_3_, ...), custom_call_target="tpu_custom_call" | custom-call | flops 1000000000 | bytes 2883588 | tf_op jit(solution)/shard_map/pallas_call | solution.py:40
  183.9 6.1 %all-to-all-start.3 = ((bf16[32,32,512]{2,1,0:T(8,128)(2,1)}), bf16[32,32,512]{2,1,0:T(8,128)(2,1)}, u32[]{:S(2)}, u32[]{:S(2)}) async-start(bf16[32,32,512]{2,1,0:T(8,128)(2,1)} %bitcast.24), calls=%async_computation.3 | async-start | bytes 2097152 | tf_op jit(solution)/shard_map/all_to_all | solution.py:283
  190.1 4.2 %collective-permute-start.15 = (bf16[4,64,768]{2,1,0:T(8,128)(2,1)S(1)}, bf16[4,64,768]{2,1,0:T(8,128)(2,1)S(1)}, u32[]{:S(2)}, u32[]{:S(2)}) collective-permute-start(bf16[4,64,768]{2,1,0:T(8,128)(2,1)S(1)} %pad_maximum_fusion), channel_id=1, source_target_pairs={{0,64},{64,0},{128,192},{192,128},{256,320},{320,256},{384,448},{4... | collective-permute-start | bytes 1179656 | tf_op jit(solution)/shard_map/ppermute | solution.py:233
  194.3 9.1 %collective-permute-done.15.refs_5_ = bf16[4,64,768]{2,1,0:T(8,128)(2,1)S(1)} collective-permute-done((bf16[4,64,768]{2,1,0:T(8,128)(2,1)S(1)}, bf16[4,64,768]{2,1,0:T(8,128)(2,1)S(1)}, u32[]{:S(2)}, u32[]{:S(2)}) %collective-permute-start.15) | collective-permute-done | bytes 393248 | tf_op jit(solution)/shard_map/ppermute | solution.py:233
  203.4 3.4 %shard_map.110 = (bf16[2,512,512]{2,1,0:T(8,128)(2,1)S(1)}, bf16[512,768]{1,0:T(8,128)(2,1)S(1)}) custom-call(s32[1]{0:T(128)} %bitcast.1.refs_0_, bf16[512,512]{1,0:T(8,128)(2,1)S(1)} %copy-done.20, bf16[1,64,768]{2,1,0:T(8,128)(2,1)S(1)} %bitcast.50, bf16[1,64,768]{2,1,0:T(8,128)(2,1)S(1)} %collective-permute-done.13.refs_3_, ...), custom_call_target="tpu_custom_call" | custom-call | flops 1000000000 | bytes 2883588 | tf_op jit(solution)/shard_map/pallas_call | solution.py:40
  207.8 2.1 shard_map.112
  209.9 2.7 %collective-permute-start.20 = (bf16[3,512,256]{2,1,0:T(8,128)(2,1)S(1)}, bf16[3,512,256]{2,1,0:T(8,128)(2,1)}, u32[]{:S(2)}, u32[]{:S(2)}) collective-permute-start(bf16[3,512,256]{2,1,0:T(8,128)(2,1)S(1)} %get-tuple-element.42), channel_id=1, source_target_pairs={{0,32},{32,0},{1,33},{33,1},{2,34},{34,2},{3,35},{35,3},{4,36},{36... | collective-permute-start | bytes 2359304 | tf_op jit(solution)/shard_map/ppermute | solution.py:233
  212.6 7.2 %all-to-all-start.2 = ((bf16[32,32,512]{2,1,0:T(8,128)(2,1)}), bf16[32,32,512]{2,1,0:T(8,128)(2,1)S(1)}, u32[]{:S(2)}, u32[]{:S(2)}) async-start(bf16[32,32,512]{2,1,0:T(8,128)(2,1)} %bitcast.46), calls=%async_computation.2 | async-start | bytes 2097152 | tf_op jit(solution)/shard_map/all_to_all | solution.py:283
  219.8 2.2 fusion
  222.0 1.4 bitcast_reduce_fusion
  223.4 11.3 %collective-permute-start.19 = (bf16[2,32,512]{2,1,0:T(8,128)(2,1)S(1)}, bf16[2,32,512]{2,1,0:T(8,128)(2,1)S(1)}, u32[]{:S(2)}, u32[]{:S(2)}) collective-permute-start(bf16[2,32,512]{2,1,0:T(8,128)(2,1)S(1)} %bitcast_reduce_fusion), channel_id=1, source_target_pairs={{0,1},{1,0},{2,3},{3,2},{4,5},{5,4},{6,7},{7,6},{8,9},{9,8},{10,11... | collective-permute-start | bytes 196616 | tf_op jit(solution)/shard_map/ppermute | solution.py:233
  234.7 1.5 all-to-all-done.2
  (87 shorter events, 13.4 us)
Async XLA Ops:
  0.6 1.0 copy-start
  2.9 27.1 %all-to-all-start = ((bf16[32,32,512]{2,1,0:T(8,128)(2,1)}), bf16[32,32,512]{2,1,0:T(8,128)(2,1)S(1)}, u32[]{:S(2)}, u32[]{:S(2)}) async-start(bf16[32,32,512]{2,1,0:T(8,128)(2,1)} %bitcast.4), calls=%async_computation | async-start | bytes 2097152 | tf_op jit(solution)/shard_map/all_to_all | solution.py:283
  13.5 15.7 %collective-permute-start.4 = (bf16[2,1,32,512]{3,2,0,1:T(8,128)(2,1)S(1)}, bf16[2,1,32,512]{3,2,0,1:T(8,128)(2,1)S(1)}, u32[]{:S(2)}, u32[]{:S(2)}) collective-permute-start(bf16[2,1,32,512]{3,2,0,1:T(8,128)(2,1)S(1)} %bitcast.70), channel_id=1, source_target_pairs={{0,1},{1,0},{2,3},{3,2},{4,5},{5,4},{6,7},{7,6},{8,9},{9,8},{10,11... | collective-permute-start | bytes 196616 | tf_op jit(solution)/shard_map/ppermute | solution.py:233
  30.0 8.5 %copy-start.6 = (bf16[512,3,256]{2,0,1:T(8,128)(2,1)S(1)}, bf16[512,3,256]{2,0,1:T(8,128)(2,1)}, u32[]{:S(2)}) copy-start(bf16[512,3,256]{2,0,1:T(8,128)(2,1)} %param.9) | copy-start | bytes 2359300
  30.0 10.6 %copy-start.4 = (f32[16,128]{1,0:T(8,128)S(1)}, f32[16,128]{1,0:T(8,128)}, u32[]{:S(2)}) copy-start(f32[16,128]{1,0:T(8,128)} %taps_ref.1) | copy-start | bytes 24580
  30.0 10.8 %copy-start.21 = (f32[16]{0:T(128)S(1)}, f32[16]{0:T(128)}, u32[]{:S(2)}) copy-start(f32[16]{0:T(128)} %param.12) | copy-start | bytes 196
  31.1 23.7 %all-to-all-start.1 = ((bf16[32,32,512]{2,1,0:T(8,128)(2,1)}), bf16[32,32,512]{2,1,0:T(8,128)(2,1)S(1)}, u32[]{:S(2)}, u32[]{:S(2)}) async-start(bf16[32,32,512]{2,1,0:T(8,128)(2,1)} %bitcast.68), calls=%async_computation.1 | async-start | bytes 2097152 | tf_op jit(solution)/shard_map/all_to_all | solution.py:283
  38.5 7.1 %collective-permute-start = (bf16[3,512,256]{2,1,0:T(8,128)(2,1)S(1)}, bf16[3,512,256]{2,1,0:T(8,128)(2,1)}, u32[]{:S(2)}, u32[]{:S(2)}) collective-permute-start(bf16[3,512,256]{2,1,0:T(8,128)(2,1)S(1)} %bitcast.60), channel_id=1, source_target_pairs={{0,32},{32,0},{1,33},{33,1},{2,34},{34,2},{3,35},{35,3},{4,36},{36... | collective-permute-start | bytes 2359304 | tf_op jit(solution)/shard_map/ppermute | solution.py:233
  42.8 1.0 copy-start.11
  43.8 1.0 copy-start.13
  44.7 0.8 copy-start.19
  45.5 2.4 copy-start.15
  45.5 2.4 copy-start.17
  47.9 18.8 %collective-permute-start.1 = (bf16[4,64,768]{2,1,0:T(8,128)(2,1)S(1)}, bf16[4,64,768]{2,1,0:T(8,128)(2,1)}, u32[]{:S(2)}, u32[]{:S(2)}) collective-permute-start(bf16[4,64,768]{2,1,0:T(8,128)(2,1)S(1)} %shard_map.105), channel_id=1, source_target_pairs={{0,64},{64,0},{128,192},{192,128},{256,320},{320,256},{384,448},{4... | collective-permute-start | bytes 1179656 | tf_op jit(solution)/shard_map/ppermute | solution.py:233
  54.7 9.7 %copy-start.1 = (bf16[32,32,512]{2,1,0:T(8,128)(2,1)}, bf16[32,32,512]{2,1,0:T(8,128)(2,1)S(1)}, u32[]{:S(2)}) copy-start(bf16[32,32,512]{2,1,0:T(8,128)(2,1)S(1)} %all-to-all-done.1) | copy-start | bytes 3145732
  54.7 1.1 copy-start.18
  55.9 6.2 %copy-start.16 = (bf16[256,512]{1,0:T(8,128)(2,1)S(1)}, bf16[256,512]{1,0:T(8,128)(2,1)}, u32[]{:S(2)}) copy-start(bf16[256,512]{1,0:T(8,128)(2,1)} %copy-done.15) | copy-start | bytes 786436
  58.1 12.3 %collective-permute-start.5 = (bf16[4,64,768]{2,1,0:T(8,128)(2,1)S(1)}, bf16[4,64,768]{2,1,0:T(8,128)(2,1)S(1)}, u32[]{:S(2)}, u32[]{:S(2)}) collective-permute-start(bf16[4,64,768]{2,1,0:T(8,128)(2,1)S(1)} %shard_map.107), channel_id=1, source_target_pairs={{0,64},{64,0},{128,192},{192,128},{256,320},{320,256},{384,448},{4... | collective-permute-start | bytes 1179656 | tf_op jit(solution)/shard_map/ppermute | solution.py:233
  67.8 47.0 %copy-start.5 = (bf16[128,1,256]{2,0,1:T(8,128)(2,1)S(1)}, bf16[128,1,256]{2,0,1:T(8,128)(2,1)}, u32[]{:S(2)}) copy-start(bf16[128,1,256]{2,0,1:T(8,128)(2,1)} %param.14) | copy-start | bytes 196612
  67.8 51.9 %copy-start.7 = (f32[3,3,256]{2,1,0:T(4,128)S(1)}, f32[3,3,256]{2,1,0:T(4,128)}, u32[]{:S(2)}) copy-start(f32[3,3,256]{2,1,0:T(4,128)} %refs_13_.1) | copy-start | bytes 27652
  67.9 17.9 %collective-permute-start.2 = (bf16[2,64,768]{2,1,0:T(8,128)(2,1)S(1)}, bf16[2,64,768]{2,1,0:T(8,128)(2,1)S(1)}, u32[]{:S(2)}, u32[]{:S(2)}) collective-permute-start(bf16[2,64,768]{2,1,0:T(8,128)(2,1)S(1)} %get-tuple-element.46), channel_id=1, source_target_pairs={{0,128},{64,192},{128,0},{192,64},{256,384},{320,448},{384,256},{4... | collective-permute-start | bytes 589832 | tf_op jit(solution)/shard_map/ppermute | solution.py:233
  70.6 21.4 %collective-permute-start.6 = (bf16[2,64,768]{2,1,0:T(8,128)(2,1)S(1)}, bf16[2,64,768]{2,1,0:T(8,128)(2,1)S(1)}, u32[]{:S(2)}, u32[]{:S(2)}) collective-permute-start(bf16[2,64,768]{2,1,0:T(8,128)(2,1)S(1)} %get-tuple-element.44), channel_id=1, source_target_pairs={{0,128},{64,192},{128,0},{192,64},{256,384},{320,448},{384,256},{4... | collective-permute-start | bytes 589832 | tf_op jit(solution)/shard_map/ppermute | solution.py:233
  85.8 10.4 %collective-permute-start.3 = (bf16[1,64,768]{2,1,0:T(8,128)(2,1)S(1)}, bf16[1,64,768]{2,1,0:T(8,128)(2,1)S(1)}, u32[]{:S(2)}, u32[]{:S(2)}) collective-permute-start(bf16[1,64,768]{2,1,0:T(8,128)(2,1)S(1)} %add_convert_fusion.9), channel_id=1, source_target_pairs={{0,256},{64,320},{128,384},{192,448},{256,0},{320,64},{384,128},{4... | collective-permute-start | bytes 294920 | tf_op jit(solution)/shard_map/ppermute | solution.py:233
  92.0 18.0 %collective-permute-start.7 = (bf16[1,64,768]{2,1,0:T(8,128)(2,1)S(1)}, bf16[1,64,768]{2,1,0:T(8,128)(2,1)S(1)}, u32[]{:S(2)}, u32[]{:S(2)}) collective-permute-start(bf16[1,64,768]{2,1,0:T(8,128)(2,1)S(1)} %add_convert_fusion.6), channel_id=1, source_target_pairs={{0,256},{64,320},{128,384},{192,448},{256,0},{320,64},{384,128},{4... | collective-permute-start | bytes 294920 | tf_op jit(solution)/shard_map/ppermute | solution.py:233
  110.1 9.7 %collective-permute-start.8 = (bf16[8,768]{1,0:T(8,128)(2,1)S(1)}, bf16[8,768]{1,0:T(8,128)(2,1)S(1)}, u32[]{:S(2)}, u32[]{:S(2)}) collective-permute-start(bf16[8,768]{1,0:T(8,128)(2,1)S(1)} %fusion.4), channel_id=1, source_target_pairs={{0,32},{32,64},{64,96},{96,128},{128,160},{160,192},{192,224},{224... | collective-permute-start | bytes 36872 | tf_op jit(solution)/shard_map/ppermute | solution.py:239
  112.0 7.7 %collective-permute-start.9 = (bf16[16,768]{1,0:T(8,128)(2,1)S(1)}, bf16[16,768]{1,0:T(8,128)(2,1)S(1)}, u32[]{:S(2)}, u32[]{:S(2)}) collective-permute-start(bf16[16,768]{1,0:T(8,128)(2,1)S(1)} %fusion.1), channel_id=1, source_target_pairs={{32,0},{64,32},{96,64},{128,96},{160,128},{192,160},{224,192},{256... | collective-permute-start | bytes 73736 | tf_op jit(solution)/shard_map/ppermute | solution.py:239
  114.8 5.0 %collective-permute-start.10 = (bf16[16,256]{1,0:T(8,128)(2,1)S(1)}, bf16[16,256]{1,0:T(8,128)(2,1)S(1)}, u32[]{:S(2)}, u32[]{:S(2)}) collective-permute-start(bf16[16,256]{1,0:T(8,128)(2,1)S(1)} %slice_bitcast_fusion), channel_id=1, source_target_pairs={{32,0},{64,32},{96,64},{128,96},{160,128},{192,160},{224,192},{256... | collective-permute-start | bytes 24584 | tf_op jit(solution)/shard_map/ppermute | solution.py:239
  119.8 7.6 %copy-start.8 = (f32[256]{0:T(256)S(1)}, f32[256]{0:T(256)}, u32[]{:S(2)}) copy-start(f32[256]{0:T(256)} %param.13) | copy-start | bytes 3076
  119.8 7.6 %copy-start.12 = (bf16[2048,256]{1,0:T(8,128)(2,1)S(1)}, bf16[2048,256]{1,0:T(8,128)(2,1)}, u32[]{:S(2)}) copy-start(bf16[2048,256]{1,0:T(8,128)(2,1)} %copy-done.11) | copy-start | bytes 3145732
  119.8 7.6 %copy-start.14 = (bf16[2048,256]{1,0:T(8,128)(2,1)S(1)}, bf16[2048,256]{1,0:T(8,128)(2,1)}, u32[]{:S(2)}) copy-start(bf16[2048,256]{1,0:T(8,128)(2,1)} %copy-done.13) | copy-start | bytes 3145732
  120.5 6.9 %collective-permute-start.12 = (bf16[144,256]{1,0:T(8,128)(2,1)S(1)}, bf16[144,256]{1,0:T(8,128)(2,1)S(1)}, u32[]{:S(2)}, u32[]{:S(2)}) collective-permute-start(bf16[144,256]{1,0:T(8,128)(2,1)S(1)} %get-tuple-element.28.refs_4_), channel_id=1, source_target_pairs={{32,0},{64,32},{96,64},{128,96},{160,128},{192,160},{224,192},{256... | collective-permute-start | bytes 221192 | tf_op jit(solution)/shard_map/ppermute | solution.py:239
  122.4 5.0 %collective-permute-start.11 = (bf16[128,256]{1,0:T(8,128)(2,1)S(1)}, bf16[128,256]{1,0:T(8,128)(2,1)S(1)}, u32[]{:S(2)}, u32[]{:S(2)}) collective-permute-start(bf16[128,256]{1,0:T(8,128)(2,1)S(1)} %get-tuple-element.27.refs_2_), channel_id=1, source_target_pairs={{0,32},{32,64},{64,96},{96,128},{128,160},{160,192},{192,224},{224... | collective-permute-start | bytes 196616 | tf_op jit(solution)/shard_map/ppermute | solution.py:239
  130.2 48.4 %copy-start.20 = (bf16[512,512]{1,0:T(8,128)(2,1)S(1)}, bf16[512,512]{1,0:T(8,128)(2,1)}, u32[]{:S(2)}) copy-start(bf16[512,512]{1,0:T(8,128)(2,1)} %copy-done.19) | copy-start | bytes 1572868
  130.2 15.5 %collective-permute-start.16 = (bf16[1,64,768]{2,1,0:T(8,128)(2,1)S(1)}, bf16[1,64,768]{2,1,0:T(8,128)(2,1)S(1)}, u32[]{:S(2)}, u32[]{:S(2)}) collective-permute-start(bf16[1,64,768]{2,1,0:T(8,128)(2,1)S(1)} %bitcast.51), channel_id=1, source_target_pairs={{0,256},{64,320},{128,384},{192,448},{256,0},{320,64},{384,128},{4... | collective-permute-start | bytes 294920 | tf_op jit(solution)/shard_map/ppermute | solution.py:233
  145.8 12.3 %collective-permute-start.17 = (bf16[2,64,768]{2,1,0:T(8,128)(2,1)S(1)}, bf16[2,64,768]{2,1,0:T(8,128)(2,1)S(1)}, u32[]{:S(2)}, u32[]{:S(2)}) collective-permute-start(bf16[2,64,768]{2,1,0:T(8,128)(2,1)S(1)} %pad_maximum_fusion.3), channel_id=1, source_target_pairs={{0,128},{64,192},{128,0},{192,64},{256,384},{320,448},{384,256},{4... | collective-permute-start | bytes 589832 | tf_op jit(solution)/shard_map/ppermute | solution.py:233
  158.1 20.6 %collective-permute-start.18 = (bf16[4,64,768]{2,1,0:T(8,128)(2,1)S(1)}, bf16[4,64,768]{2,1,0:T(8,128)(2,1)S(1)}, u32[]{:S(2)}, u32[]{:S(2)}) collective-permute-start(bf16[4,64,768]{2,1,0:T(8,128)(2,1)S(1)} %pad_maximum_fusion.1), channel_id=1, source_target_pairs={{0,64},{64,0},{128,192},{192,128},{256,320},{320,256},{384,448},{4... | collective-permute-start | bytes 1179656 | tf_op jit(solution)/shard_map/ppermute | solution.py:233
  160.0 10.3 %collective-permute-start.13 = (bf16[1,64,768]{2,1,0:T(8,128)(2,1)S(1)}, bf16[1,64,768]{2,1,0:T(8,128)(2,1)S(1)}, u32[]{:S(2)}, u32[]{:S(2)}) collective-permute-start(bf16[1,64,768]{2,1,0:T(8,128)(2,1)S(1)} %bitcast.47), channel_id=1, source_target_pairs={{0,256},{64,320},{128,384},{192,448},{256,0},{320,64},{384,128},{4... | collective-permute-start | bytes 294920 | tf_op jit(solution)/shard_map/ppermute | solution.py:233
  170.4 19.6 %collective-permute-start.14 = (bf16[2,64,768]{2,1,0:T(8,128)(2,1)S(1)}, bf16[2,64,768]{2,1,0:T(8,128)(2,1)S(1)}, u32[]{:S(2)}, u32[]{:S(2)}) collective-permute-start(bf16[2,64,768]{2,1,0:T(8,128)(2,1)S(1)} %pad_maximum_fusion.2), channel_id=1, source_target_pairs={{0,128},{64,192},{128,0},{192,64},{256,384},{320,448},{384,256},{4... | collective-permute-start | bytes 589832 | tf_op jit(solution)/shard_map/ppermute | solution.py:233
  183.0 0.9 copy-start.9
  183.9 28.7 %all-to-all-start.3 = ((bf16[32,32,512]{2,1,0:T(8,128)(2,1)}), bf16[32,32,512]{2,1,0:T(8,128)(2,1)}, u32[]{:S(2)}, u32[]{:S(2)}) async-start(bf16[32,32,512]{2,1,0:T(8,128)(2,1)} %bitcast.24), calls=%async_computation.3 | async-start | bytes 2097152 | tf_op jit(solution)/shard_map/all_to_all | solution.py:283
  190.1 17.7 %copy-start.2 = (bf16[32,32,512]{2,1,0:T(8,128)(2,1)S(1)}, bf16[32,32,512]{2,1,0:T(8,128)(2,1)}, u32[]{:S(2)}) copy-start(bf16[32,32,512]{2,1,0:T(8,128)(2,1)} %copy-done.1) | copy-start | bytes 3145732
  190.1 17.7 %copy-start.10 = (bf16[512,768]{1,0:T(8,128)(2,1)S(1)}, bf16[512,768]{1,0:T(8,128)(2,1)}, u32[]{:S(2)}) copy-start(bf16[512,768]{1,0:T(8,128)(2,1)} %copy-done.9) | copy-start | bytes 2359300
  190.1 13.3 %collective-permute-start.15 = (bf16[4,64,768]{2,1,0:T(8,128)(2,1)S(1)}, bf16[4,64,768]{2,1,0:T(8,128)(2,1)S(1)}, u32[]{:S(2)}, u32[]{:S(2)}) collective-permute-start(bf16[4,64,768]{2,1,0:T(8,128)(2,1)S(1)} %pad_maximum_fusion), channel_id=1, source_target_pairs={{0,64},{64,0},{128,192},{192,128},{256,320},{320,256},{384,448},{4... | collective-permute-start | bytes 1179656 | tf_op jit(solution)/shard_map/ppermute | solution.py:233
  206.8 1.0 copy-start.3
  209.9 9.9 %collective-permute-start.20 = (bf16[3,512,256]{2,1,0:T(8,128)(2,1)S(1)}, bf16[3,512,256]{2,1,0:T(8,128)(2,1)}, u32[]{:S(2)}, u32[]{:S(2)}) collective-permute-start(bf16[3,512,256]{2,1,0:T(8,128)(2,1)S(1)} %get-tuple-element.42), channel_id=1, source_target_pairs={{0,32},{32,0},{1,33},{33,1},{2,34},{34,2},{3,35},{35,3},{4,36},{36... | collective-permute-start | bytes 2359304 | tf_op jit(solution)/shard_map/ppermute | solution.py:233
  212.6 23.6 %all-to-all-start.2 = ((bf16[32,32,512]{2,1,0:T(8,128)(2,1)}), bf16[32,32,512]{2,1,0:T(8,128)(2,1)S(1)}, u32[]{:S(2)}, u32[]{:S(2)}) async-start(bf16[32,32,512]{2,1,0:T(8,128)(2,1)} %bitcast.46), calls=%async_computation.2 | async-start | bytes 2097152 | tf_op jit(solution)/shard_map/all_to_all | solution.py:283
  223.4 14.0 %collective-permute-start.19 = (bf16[2,32,512]{2,1,0:T(8,128)(2,1)S(1)}, bf16[2,32,512]{2,1,0:T(8,128)(2,1)S(1)}, u32[]{:S(2)}, u32[]{:S(2)}) collective-permute-start(bf16[2,32,512]{2,1,0:T(8,128)(2,1)S(1)} %bitcast_reduce_fusion), channel_id=1, source_target_pairs={{0,1},{1,0},{2,3},{3,2},{4,5},{5,4},{6,7},{7,6},{8,9},{9,8},{10,11... | collective-permute-start | bytes 196616 | tf_op jit(solution)/shard_map/ppermute | solution.py:233
